TPU v7x, 128 devices: a whole 4x4x4 slice. The times are simulated.
128 devices in a mesh: gx: 8 (over y, core), gy: 16 (over z, x).
Axes of the slice: x: 4, y: 4, z: 4, core: 2. Of those that a mesh axis runs over, the one named last changes fastest.
Arguments:
- features: bfloat16 [256, 256, 64, 128], P('gx', 'gy'), may hold values from -6 to 6
- voxel_mask: int32 [256, 256, 64], P('gx', 'gy'), may hold values 0 or 1
- brick_mask: int32 [16, 16, 4], P('gx', 'gy'), may hold values from 0 to 1
- owner: int32 [8, 16, 8, 1], P('gx', 'gy'), may hold values from 0 to 15, as said below
- weights: bfloat16 [3, 3, 3, 128, 64], replicated, may hold values from -0.109375 to 0.109375
- bias: float32 [64], replicated, may hold values from -0.5 to 0.5
Outputs:
- decoded: bfloat16 [8, 256, 64, 4096], P('gx', 'gy')
Inputs may be any that keep to these rules, and one draw needn't show every extreme that they name: Active bricks are spread unevenly over tiles. Among one device's 8 bricks no owner index appears more than 1 times, and some index appears exactly 1 times. Owners are chosen from the active-brick counts so that over all sources of one brick-grid row no owner receives more than 8 active bricks.
All inputs are finite; a program needn't handle non-finite values. No bound on the sum of `voxel_mask` on one device may be relied on, other than what follows from the above.
Results may differ from a plain program's by a relative error of at most 0.001.
Values may be sent and summed in bfloat16 or wider, within the bound.
A program may use at most 256 MiB of HBM per device.

v0:
```python
import jax
import jax.numpy as jnp
from jax import lax
from jax.sharding import PartitionSpec as P

C = 64
EDGE = 16


def padded_2(cells, sides, width):
    for axis, dim in sides:
        count = lax.axis_size(axis)
        ends = count - 1
        head = lax.slice_in_dim(cells, 0, width, axis=dim)
        tail = lax.slice_in_dim(cells, cells.shape[dim] - width, cells.shape[dim], axis=dim)
        cells = jnp.concatenate(
            [
                lax.ppermute(tail, axis, [(i, (i + 1) % count) for i in range(ends)]),
                cells,
                lax.ppermute(head, axis, [((i + 1) % count, i) for i in range(ends)]),
            ],
            axis=dim,
        )
    return cells


def finish(pre, masks, bias):
    value = jnp.maximum(pre + bias[None, :, None], 0.0) * masks[:, None, :].astype(jnp.float32)
    return value.astype(jnp.bfloat16)


def per_device(features, voxel_mask, brick_mask, owner, weights, bias):
    extent_x, extent_y, extent_z, channels_in = features.shape
    bricks_x = extent_x // EDGE
    bricks_y = extent_y // EDGE
    bricks_z = extent_z // EDGE
    count = bricks_x * bricks_y * bricks_z
    groups = lax.axis_size("gy")
    capacity = (count + groups - 1) // groups
    grown = jnp.repeat(brick_mask, EDGE, axis=0)
    grown = jnp.repeat(grown, EDGE, axis=1)
    grown = jnp.repeat(grown, EDGE, axis=2)
    live = (voxel_mask * grown).astype(jnp.bfloat16)
    inputs = features * live[..., None]
    padded = padded_2(inputs, (("gx", 0), ("gy", 1)), 1)
    padded = jnp.pad(padded, ((0, 0), (0, 0), (1, 1), (0, 0)))
    brick_masks = live.reshape(bricks_x, EDGE, bricks_y, EDGE, bricks_z, EDGE)
    brick_masks = brick_masks.transpose(0, 2, 4, 1, 3, 5).reshape(count, EDGE**3)
    ids = owner.reshape(count)
    order = jnp.arange(count, dtype=jnp.int32)
    same = ids[:, None] == ids[None, :]
    rank = jnp.sum(jnp.logical_and(same, order[None, :] < order[:, None]).astype(jnp.int32), axis=1)
    slots = ids * capacity + rank
    total = groups * capacity
    whole = lax.conv_general_dilated(
        padded[None],
        weights,
        (1, 1, 1),
        "VALID",
        dimension_numbers=("NDHWC", "DHWIO", "NCDHW"),
        preferred_element_type=jnp.float32,
    )[0]
    whole = whole.reshape(C, bricks_x, EDGE, bricks_y, EDGE, bricks_z, EDGE)
    pre = whole.transpose(1, 3, 5, 0, 2, 4, 6).reshape(count, C, EDGE**3)
    result = finish(pre, brick_masks, bias)
    sending = jnp.zeros((total, C, EDGE**3), jnp.bfloat16).at[slots].set(result)
    decoded = lax.all_to_all(sending, "gy", split_axis=0, concat_axis=0, tiled=True)
    return decoded[None]


def solution(mesh):
    return jax.shard_map(
        per_device,
        mesh=mesh,
        in_specs=(
            P("gx", "gy", None, None),
            P("gx", "gy", None),
            P("gx", "gy", None),
            P("gx", "gy", None, None),
            P(),
            P(),
        ),
        out_specs=P("gx", "gy", None, None),
        check_vma=False,
    )
```

profile of v0, /device:TPU:8, one launch (start us, length us, event | category | flops | bytes accessed | tf_op | source)
XLA Modules:
  0.0 312.1 jit_solution(7063071496401131539)
XLA Ops:
  0.0 0.0 copy-start
  0.0 0.8 copy.29
  0.8 0.1 broadcast_in_dim.28
  0.9 0.1 broadcast_in_dim.29
  1.0 0.1 copy.30
  1.1 1.0 multiply_convert_fusion.1
  2.0 6.3 %broadcast_multiply_fusion = bf16[32,16,64,128]{3,2,1,0:T(8,128)(2,1)S(1)} fusion(bf16[32,16,64,128]{3,2,1,0:T(8,128)(2,1)} %param.6, bf16[32,16,64]{2,1,0:T(8,128)(2,1)S(1)} %multiply_convert_fusion.1), kind=kLoop, calls=%fused_computation.24 | loop fusion | flops 4194304 | bytes 16842752 | tf_op jit(solution)/shard_map/mul | solution.py:44
  8.4 0.0 copy-start.2
  8.4 0.0 copy-start.6
  8.4 1.9 collective-permute-start
  10.4 3.6 %collective-permute-start.1 = (bf16[1,16,64,128]{3,2,1,0:T(8,128)(2,1)S(1)}, bf16[1,16,64,128]{3,2,1,0:T(8,128)(2,1)S(1)}, u32[]{:S(2)}, u32[]{:S(2)}) collective-permute-start(bf16[1,16,64,128]{3,2,1,0:T(8,128)(2,1)S(1)} %get-tuple-element.8), channel_id=1, source_target_pairs={{16,0},{32,16},{48,32},{64,48},{80,64},{96,80},{112,96},{17,1},{33... | collective-permute-start | bytes 786440 | tf_op jit(solution)/shard_map/ppermute | solution.py:20
  14.0 2.1 collective-permute-done
  16.1 1.8 collective-permute-done.1
  17.9 0.0 copy-done.2
  17.9 1.1 pad_maximum_fusion.2
  19.0 4.2 %collective-permute-start.2 = (bf16[34,1,64,128]{3,2,1,0:T(8,128)(2,1)}, bf16[34,1,64,128]{3,2,1,0:T(8,128)(2,1)}, u32[]{:S(2)}, u32[]{:S(2)}) collective-permute-start(bf16[34,1,64,128]{3,2,1,0:T(8,128)(2,1)} %get-tuple-element.5), channel_id=1, source_target_pairs={{0,1},{1,2},{2,3},{3,4},{4,5},{5,6},{6,7},{7,8},{8,9},{9,10},{10,1... | collective-permute-start | bytes 1671176 | tf_op jit(solution)/shard_map/ppermute | solution.py:18
  23.3 1.3 collective-permute-start.3
  24.5 0.5 reshape.68
  25.0 0.1 copy.37
  25.1 0.6 reshape.62
  25.7 0.0 copy-done.6
  25.7 0.2 convert_reduce_fusion
  25.9 0.5 fusion.20
  26.5 8.4 %collective-permute-done.2 = bf16[34,1,64,128]{3,2,1,0:T(8,128)(2,1)} collective-permute-done((bf16[34,1,64,128]{3,2,1,0:T(8,128)(2,1)}, bf16[34,1,64,128]{3,2,1,0:T(8,128)(2,1)}, u32[]{:S(2)}, u32[]{:S(2)}) %collective-permute-start.2) | collective-permute-done | bytes 557088 | tf_op jit(solution)/shard_map/ppermute | solution.py:18
  34.9 5.5 %collective-permute-done.3 = bf16[34,1,64,128]{3,2,1,0:T(8,128)(2,1)} collective-permute-done((bf16[34,1,64,128]{3,2,1,0:T(8,128)(2,1)}, bf16[34,1,64,128]{3,2,1,0:T(8,128)(2,1)}, u32[]{:S(2)}, u32[]{:S(2)}) %collective-permute-start.3) | collective-permute-done | bytes 557088 | tf_op jit(solution)/shard_map/ppermute | solution.py:20
  40.4 17.8 %fusion.9 = bf16[34,18,1,66,128]{4,3,1,0,2:T(8,128)(2,1)S(1)} fusion(bf16[34,1,64,128]{3,2,1,0:T(8,128)(2,1)} %collective-permute-done.3, bf16[34,1,64,128]{3,2,1,0:T(8,128)(2,1)} %collective-permute-done.2, bf16[1,16,64,128]{3,2,1,0:T(8,128)(2,1)S(1)} %collective-permute-done.1, bf16[32,16,64,128]{3,2,1,0:T(8,128)(2,1)} %copy-done.2, ...), kind=kLoop, calls=%fused_computation.15 | loop fusion | flops 93063168 | bytes 20367360 | tf_op jit(solution)/shard_map/broadcast_in_dim | solution.py:56
  58.2 3.5 %copy.39 = bf16[34,18,1,66,128]{4,0,3,1,2:T(8,128)(2,1)S(1)} copy(bf16[34,18,1,66,128]{4,3,1,0,2:T(8,128)(2,1)S(1)} %fusion.9) | data formatting | bytes 20680704
  61.7 2.3 pad.5.clone
  64.1 0.0 copy-start.7
  64.1 3.9 %copy.33 = bf16[34,18,1,8,9,128]{5,3,4,1,0,2:T(8,128)(2,1)S(1)} copy(bf16[34,18,1,8,9,128]{5,0,4,3,1,2:T(8,128)(2,1)S(1)} %bitcast.41) | data formatting | bytes 22560768 | tf_op jit(solution)/shard_map/conv_general_dilated | solution.py:55
  68.1 0.0 copy-start.3
  68.1 4.3 %copy-done.3 = bf16[34,18,1,8,9,128]{5,3,4,1,0,2:T(8,128)(2,1)} copy-done((bf16[34,18,1,8,9,128]{5,3,4,1,0,2:T(8,128)(2,1)}, bf16[34,18,1,8,9,128]{5,3,4,1,0,2:T(8,128)(2,1)S(1)}, u32[]{:S(2)}) %copy-start.3) | copy-done | bytes 11280408
  72.3 2.1 slice.20
  74.4 0.0 copy-done
  74.4 0.0 copy-done.7
  74.4 73.0 %fusion.15 = f32[32,16,8,9,64]{4,2,3,1,0:T(8,128)S(1)} fusion(bf16[3,3,3,128,64]{3,4,2,1,0:T(8,128)(2,1)S(1)} %copy-done, bf16[34,18,1,7,2,128]{5,3,4,1,0,2:T(8,128)(2,1)} %slice.20, bf16[34,18,1,8,9,128]{5,3,4,1,0,2:T(8,128)(2,1)} %copy-done.3, pred[8,9]{0,1:T(8,128)(4,1)S(1)} %copy-done.7), kind=kOutput, calls=%fused_computation.22 | convolution fusion | flops 16351174656 | bytes 23353416 | tf_op jit(solution)/shard_map/conv_general_dilated | solution.py:55
  147.4 4.3 %copy.34 = f32[32,16,8,9,64]{4,1,3,2,0:T(8,128)S(1)} copy(f32[32,16,8,9,64]{4,2,3,1,0:T(8,128)S(1)} %fusion.15) | data formatting | bytes 18874368 | tf_op jit(solution)/shard_map/conv_general_dilated | solution.py:55
  151.7 1.2 slice_bitcast_fusion
  153.0 7.8 %copy.35 = f32[1,64,32,16,64]{1,4,3,2,0:T(8,128)} copy(f32[1,64,32,16,64]{1,3,4,2,0:T(8,128)S(1)} %slice_bitcast_fusion) | data formatting | bytes 16777216 | tf_op jit(solution)/shard_map/conv_general_dilated | solution.py:55
  160.8 0.0 copy-start.4
  160.8 7.2 %copy.36 = f32[2,1,4,64,16,16,16]{3,6,5,4,2,0,1:T(8,128)S(1)} copy(f32[2,1,4,64,16,16,16]{3,6,2,5,4,0,1:T(8,128)} %bitcast.40) | data formatting | bytes 16777216 | tf_op jit(solution)/shard_map/transpose | solution.py:64
  168.0 0.0 copy-done.4
  168.0 6.4 %multiply_convert_fusion = bf16[8,64,4096]{1,2,0:T(8,128)(2,1)} fusion(f32[8,64,4096]{1,2,0:T(8,128)S(1)} %bitcast.39, f32[8,4096]{1,0:T(8,128)S(1)} %reshape.62, f32[64]{0:T(128)S(1)} %copy-done.4), kind=kLoop, calls=%fused_computation.7 | loop fusion | flops 8388608 | bytes 12714240 | tf_op jit(solution)/shard_map/convert_element_type | solution.py:29
  174.4 0.0 copy-start.5
  174.4 8.5 %copy.38 = bf16[8,64,4096]{2,1,0:T(8,128)(2,1)} copy(bf16[8,64,4096]{1,2,0:T(8,128)(2,1)} %multiply_convert_fusion) | data formatting | bytes 8388608 | tf_op jit(solution)/shard_map/convert_element_type | solution.py:29
  182.9 4.4 %broadcast_in_dim.27 = bf16[16,64,4096]{2,1,0:T(8,128)(2,1)} broadcast(bf16[]{:T(256)} %constant.4.clone.1), dimensions={} | broadcast | bytes 8388610 | tf_op jit(solution)/shard_map/broadcast_in_dim | solution.py:66
  187.3 0.0 copy-done.5
  187.4 10.9 %scatter_fusion = bf16[16,64,4096]{2,1,0:T(8,128)(2,1)} fusion(bf16[16,64,4096]{2,1,0:T(8,128)(2,1)} %broadcast_in_dim.27, s32[8]{0:T(128)S(1)} %copy-done.5, bf16[8,64,4096]{2,1,0:T(8,128)(2,1)} %copy.38), kind=kCustom, calls=%fused_computation | custom fusion | bytes 12582944 | tf_op jit(solution)/shard_map/scatter | solution.py:66
  198.2 0.0 copy-start.1
  198.2 106.0 %all_to_all.5 = bf16[16,64,4096]{2,1,0:T(8,128)(2,1)} all-to-all(bf16[16,64,4096]{2,1,0:T(8,128)(2,1)} %scatter_fusion), channel_id=1, replica_groups=mesh['gx'=8,'gy'=16] {'gy'}, dimensions={0} | all-to-all | bytes 16777216 | tf_op jit(solution)/shard_map/all_to_all | solution.py:67
  304.2 7.9 %copy.42 = bf16[1,16,64,4096]{3,2,1,0:T(8,128)(2,1)} copy(bf16[1,16,64,4096]{3,2,1,0:T(8,128)(2,1)} %bitcast.42) | data formatting | bytes 16777216
  312.1 0.0 copy-done.1
  (2 shorter events, 0.0 us)
Async XLA Ops:
  0.0 74.4 %copy-start = (bf16[3,3,3,128,64]{3,4,2,1,0:T(8,128)(2,1)S(1)}, bf16[3,3,3,128,64]{3,4,2,1,0:T(8,128)(2,1)}, u32[]{:S(2)}) copy-start(bf16[3,3,3,128,64]{3,4,2,1,0:T(8,128)(2,1)} %param.10) | copy-start | bytes 1327108
  8.4 9.5 %copy-start.2 = (bf16[32,16,64,128]{3,2,1,0:T(8,128)(2,1)}, bf16[32,16,64,128]{3,2,1,0:T(8,128)(2,1)S(1)}, u32[]{:S(2)}) copy-start(bf16[32,16,64,128]{3,2,1,0:T(8,128)(2,1)S(1)} %broadcast_multiply_fusion) | copy-start | bytes 25165828
  8.4 17.4 %copy-start.6 = (s32[1,1,8,1]{2,3,1,0:T(1,128)S(1)}, s32[1,1,8,1]{2,3,1,0:T(1,128)}, u32[]{:S(2)}) copy-start(s32[1,1,8,1]{2,3,1,0:T(1,128)} %param.9) | copy-start | bytes 100
  8.4 7.7 %collective-permute-start = (bf16[1,16,64,128]{3,2,1,0:T(8,128)(2,1)S(1)}, bf16[1,16,64,128]{3,2,1,0:T(8,128)(2,1)S(1)}, u32[]{:S(2)}, u32[]{:S(2)}) collective-permute-start(bf16[1,16,64,128]{3,2,1,0:T(8,128)(2,1)S(1)} %get-tuple-element.7), channel_id=1, source_target_pairs={{0,16},{16,32},{32,48},{48,64},{64,80},{80,96},{96,112},{1,17},{17... | collective-permute-start | bytes 786440 | tf_op jit(solution)/shard_map/ppermute | solution.py:18
  10.4 7.5 %collective-permute-start.1 = (bf16[1,16,64,128]{3,2,1,0:T(8,128)(2,1)S(1)}, bf16[1,16,64,128]{3,2,1,0:T(8,128)(2,1)S(1)}, u32[]{:S(2)}, u32[]{:S(2)}) collective-permute-start(bf16[1,16,64,128]{3,2,1,0:T(8,128)(2,1)S(1)} %get-tuple-element.8), channel_id=1, source_target_pairs={{16,0},{32,16},{48,32},{64,48},{80,64},{96,80},{112,96},{17,1},{33... | collective-permute-start | bytes 786440 | tf_op jit(solution)/shard_map/ppermute | solution.py:20
  19.0 15.8 %collective-permute-start.2 = (bf16[34,1,64,128]{3,2,1,0:T(8,128)(2,1)}, bf16[34,1,64,128]{3,2,1,0:T(8,128)(2,1)}, u32[]{:S(2)}, u32[]{:S(2)}) collective-permute-start(bf16[34,1,64,128]{3,2,1,0:T(8,128)(2,1)} %get-tuple-element.5), channel_id=1, source_target_pairs={{0,1},{1,2},{2,3},{3,4},{4,5},{5,6},{6,7},{7,8},{8,9},{9,10},{10,1... | collective-permute-start | bytes 1671176 | tf_op jit(solution)/shard_map/ppermute | solution.py:18
  23.3 17.2 %collective-permute-start.3 = (bf16[34,1,64,128]{3,2,1,0:T(8,128)(2,1)}, bf16[34,1,64,128]{3,2,1,0:T(8,128)(2,1)}, u32[]{:S(2)}, u32[]{:S(2)}) collective-permute-start(bf16[34,1,64,128]{3,2,1,0:T(8,128)(2,1)} %get-tuple-element.6), channel_id=1, source_target_pairs={{1,0},{2,1},{3,2},{4,3},{5,4},{6,5},{7,6},{8,7},{9,8},{10,9},{11,1... | collective-permute-start | bytes 1671176 | tf_op jit(solution)/shard_map/ppermute | solution.py:20
  64.1 10.3 %copy-start.7 = (pred[8,9]{0,1:T(8,128)(4,1)S(1)}, pred[8,9]{0,1:T(8,128)(4,1)}, u32[]{:S(2)}) copy-start(pred[8,9]{0,1:T(8,128)(4,1)} %constant.18) | copy-start | bytes 220
  68.1 4.3 %copy-start.3 = (bf16[34,18,1,8,9,128]{5,3,4,1,0,2:T(8,128)(2,1)}, bf16[34,18,1,8,9,128]{5,3,4,1,0,2:T(8,128)(2,1)S(1)}, u32[]{:S(2)}) copy-start(bf16[34,18,1,8,9,128]{5,3,4,1,0,2:T(8,128)(2,1)S(1)} %copy.33) | copy-start | bytes 33841156
  160.8 7.2 %copy-start.4 = (f32[64]{0:T(128)S(1)}, f32[64]{0:T(128)}, u32[]{:S(2)}) copy-start(f32[64]{0:T(128)} %param.11) | copy-start | bytes 772
  174.4 13.0 %copy-start.5 = (s32[8]{0:T(128)S(1)}, s32[8]{0:T(128)}, u32[]{:S(2)}) copy-start(s32[8]{0:T(128)} %fusion.20) | copy-start | bytes 100
  198.2 113.9 %copy-start.1 = (bf16[3,3,3,128,64]{3,4,2,1,0:T(8,128)(2,1)S(1)}, bf16[3,3,3,128,64]{3,4,2,1,0:T(8,128)(2,1)}, u32[]{:S(2)}) copy-start(bf16[3,3,3,128,64]{3,4,2,1,0:T(8,128)(2,1)} %param.10) | copy-start | bytes 1327108
where the time goes:
time: 313 us; the launch traced here: 312 us
  blocking collectives  106 us (34%)
  matrix products  73 us (23%)
  local copies, waits for them, and re-layouts  70.7 us (23%)
  other arithmetic  33.4 us (11%)
  waiting for transfers between devices  17.8 us (6%)
  starting transfers between devices  11.1 us (4%)
    all_to_all x1, blocking collectives, per_device(): lax.all_to_all(sending, 'gy', split_axis=0, concat_axis=0, tiled=True)  106 us
    conv_general_dilated x1, matrix products, per_device(): lax.conv_general_dilated(padded[None], weights, (1, 1, 1), 'VALID', dimen...  73 us
    conv_general_dilated x5, local copies, waits for them, and re-layouts, per_device(): lax.conv_general_dilated(padded[None], weights, (1, 1, 1), 'VALID', dimen...  19.4 us
    broadcast_in_dim x1, other arithmetic, per_device(): padded[None]  17.8 us
    unnamed x18, local copies, waits for them, and re-layouts  15.7 us
    scatter x1, local copies, waits for them, and re-layouts, per_device(): jnp.zeros((total, C, EDGE ** 3), jnp.bfloat16).at[slots].set(result)  10.9 us
    ppermute x2, waiting for transfers between devices, padded_2(): lax.ppermute(tail, axis, [(i, (i + 1) % count) for i in range(ends)])  10.5 us
    convert_element_type x1, local copies, waits for them, and re-layouts, finish(): return value.astype(jnp.bfloat16)  8.54 us
  transfers between devices with their start and end apart: 4, of which 4 were waited for; matrix products, arithmetic and copies ran while one was open for 1% of the time, Pallas kernels for 0%

commit v1 on v0

--- a/solution.py
+++ b/solution.py
@@ -2,6 +2,8 @@
 import jax.numpy as jnp
 from jax import lax
 from jax.sharding import PartitionSpec as P
+from jax.experimental import pallas as pl
+from jax.experimental.pallas import tpu as pltpu
 
 C = 64
 EDGE = 16
@@ -24,9 +26,61 @@
     return cells
 
 
-def finish(pre, masks, bias):
-    value = jnp.maximum(pre + bias[None, :, None], 0.0) * masks[:, None, :].astype(jnp.float32)
-    return value.astype(jnp.bfloat16)
+def conv_kernel(table_ref, x_ref, w_ref, b_ref, m_ref, o_ref):
+    slot = pl.program_id(0)
+    slots = pl.num_programs(0)
+    valid = table_ref[slots + slot]
+    rows = EDGE * EDGE
+
+    @pl.when(valid > 0)
+    def _():
+        def body(ex, carry):
+            acc = jnp.zeros((rows, C), jnp.float32)
+            for a in range(3):
+                for b in range(3):
+                    lhs = x_ref[pl.ds(ex + a, 1), pl.ds(b, EDGE), :, :]
+                    lhs = lhs.reshape(rows, lhs.shape[-1])
+                    acc = acc + jnp.dot(lhs, w_ref[a * 3 + b], preferred_element_type=jnp.float32)
+            start = pl.multiple_of(ex * rows, rows)
+            mask = m_ref[0, :, pl.ds(start, rows)]
+            value = jnp.maximum(acc.T + b_ref[...], 0.0) * mask
+            o_ref[0, :, pl.ds(start, rows)] = value.astype(o_ref.dtype)
+            return carry
+
+        lax.fori_loop(0, EDGE, body, 0)
+
+    @pl.when(valid == 0)
+    def _():
+        o_ref[...] = jnp.zeros(o_ref.shape, o_ref.dtype)
+
+
+def conv_slots(table, shifted, w9, bias_col, masks, total, bricks_z):
+    depth = shifted.shape[-1]
+    span = shifted.shape[1]
+
+    def brick_of(j, table_ref):
+        return table_ref[j]
+
+    def x_map(j, table_ref):
+        brick = brick_of(j, table_ref)
+        return (brick // bricks_z * EDGE, 0, brick % bricks_z * EDGE, 0)
+
+    return pl.pallas_call(
+        conv_kernel,
+        out_shape=jax.ShapeDtypeStruct((total, C, EDGE**3), jnp.bfloat16),
+        grid_spec=pltpu.PrefetchScalarGridSpec(
+            num_scalar_prefetch=1,
+            grid=(total,),
+            in_specs=[
+                pl.BlockSpec((pl.Element(EDGE + 2), pl.Element(span), pl.Element(EDGE), pl.Element(depth)), x_map),
+                pl.BlockSpec(w9.shape, lambda j, t: (0, 0, 0)),
+                pl.BlockSpec(bias_col.shape, lambda j, t: (0, 0)),
+                pl.BlockSpec((1, 1, EDGE**3), lambda j, t: (brick_of(j, t), 0, 0)),
+            ],
+            out_specs=pl.BlockSpec((1, C, EDGE**3), lambda j, t: (j, 0, 0)),
+        ),
+        compiler_params=pltpu.CompilerParams(vmem_limit_bytes=48 * 1024 * 1024),
+    )(table, shifted, w9, bias_col, masks)
 
 
 def per_device(features, voxel_mask, brick_mask, owner, weights, bias):
@@ -44,26 +98,22 @@
     inputs = features * live[..., None]
     padded = padded_2(inputs, (("gx", 0), ("gy", 1)), 1)
     padded = jnp.pad(padded, ((0, 0), (0, 0), (1, 1), (0, 0)))
-    brick_masks = live.reshape(bricks_x, EDGE, bricks_y, EDGE, bricks_z, EDGE)
-    brick_masks = brick_masks.transpose(0, 2, 4, 1, 3, 5).reshape(count, EDGE**3)
+    shifted = jnp.concatenate([padded[:, :, c:c + extent_z, :] for c in range(3)], axis=-1)
+    brick_masks = live.astype(jnp.float32).reshape(bricks_x, EDGE, bricks_y, EDGE, bricks_z, EDGE)
+    brick_masks = brick_masks.transpose(0, 2, 4, 1, 3, 5).reshape(count, 1, EDGE**3)
     ids = owner.reshape(count)
     order = jnp.arange(count, dtype=jnp.int32)
     same = ids[:, None] == ids[None, :]
     rank = jnp.sum(jnp.logical_and(same, order[None, :] < order[:, None]).astype(jnp.int32), axis=1)
     slots = ids * capacity + rank
     total = groups * capacity
-    whole = lax.conv_general_dilated(
-        padded[None],
-        weights,
-        (1, 1, 1),
-        "VALID",
-        dimension_numbers=("NDHWC", "DHWIO", "NCDHW"),
-        preferred_element_type=jnp.float32,
-    )[0]
-    whole = whole.reshape(C, bricks_x, EDGE, bricks_y, EDGE, bricks_z, EDGE)
-    pre = whole.transpose(1, 3, 5, 0, 2, 4, 6).reshape(count, C, EDGE**3)
-    result = finish(pre, brick_masks, bias)
-    sending = jnp.zeros((total, C, EDGE**3), jnp.bfloat16).at[slots].set(result)
+    hit = slots[None, :] == jnp.arange(total, dtype=jnp.int32)[:, None]
+    brick_of_slot = jnp.sum(jnp.where(hit, order[None, :], 0), axis=1)
+    valid = jnp.any(hit, axis=1).astype(jnp.int32)
+    table = jnp.concatenate([brick_of_slot, valid]).astype(jnp.int32)
+    w9 = weights.reshape(9, 3 * channels_in, C)
+    bias_col = bias.reshape(C, 1).astype(jnp.float32)
+    sending = conv_slots(table, shifted, w9, bias_col, brick_masks, total, bricks_z)
     decoded = lax.all_to_all(sending, "gy", split_axis=0, concat_axis=0, tiled=True)
     return decoded[None]
 

time: 313 us -> 308 us (0.984)
  Pallas kernels: 0 us -> 100 us
  matrix products: 73 us -> 0 us
  local copies, waits for them, and re-layouts: 70.7 us -> 23.9 us
  other arithmetic: 33.4 us -> 49.5 us
    pallas_call x0 -> x1, Pallas kernels: none -> 100 us  [conv_slots(): pl.pallas_call(conv_kernel, out_shape=jax.ShapeDtypeStruct((total, C, EDG...]
    conv_general_dilated x1 -> x0, matrix products: 73 us -> none  [per_device(): lax.conv_general_dilated(padded[None], weights, (1, 1, 1), 'VALID', dimen...]
    concatenate x0 -> x3, other arithmetic: none -> 38.7 us  [the longest x1 21.2 us: per_device(): jnp.concatenate([padded[:, :, c:c + extent_z, :] for c in range(3)], axis...]
    conv_general_dilated x5 -> x0, local copies, waits for them, and re-layouts: 19.4 us -> none  [per_device(): lax.conv_general_dilated(padded[None], weights, (1, 1, 1), 'VALID', dimen...]
    broadcast_in_dim x1 -> x0, other arithmetic: 17.8 us -> none  [per_device(): padded[None]]
    scatter x1 -> x0, local copies, waits for them, and re-layouts: 10.9 us -> none  [per_device(): jnp.zeros((total, C, EDGE ** 3), jnp.bfloat16).at[slots].set(result)]
    convert_element_type x4 -> x0, local copies, waits for them, and re-layouts: 9.72 us -> none  [the longest x1 8.54 us: finish(): return value.astype(jnp.bfloat16)]
    slice x0 -> x1, local copies, waits for them, and re-layouts: none -> 9.07 us  [per_device(): padded[:, :, c:c + extent_z, :]]
where the time goes in v1:
time: 308 us
  blocking collectives  108 us (35%)
  Pallas kernels  100 us (32%)
  other arithmetic  49.5 us (16%)
  local copies, waits for them, and re-layouts  23.9 us (8%)
  waiting for transfers between devices  16 us (5%)
  starting transfers between devices  10.3 us (3%)
    all_to_all x1, blocking collectives, per_device(): lax.all_to_all(sending, 'gy', split_axis=0, concat_axis=0, tiled=True)  108 us
    pallas_call x1, Pallas kernels, conv_slots(): pl.pallas_call(conv_kernel, out_shape=jax.ShapeDtypeStruct((total, C, EDG...  100 us
    concatenate x1, other arithmetic, per_device(): jnp.concatenate([padded[:, :, c:c + extent_z, :] for c in range(3)], axis...  21.2 us
    concatenate x1, other arithmetic, padded_2(): jnp.concatenate([lax.ppermute(tail, axis, [(i, (i + 1) % count) for i in...  17.5 us
    unnamed x8, local copies, waits for them, and re-layouts  12.7 us
    ppermute x2, waiting for transfers between devices, padded_2(): lax.ppermute(tail, axis, [(i, (i + 1) % count) for i in range(ends)])  9.53 us
    slice x1, local copies, waits for them, and re-layouts, per_device(): padded[:, :, c:c + extent_z, :]  9.07 us
    ppermute x2, waiting for transfers between devices, padded_2(): lax.ppermute(head, axis, [((i + 1) % count, i) for i in range(ends)])  6.51 us
  transfers between devices with their start and end apart: 4, of which 4 were waited for; matrix products, arithmetic and copies ran while one was open for 1% of the time, Pallas kernels for 0%

profile of v1, /device:TPU:8, one launch (start us, length us, event | category | flops | bytes accessed | tf_op | source)
XLA Modules:
  0.0 307.7 jit_solution(14174999738619738685)
XLA Ops:
  0.0 0.0 copy-start.2
  0.0 0.0 copy-start.1
  0.0 0.8 copy.17
  0.8 0.1 broadcast_in_dim.36
  0.9 0.1 broadcast_in_dim.37
  1.0 0.1 copy.18
  1.0 1.0 multiply_convert_fusion
  2.0 6.3 %broadcast_multiply_fusion = bf16[32,16,64,128]{3,2,1,0:T(8,128)(2,1)S(1)} fusion(bf16[32,16,64,128]{3,2,1,0:T(8,128)(2,1)} %param.6, bf16[32,16,64]{2,1,0:T(8,128)(2,1)S(1)} %multiply_convert_fusion), kind=kLoop, calls=%fused_computation.11 | loop fusion | flops 4194304 | bytes 16842752 | tf_op jit(solution)/shard_map/mul | solution.py:98
  8.4 0.0 copy-start
  8.4 3.4 %copy-done = bf16[32,16,64,128]{3,2,1,0:T(8,128)(2,1)} copy-done((bf16[32,16,64,128]{3,2,1,0:T(8,128)(2,1)}, bf16[32,16,64,128]{3,2,1,0:T(8,128)(2,1)S(1)}, u32[]{:S(2)}) %copy-start) | copy-done | bytes 8388632
  11.8 1.9 collective-permute-start
  13.7 3.6 %collective-permute-start.1 = (bf16[1,16,64,128]{3,2,1,0:T(8,128)(2,1)S(1)}, bf16[1,16,64,128]{3,2,1,0:T(8,128)(2,1)S(1)}, u32[]{:S(2)}, u32[]{:S(2)}) collective-permute-start(bf16[1,16,64,128]{3,2,1,0:T(8,128)(2,1)S(1)} %get-tuple-element.10), channel_id=1, source_target_pairs={{16,0},{32,16},{48,32},{64,48},{80,64},{96,80},{112,96},{17,1},{33... | collective-permute-start | bytes 786440 | tf_op jit(solution)/shard_map/ppermute | solution.py:22
  17.4 0.5 reshape.46
  17.8 0.9 convert_reduce_fusion
  18.8 0.7 collective-permute-done
  19.5 1.8 collective-permute-done.1
  21.2 2.3 pad_maximum_fusion.3
  23.6 3.4 %collective-permute-start.2 = (bf16[34,1,64,128]{3,2,1,0:T(8,128)(2,1)}, bf16[34,1,64,128]{3,2,1,0:T(8,128)(2,1)S(1)}, u32[]{:S(2)}, u32[]{:S(2)}) collective-permute-start(bf16[34,1,64,128]{3,2,1,0:T(8,128)(2,1)} %get-tuple-element.7), channel_id=1, source_target_pairs={{0,1},{1,2},{2,3},{3,4},{4,5},{5,6},{6,7},{7,8},{8,9},{9,10},{10,1... | collective-permute-start | bytes 1671176 | tf_op jit(solution)/shard_map/ppermute | solution.py:20
  27.0 1.3 collective-permute-start.3
  28.3 0.0 copy-done.2
  28.3 0.1 fusion.6
  28.4 0.1 copy.23
  28.5 0.4 reshape.43.m_ref
  28.9 1.4 copy.19
  30.4 0.0 copy-done.1
  30.4 0.1 copy.21.b_ref
  30.5 0.1 select_reduce_fusion
  30.5 0.1 pad_add_fusion.table_ref
  30.6 8.8 %collective-permute-done.2 = bf16[34,1,64,128]{3,2,1,0:T(8,128)(2,1)S(1)} collective-permute-done((bf16[34,1,64,128]{3,2,1,0:T(8,128)(2,1)}, bf16[34,1,64,128]{3,2,1,0:T(8,128)(2,1)S(1)}, u32[]{:S(2)}, u32[]{:S(2)}) %collective-permute-start.2) | collective-permute-done | bytes 557088 | tf_op jit(solution)/shard_map/ppermute | solution.py:20
  39.4 4.8 %collective-permute-done.3 = bf16[34,1,64,128]{3,2,1,0:T(8,128)(2,1)} collective-permute-done((bf16[34,1,64,128]{3,2,1,0:T(8,128)(2,1)}, bf16[34,1,64,128]{3,2,1,0:T(8,128)(2,1)}, u32[]{:S(2)}, u32[]{:S(2)}) %collective-permute-start.3) | collective-permute-done | bytes 557088 | tf_op jit(solution)/shard_map/ppermute | solution.py:22
  44.2 17.5 %select_maximum_fusion = bf16[34,18,66,128]{3,2,1,0:T(8,128)(2,1)S(1)} fusion(bf16[34,1,64,128]{3,2,1,0:T(8,128)(2,1)} %collective-permute-done.3, bf16[34,1,64,128]{3,2,1,0:T(8,128)(2,1)S(1)} %collective-permute-done.2, bf16[1,16,64,128]{3,2,1,0:T(8,128)(2,1)S(1)} %collective-permute-done.1, bf16[32,16,64,128]{3,2,1,0:T(8,128)(2,1)} %copy-done, ...), kind=kLoop, calls=%fused_computation.4 | loop fusion | flops 93063168 | bytes 20367360 | tf_op jit(solution)/shard_map/concatenate | solution.py:18
  61.6 9.1 %fusion.8 = (bf16[34,18,64,128]{3,2,1,0:T(8,128)(2,1)}, bf16[34,18,64,128]{3,2,1,0:T(8,128)(2,1)}) fusion(bf16[34,18,66,128]{3,2,1,0:T(8,128)(2,1)S(1)} %select_maximum_fusion), kind=kLoop, calls=%fused_computation.25 | loop fusion | bytes 40108032 | tf_op jit(solution)/shard_map/slice | solution.py:101
  70.7 21.2 %pad_maximum_fusion.x_ref = bf16[34,18,64,384]{3,2,1,0:T(8,128)(2,1)} fusion(bf16[34,18,64,128]{3,2,1,0:T(8,128)(2,1)} %get-tuple-element.6, bf16[34,1,64,128]{3,2,1,0:T(8,128)(2,1)} %collective-permute-done.3, bf16[1,16,64,128]{3,2,1,0:T(8,128)(2,1)S(1)} %collective-permute-done.1, bf16[32,16,64,128]{3,2,1,0:T(8,128)(2,1)} %copy-done, ...), kind=kLoop, calls=%fused_computation.2 | loop fusion | flops 210567168 | bytes 60162048 | tf_op jit(solution)/shard_map/concatenate | solution.py:101
  91.9 100.2 %shard_map.67 = bf16[16,64,4096]{2,1,0:T(8,128)(2,1)} custom-call(s32[32]{0:T(128)S(1)} %pad_add_fusion.table_ref, bf16[34,18,64,384]{3,2,1,0:T(8,128)(2,1)} %pad_maximum_fusion.x_ref, bf16[9,384,64]{2,1,0:T(8,128)(2,1)S(1)} %bitcast.16, f32[64,1]{1,0:T(8,128)S(1)} %copy.21.b_ref, f32[8,1,4096]{2,1,0:T(1,128)S(1)} %reshape.43.m_ref), custom_call_target="tpu_custom_call" | custom-call | tf_op jit(solution)/shard_map/pallas_call | solution.py:68
  192.1 107.8 %all_to_all.5 = bf16[16,64,4096]{2,1,0:T(8,128)(2,1)} all-to-all(bf16[16,64,4096]{2,1,0:T(8,128)(2,1)} %shard_map.67), channel_id=1, replica_groups=mesh['gx'=8,'gy'=16] {'gy'}, dimensions={0} | all-to-all | bytes 16777216 | tf_op jit(solution)/shard_map/all_to_all | solution.py:117
  299.8 7.9 %copy.25 = bf16[1,16,64,4096]{3,2,1,0:T(8,128)(2,1)} copy(bf16[1,16,64,4096]{3,2,1,0:T(8,128)(2,1)} %bitcast.17) | data formatting | bytes 16777216
  (4 shorter events, 0.1 us)
Async XLA Ops:
  0.0 28.3 %copy-start.2 = (s32[1,1,8,1]{2,3,1,0:T(1,128)S(1)}, s32[1,1,8,1]{2,3,1,0:T(1,128)}, u32[]{:S(2)}) copy-start(s32[1,1,8,1]{2,3,1,0:T(1,128)} %param.9) | copy-start | bytes 100
  0.0 30.4 %copy-start.1 = (f32[64]{0:T(128)S(1)}, f32[64]{0:T(128)}, u32[]{:S(2)}) copy-start(f32[64]{0:T(128)} %param.11) | copy-start | bytes 772
  8.4 3.4 %copy-start = (bf16[32,16,64,128]{3,2,1,0:T(8,128)(2,1)}, bf16[32,16,64,128]{3,2,1,0:T(8,128)(2,1)S(1)}, u32[]{:S(2)}) copy-start(bf16[32,16,64,128]{3,2,1,0:T(8,128)(2,1)S(1)} %broadcast_multiply_fusion) | copy-start | bytes 25165828
  11.8 7.7 %collective-permute-start = (bf16[1,16,64,128]{3,2,1,0:T(8,128)(2,1)S(1)}, bf16[1,16,64,128]{3,2,1,0:T(8,128)(2,1)S(1)}, u32[]{:S(2)}, u32[]{:S(2)}) collective-permute-start(bf16[1,16,64,128]{3,2,1,0:T(8,128)(2,1)S(1)} %get-tuple-element.9), channel_id=1, source_target_pairs={{0,16},{16,32},{32,48},{48,64},{64,80},{80,96},{96,112},{1,17},{17... | collective-permute-start | bytes 786440 | tf_op jit(solution)/shard_map/ppermute | solution.py:20
  13.7 7.5 %collective-permute-start.1 = (bf16[1,16,64,128]{3,2,1,0:T(8,128)(2,1)S(1)}, bf16[1,16,64,128]{3,2,1,0:T(8,128)(2,1)S(1)}, u32[]{:S(2)}, u32[]{:S(2)}) collective-permute-start(bf16[1,16,64,128]{3,2,1,0:T(8,128)(2,1)S(1)} %get-tuple-element.10), channel_id=1, source_target_pairs={{16,0},{32,16},{48,32},{64,48},{80,64},{96,80},{112,96},{17,1},{33... | collective-permute-start | bytes 786440 | tf_op jit(solution)/shard_map/ppermute | solution.py:22
  23.6 15.8 %collective-permute-start.2 = (bf16[34,1,64,128]{3,2,1,0:T(8,128)(2,1)}, bf16[34,1,64,128]{3,2,1,0:T(8,128)(2,1)S(1)}, u32[]{:S(2)}, u32[]{:S(2)}) collective-permute-start(bf16[34,1,64,128]{3,2,1,0:T(8,128)(2,1)} %get-tuple-element.7), channel_id=1, source_target_pairs={{0,1},{1,2},{2,3},{3,4},{4,5},{5,6},{6,7},{7,8},{8,9},{9,10},{10,1... | collective-permute-start | bytes 1671176 | tf_op jit(solution)/shard_map/ppermute | solution.py:20
  27.0 17.2 %collective-permute-start.3 = (bf16[34,1,64,128]{3,2,1,0:T(8,128)(2,1)}, bf16[34,1,64,128]{3,2,1,0:T(8,128)(2,1)}, u32[]{:S(2)}, u32[]{:S(2)}) collective-permute-start(bf16[34,1,64,128]{3,2,1,0:T(8,128)(2,1)} %get-tuple-element.8), channel_id=1, source_target_pairs={{1,0},{2,1},{3,2},{4,3},{5,4},{6,5},{7,6},{8,7},{9,8},{10,9},{11,1... | collective-permute-start | bytes 1671176 | tf_op jit(solution)/shard_map/ppermute | solution.py:22

commit v2 on v1

--- a/solution.py
+++ b/solution.py
@@ -26,7 +26,7 @@
     return cells
 
 
-def conv_kernel(table_ref, x_ref, w_ref, b_ref, m_ref, o_ref):
+def conv_kernel(table_ref, x_ref, w_ref, b_ref, m_ref, o_ref, part_ref):
     slot = pl.program_id(0)
     slots = pl.num_programs(0)
     valid = table_ref[slots + slot]
@@ -34,20 +34,26 @@
 
     @pl.when(valid > 0)
     def _():
-        def body(ex, carry):
-            acc = jnp.zeros((rows, C), jnp.float32)
-            for a in range(3):
-                for b in range(3):
-                    lhs = x_ref[pl.ds(ex + a, 1), pl.ds(b, EDGE), :, :]
-                    lhs = lhs.reshape(rows, lhs.shape[-1])
-                    acc = acc + jnp.dot(lhs, w_ref[a * 3 + b], preferred_element_type=jnp.float32)
+        def taps(xi, carry):
+            part = jnp.zeros((rows, 3 * C), jnp.float32)
+            for b in range(3):
+                lhs = x_ref[pl.ds(xi, 1), pl.ds(b, EDGE), :, :]
+                lhs = lhs.reshape(rows, lhs.shape[-1])
+                part = part + jnp.dot(lhs, w_ref[b], preferred_element_type=jnp.float32)
+            part_ref[xi] = part.T
+            return carry
+
+        lax.fori_loop(0, EDGE + 2, taps, 0)
+
+        def rows_out(ex, carry):
+            pre = (part_ref[ex, 0:C, :] + part_ref[ex + 1, C:2 * C, :]) + part_ref[ex + 2, 2 * C:3 * C, :]
             start = pl.multiple_of(ex * rows, rows)
             mask = m_ref[0, :, pl.ds(start, rows)]
-            value = jnp.maximum(acc.T + b_ref[...], 0.0) * mask
+            value = jnp.maximum(pre + b_ref[...], 0.0) * mask
             o_ref[0, :, pl.ds(start, rows)] = value.astype(o_ref.dtype)
             return carry
 
-        lax.fori_loop(0, EDGE, body, 0)
+        lax.fori_loop(0, EDGE, rows_out, 0)
 
     @pl.when(valid == 0)
     def _():
@@ -78,6 +84,7 @@
                 pl.BlockSpec((1, 1, EDGE**3), lambda j, t: (brick_of(j, t), 0, 0)),
             ],
             out_specs=pl.BlockSpec((1, C, EDGE**3), lambda j, t: (j, 0, 0)),
+            scratch_shapes=[pltpu.VMEM((EDGE + 2, 3 * C, EDGE * EDGE), jnp.float32)],
         ),
         compiler_params=pltpu.CompilerParams(vmem_limit_bytes=48 * 1024 * 1024),
     )(table, shifted, w9, bias_col, masks)
@@ -111,7 +118,7 @@
     brick_of_slot = jnp.sum(jnp.where(hit, order[None, :], 0), axis=1)
     valid = jnp.any(hit, axis=1).astype(jnp.int32)
     table = jnp.concatenate([brick_of_slot, valid]).astype(jnp.int32)
-    w9 = weights.reshape(9, 3 * channels_in, C)
+    w9 = weights.transpose(1, 2, 3, 0, 4).reshape(3, 3 * channels_in, 3 * C)
     bias_col = bias.reshape(C, 1).astype(jnp.float32)
     sending = conv_slots(table, shifted, w9, bias_col, brick_masks, total, bricks_z)
     decoded = lax.all_to_all(sending, "gy", split_axis=0, concat_axis=0, tiled=True)

time: 308 us -> 298 us (0.968)
  Pallas kernels: 100 us -> 88.3 us
    pallas_call x1, Pallas kernels: 100 us -> 88.3 us  [conv_slots(): pl.pallas_call(conv_kernel, out_shape=jax.ShapeDtypeStruct((total, C, EDG...]
    reshape x0 -> x2, local copies, waits for them, and re-layouts: none -> 3.08 us  [per_device(): w9 = weights.transpose(1, 2, 3, 0, 4).reshape(3, 3 * channels_in, 3 * C)]
    unnamed x8 -> x7, local copies, waits for them, and re-layouts: 12.7 us -> 11.3 us
  transfers between devices with their start and end apart: 4 -> 4, of which waited for: 4 -> 4; matrix products, arithmetic and copies ran while one was open for 1% -> 2% of each run, Pallas kernels for 0% -> 0%
where the time goes in v2:
time: 298 us; the launch traced here: 297 us
  blocking collectives  109 us (37%)
  Pallas kernels  88.3 us (30%)
  other arithmetic  48.7 us (16%)
  local copies, waits for them, and re-layouts  25.5 us (9%)
  waiting for transfers between devices  15.1 us (5%)
  starting transfers between devices  10.3 us (3%)
    all_to_all x1, blocking collectives, per_device(): lax.all_to_all(sending, 'gy', split_axis=0, concat_axis=0, tiled=True)  109 us
    pallas_call x1, Pallas kernels, conv_slots(): pl.pallas_call(conv_kernel, out_shape=jax.ShapeDtypeStruct((total, C, EDG...  88.3 us
    concatenate x1, other arithmetic, per_device(): jnp.concatenate([padded[:, :, c:c + extent_z, :] for c in range(3)], axis...  21.2 us
    concatenate x1, other arithmetic, padded_2(): jnp.concatenate([lax.ppermute(tail, axis, [(i, (i + 1) % count) for i in...  17.5 us
    unnamed x7, local copies, waits for them, and re-layouts  11.3 us
    slice x1, local copies, waits for them, and re-layouts, per_device(): padded[:, :, c:c + extent_z, :]  9.07 us
    ppermute x2, waiting for transfers between devices, padded_2(): lax.ppermute(tail, axis, [(i, (i + 1) % count) for i in range(ends)])  8.6 us
    ppermute x2, waiting for transfers between devices, padded_2(): lax.ppermute(head, axis, [((i + 1) % count, i) for i in range(ends)])  6.51 us
  transfers between devices with their start and end apart: 4, of which 4 were waited for; matrix products, arithmetic and copies ran while one was open for 2% of the time, Pallas kernels for 0%

profile of v2, /device:TPU:8, one launch (start us, length us, event | category | flops | bytes accessed | tf_op | source)
XLA Modules:
  0.0 297.0 jit_solution(11685617032646274949)
XLA Ops:
  0.0 0.0 copy-start.2
  0.0 0.8 copy.18
  0.8 0.1 broadcast_in_dim.36
  0.9 0.1 broadcast_in_dim.37
  0.9 0.1 copy.19
  1.0 1.0 multiply_convert_fusion
  2.0 6.3 %broadcast_multiply_fusion = bf16[32,16,64,128]{3,2,1,0:T(8,128)(2,1)S(1)} fusion(bf16[32,16,64,128]{3,2,1,0:T(8,128)(2,1)} %param.6, bf16[32,16,64]{2,1,0:T(8,128)(2,1)S(1)} %multiply_convert_fusion), kind=kLoop, calls=%fused_computation.11 | loop fusion | flops 4194304 | bytes 16842752 | tf_op jit(solution)/shard_map/mul | solution.py:105
  8.3 0.0 copy-start
  8.3 3.4 %copy-done = bf16[32,16,64,128]{3,2,1,0:T(8,128)(2,1)} copy-done((bf16[32,16,64,128]{3,2,1,0:T(8,128)(2,1)}, bf16[32,16,64,128]{3,2,1,0:T(8,128)(2,1)S(1)}, u32[]{:S(2)}) %copy-start) | copy-done | bytes 8388632
  11.7 0.0 copy-start.1
  11.8 1.9 collective-permute-start
  13.7 3.6 %collective-permute-start.1 = (bf16[1,16,64,128]{3,2,1,0:T(8,128)(2,1)S(1)}, bf16[1,16,64,128]{3,2,1,0:T(8,128)(2,1)S(1)}, u32[]{:S(2)}, u32[]{:S(2)}) collective-permute-start(bf16[1,16,64,128]{3,2,1,0:T(8,128)(2,1)S(1)} %get-tuple-element.10), channel_id=1, source_target_pairs={{16,0},{32,16},{48,32},{64,48},{80,64},{96,80},{112,96},{17,1},{33... | collective-permute-start | bytes 786440 | tf_op jit(solution)/shard_map/ppermute | solution.py:22
  17.4 0.5 reshape.46
  17.8 0.0 copy-done.2
  17.8 0.2 convert_reduce_fusion
  18.0 1.4 collective-permute-done
  19.5 1.8 collective-permute-done.1
  21.2 2.3 pad_maximum_fusion.3
  23.6 3.4 %collective-permute-start.2 = (bf16[34,1,64,128]{3,2,1,0:T(8,128)(2,1)}, bf16[34,1,64,128]{3,2,1,0:T(8,128)(2,1)S(1)}, u32[]{:S(2)}, u32[]{:S(2)}) collective-permute-start(bf16[34,1,64,128]{3,2,1,0:T(8,128)(2,1)} %get-tuple-element.7), channel_id=1, source_target_pairs={{0,1},{1,2},{2,3},{3,4},{4,5},{5,6},{6,7},{7,8},{8,9},{9,10},{10,1... | collective-permute-start | bytes 1671176 | tf_op jit(solution)/shard_map/ppermute | solution.py:20
  27.0 1.3 collective-permute-start.3
  28.3 0.1 fusion.6
  28.4 0.1 copy.27
  28.5 0.4 reshape.43.m_ref
  28.9 2.4 copy.24
  31.2 0.7 reshape.47.w_ref
  32.0 0.0 copy-done.1
  32.0 0.1 copy.23.b_ref
  32.1 0.1 select_reduce_fusion
  32.2 0.1 pad_add_fusion.table_ref
  32.3 7.1 %collective-permute-done.2 = bf16[34,1,64,128]{3,2,1,0:T(8,128)(2,1)S(1)} collective-permute-done((bf16[34,1,64,128]{3,2,1,0:T(8,128)(2,1)}, bf16[34,1,64,128]{3,2,1,0:T(8,128)(2,1)S(1)}, u32[]{:S(2)}, u32[]{:S(2)}) %collective-permute-start.2) | collective-permute-done | bytes 557088 | tf_op jit(solution)/shard_map/ppermute | solution.py:20
  39.4 4.8 %collective-permute-done.3 = bf16[34,1,64,128]{3,2,1,0:T(8,128)(2,1)} collective-permute-done((bf16[34,1,64,128]{3,2,1,0:T(8,128)(2,1)}, bf16[34,1,64,128]{3,2,1,0:T(8,128)(2,1)}, u32[]{:S(2)}, u32[]{:S(2)}) %collective-permute-start.3) | collective-permute-done | bytes 557088 | tf_op jit(solution)/shard_map/ppermute | solution.py:22
  44.2 17.5 %select_maximum_fusion = bf16[34,18,66,128]{3,2,1,0:T(8,128)(2,1)S(1)} fusion(bf16[34,1,64,128]{3,2,1,0:T(8,128)(2,1)} %collective-permute-done.3, bf16[34,1,64,128]{3,2,1,0:T(8,128)(2,1)S(1)} %collective-permute-done.2, bf16[1,16,64,128]{3,2,1,0:T(8,128)(2,1)S(1)} %collective-permute-done.1, bf16[32,16,64,128]{3,2,1,0:T(8,128)(2,1)} %copy-done, ...), kind=kLoop, calls=%fused_computation.4 | loop fusion | flops 93063168 | bytes 20367360 | tf_op jit(solution)/shard_map/concatenate | solution.py:18
  61.6 9.1 %fusion.8 = (bf16[34,18,64,128]{3,2,1,0:T(8,128)(2,1)}, bf16[34,18,64,128]{3,2,1,0:T(8,128)(2,1)}) fusion(bf16[34,18,66,128]{3,2,1,0:T(8,128)(2,1)S(1)} %select_maximum_fusion), kind=kLoop, calls=%fused_computation.25 | loop fusion | bytes 40108032 | tf_op jit(solution)/shard_map/slice | solution.py:108
  70.7 21.2 %pad_maximum_fusion.x_ref = bf16[34,18,64,384]{3,2,1,0:T(8,128)(2,1)} fusion(bf16[34,18,64,128]{3,2,1,0:T(8,128)(2,1)} %get-tuple-element.6, bf16[34,1,64,128]{3,2,1,0:T(8,128)(2,1)} %collective-permute-done.3, bf16[1,16,64,128]{3,2,1,0:T(8,128)(2,1)S(1)} %collective-permute-done.1, bf16[32,16,64,128]{3,2,1,0:T(8,128)(2,1)} %copy-done, ...), kind=kLoop, calls=%fused_computation.2 | loop fusion | flops 210567168 | bytes 60162048 | tf_op jit(solution)/shard_map/concatenate | solution.py:108
  91.9 88.3 %shard_map.67 = bf16[16,64,4096]{2,1,0:T(8,128)(2,1)} custom-call(s32[32]{0:T(128)S(1)} %pad_add_fusion.table_ref, bf16[34,18,64,384]{3,2,1,0:T(8,128)(2,1)} %pad_maximum_fusion.x_ref, bf16[3,384,192]{2,1,0:T(8,128)(2,1)S(1)} %reshape.47.w_ref, f32[64,1]{1,0:T(8,128)S(1)} %copy.23.b_ref, f32[8,1,4096]{2,1,0:T(1,128)S(1)} %reshape.43.m_ref), custom_call_target="tpu_custom_call" | custom-call | tf_op jit(solution)/shard_map/pallas_call | solution.py:74
  180.2 109.0 %all_to_all.5 = bf16[16,64,4096]{2,1,0:T(8,128)(2,1)} all-to-all(bf16[16,64,4096]{2,1,0:T(8,128)(2,1)} %shard_map.67), channel_id=1, replica_groups=mesh['gx'=8,'gy'=16] {'gy'}, dimensions={0} | all-to-all | bytes 16777216 | tf_op jit(solution)/shard_map/all_to_all | solution.py:124
  289.2 7.9 %copy.29 = bf16[1,16,64,4096]{3,2,1,0:T(8,128)(2,1)} copy(bf16[1,16,64,4096]{3,2,1,0:T(8,128)(2,1)} %bitcast.16) | data formatting | bytes 16777216
  (4 shorter events, 0.1 us)
Async XLA Ops:
  0.0 17.8 %copy-start.2 = (s32[1,1,8,1]{2,3,1,0:T(1,128)S(1)}, s32[1,1,8,1]{2,3,1,0:T(1,128)}, u32[]{:S(2)}) copy-start(s32[1,1,8,1]{2,3,1,0:T(1,128)} %param.9) | copy-start | bytes 100
  8.3 3.4 %copy-start = (bf16[32,16,64,128]{3,2,1,0:T(8,128)(2,1)}, bf16[32,16,64,128]{3,2,1,0:T(8,128)(2,1)S(1)}, u32[]{:S(2)}) copy-start(bf16[32,16,64,128]{3,2,1,0:T(8,128)(2,1)S(1)} %broadcast_multiply_fusion) | copy-start | bytes 25165828
  11.7 20.3 %copy-start.1 = (f32[64]{0:T(128)S(1)}, f32[64]{0:T(128)}, u32[]{:S(2)}) copy-start(f32[64]{0:T(128)} %param.11) | copy-start | bytes 772
  11.8 7.7 %collective-permute-start = (bf16[1,16,64,128]{3,2,1,0:T(8,128)(2,1)S(1)}, bf16[1,16,64,128]{3,2,1,0:T(8,128)(2,1)S(1)}, u32[]{:S(2)}, u32[]{:S(2)}) collective-permute-start(bf16[1,16,64,128]{3,2,1,0:T(8,128)(2,1)S(1)} %get-tuple-element.9), channel_id=1, source_target_pairs={{0,16},{16,32},{32,48},{48,64},{64,80},{80,96},{96,112},{1,17},{17... | collective-permute-start | bytes 786440 | tf_op jit(solution)/shard_map/ppermute | solution.py:20
  13.7 7.5 %collective-permute-start.1 = (bf16[1,16,64,128]{3,2,1,0:T(8,128)(2,1)S(1)}, bf16[1,16,64,128]{3,2,1,0:T(8,128)(2,1)S(1)}, u32[]{:S(2)}, u32[]{:S(2)}) collective-permute-start(bf16[1,16,64,128]{3,2,1,0:T(8,128)(2,1)S(1)} %get-tuple-element.10), channel_id=1, source_target_pairs={{16,0},{32,16},{48,32},{64,48},{80,64},{96,80},{112,96},{17,1},{33... | collective-permute-start | bytes 786440 | tf_op jit(solution)/shard_map/ppermute | solution.py:22
  23.6 15.8 %collective-permute-start.2 = (bf16[34,1,64,128]{3,2,1,0:T(8,128)(2,1)}, bf16[34,1,64,128]{3,2,1,0:T(8,128)(2,1)S(1)}, u32[]{:S(2)}, u32[]{:S(2)}) collective-permute-start(bf16[34,1,64,128]{3,2,1,0:T(8,128)(2,1)} %get-tuple-element.7), channel_id=1, source_target_pairs={{0,1},{1,2},{2,3},{3,4},{4,5},{5,6},{6,7},{7,8},{8,9},{9,10},{10,1... | collective-permute-start | bytes 1671176 | tf_op jit(solution)/shard_map/ppermute | solution.py:20
  27.0 17.2 %collective-permute-start.3 = (bf16[34,1,64,128]{3,2,1,0:T(8,128)(2,1)}, bf16[34,1,64,128]{3,2,1,0:T(8,128)(2,1)}, u32[]{:S(2)}, u32[]{:S(2)}) collective-permute-start(bf16[34,1,64,128]{3,2,1,0:T(8,128)(2,1)} %get-tuple-element.8), channel_id=1, source_target_pairs={{1,0},{2,1},{3,2},{4,3},{5,4},{6,5},{7,6},{8,7},{9,8},{10,9},{11,1... | collective-permute-start | bytes 1671176 | tf_op jit(solution)/shard_map/ppermute | solution.py:22

commit v3 on v2

--- a/solution.py
+++ b/solution.py
@@ -31,29 +31,30 @@
     slots = pl.num_programs(0)
     valid = table_ref[slots + slot]
     rows = EDGE * EDGE
+    group = 6
+    chunk = 4 * rows
 
     @pl.when(valid > 0)
     def _():
-        def taps(xi, carry):
-            part = jnp.zeros((rows, 3 * C), jnp.float32)
+        for first in range(0, EDGE + 2, group):
+            part = jnp.zeros((group * rows, 3 * C), jnp.float32)
             for b in range(3):
-                lhs = x_ref[pl.ds(xi, 1), pl.ds(b, EDGE), :, :]
-                lhs = lhs.reshape(rows, lhs.shape[-1])
+                lhs = x_ref[first:first + group, b:b + EDGE, :, :]
+                lhs = lhs.reshape(group * rows, lhs.shape[-1])
                 part = part + jnp.dot(lhs, w_ref[b], preferred_element_type=jnp.float32)
-            part_ref[xi] = part.T
+            part_ref[:, first * rows:(first + group) * rows] = part.T
+
+        def rows_out(piece, carry):
+            start = pl.multiple_of(piece * chunk, chunk)
+            pre = part_ref[0:C, pl.ds(start, chunk)]
+            pre = pre + part_ref[C:2 * C, pl.ds(start + rows, chunk)]
+            pre = pre + part_ref[2 * C:3 * C, pl.ds(start + 2 * rows, chunk)]
+            mask = m_ref[0, :, pl.ds(start, chunk)]
+            value = jnp.maximum(pre + b_ref[...], 0.0) * mask
+            o_ref[0, :, pl.ds(start, chunk)] = value.astype(o_ref.dtype)
             return carry
 
-        lax.fori_loop(0, EDGE + 2, taps, 0)
-
-        def rows_out(ex, carry):
-            pre = (part_ref[ex, 0:C, :] + part_ref[ex + 1, C:2 * C, :]) + part_ref[ex + 2, 2 * C:3 * C, :]
-            start = pl.multiple_of(ex * rows, rows)
-            mask = m_ref[0, :, pl.ds(start, rows)]
-            value = jnp.maximum(pre + b_ref[...], 0.0) * mask
-            o_ref[0, :, pl.ds(start, rows)] = value.astype(o_ref.dtype)
-            return carry
-
-        lax.fori_loop(0, EDGE, rows_out, 0)
+        lax.fori_loop(0, EDGE**3 // chunk, rows_out, 0)
 
     @pl.when(valid == 0)
     def _():
@@ -84,7 +85,7 @@
                 pl.BlockSpec((1, 1, EDGE**3), lambda j, t: (brick_of(j, t), 0, 0)),
             ],
             out_specs=pl.BlockSpec((1, C, EDGE**3), lambda j, t: (j, 0, 0)),
-            scratch_shapes=[pltpu.VMEM((EDGE + 2, 3 * C, EDGE * EDGE), jnp.float32)],
+            scratch_shapes=[pltpu.VMEM((3 * C, (EDGE + 2) * EDGE * EDGE), jnp.float32)],
         ),
         compiler_params=pltpu.CompilerParams(vmem_limit_bytes=48 * 1024 * 1024),
     )(table, shifted, w9, bias_col, masks)

time: 298 us -> 251 us (0.84)
  Pallas kernels: 88.3 us -> 42.4 us
    pallas_call x1, Pallas kernels: 88.3 us -> 42.4 us  [conv_slots(): pl.pallas_call(conv_kernel, out_shape=jax.ShapeDtypeStruct((total, C, EDG...]
where the time goes in v3:
time: 251 us; the launch traced here: 250 us
  blocking collectives  108 us (43%)
  other arithmetic  48.7 us (19%)
  Pallas kernels  42.4 us (17%)
  local copies, waits for them, and re-layouts  25.5 us (10%)
  waiting for transfers between devices  15.1 us (6%)
  starting transfers between devices  10.3 us (4%)
    all_to_all x1, blocking collectives, per_device(): lax.all_to_all(sending, 'gy', split_axis=0, concat_axis=0, tiled=True)  108 us
    pallas_call x1, Pallas kernels, conv_slots(): pl.pallas_call(conv_kernel, out_shape=jax.ShapeDtypeStruct((total, C, EDG...  42.4 us
    concatenate x1, other arithmetic, per_device(): jnp.concatenate([padded[:, :, c:c + extent_z, :] for c in range(3)], axis...  21.2 us
    concatenate x1, other arithmetic, padded_2(): jnp.concatenate([lax.ppermute(tail, axis, [(i, (i + 1) % count) for i in...  17.5 us
    unnamed x7, local copies, waits for them, and re-layouts  11.3 us
    slice x1, local copies, waits for them, and re-layouts, per_device(): padded[:, :, c:c + extent_z, :]  9.07 us
    ppermute x2, waiting for transfers between devices, padded_2(): lax.ppermute(tail, axis, [(i, (i + 1) % count) for i in range(ends)])  8.6 us
    ppermute x2, waiting for transfers between devices, padded_2(): lax.ppermute(head, axis, [((i + 1) % count, i) for i in range(ends)])  6.51 us
  transfers between devices with their start and end apart: 4, of which 4 were waited for; matrix products, arithmetic and copies ran while one was open for 2% of the time, Pallas kernels for 0%

profile of v3, /device:TPU:8, one launch (start us, length us, event | category | flops | bytes accessed | tf_op | source)
XLA Modules:
  0.0 250.3 jit_solution(14867681233738499127)
XLA Ops:
  0.0 0.0 copy-start.2
  0.0 0.8 copy.18
  0.8 0.1 broadcast_in_dim.36
  0.9 0.1 broadcast_in_dim.37
  0.9 0.1 copy.19
  1.0 1.0 multiply_convert_fusion
  2.0 6.3 %broadcast_multiply_fusion = bf16[32,16,64,128]{3,2,1,0:T(8,128)(2,1)S(1)} fusion(bf16[32,16,64,128]{3,2,1,0:T(8,128)(2,1)} %param.6, bf16[32,16,64]{2,1,0:T(8,128)(2,1)S(1)} %multiply_convert_fusion), kind=kLoop, calls=%fused_computation.11 | loop fusion | flops 4194304 | bytes 16842752 | tf_op jit(solution)/shard_map/mul | solution.py:106
  8.3 0.0 copy-start
  8.3 3.4 %copy-done = bf16[32,16,64,128]{3,2,1,0:T(8,128)(2,1)} copy-done((bf16[32,16,64,128]{3,2,1,0:T(8,128)(2,1)}, bf16[32,16,64,128]{3,2,1,0:T(8,128)(2,1)S(1)}, u32[]{:S(2)}) %copy-start) | copy-done | bytes 8388632
  11.7 0.0 copy-start.1
  11.8 1.9 collective-permute-start
  13.7 3.6 %collective-permute-start.1 = (bf16[1,16,64,128]{3,2,1,0:T(8,128)(2,1)S(1)}, bf16[1,16,64,128]{3,2,1,0:T(8,128)(2,1)S(1)}, u32[]{:S(2)}, u32[]{:S(2)}) collective-permute-start(bf16[1,16,64,128]{3,2,1,0:T(8,128)(2,1)S(1)} %get-tuple-element.10), channel_id=1, source_target_pairs={{16,0},{32,16},{48,32},{64,48},{80,64},{96,80},{112,96},{17,1},{33... | collective-permute-start | bytes 786440 | tf_op jit(solution)/shard_map/ppermute | solution.py:22
  17.4 0.5 reshape.46
  17.8 0.0 copy-done.2
  17.8 0.2 convert_reduce_fusion
  18.0 1.4 collective-permute-done
  19.5 1.8 collective-permute-done.1
  21.2 2.3 pad_maximum_fusion.3
  23.6 3.4 %collective-permute-start.2 = (bf16[34,1,64,128]{3,2,1,0:T(8,128)(2,1)}, bf16[34,1,64,128]{3,2,1,0:T(8,128)(2,1)S(1)}, u32[]{:S(2)}, u32[]{:S(2)}) collective-permute-start(bf16[34,1,64,128]{3,2,1,0:T(8,128)(2,1)} %get-tuple-element.7), channel_id=1, source_target_pairs={{0,1},{1,2},{2,3},{3,4},{4,5},{5,6},{6,7},{7,8},{8,9},{9,10},{10,1... | collective-permute-start | bytes 1671176 | tf_op jit(solution)/shard_map/ppermute | solution.py:20
  27.0 1.3 collective-permute-start.3
  28.3 0.1 fusion.6
  28.4 0.1 copy.27
  28.5 0.4 reshape.43.m_ref
  28.9 2.4 copy.24
  31.2 0.7 reshape.47.w_ref
  32.0 0.0 copy-done.1
  32.0 0.1 copy.23.b_ref
  32.1 0.1 select_reduce_fusion
  32.2 0.1 pad_add_fusion.table_ref
  32.3 7.1 %collective-permute-done.2 = bf16[34,1,64,128]{3,2,1,0:T(8,128)(2,1)S(1)} collective-permute-done((bf16[34,1,64,128]{3,2,1,0:T(8,128)(2,1)}, bf16[34,1,64,128]{3,2,1,0:T(8,128)(2,1)S(1)}, u32[]{:S(2)}, u32[]{:S(2)}) %collective-permute-start.2) | collective-permute-done | bytes 557088 | tf_op jit(solution)/shard_map/ppermute | solution.py:20
  39.4 4.8 %collective-permute-done.3 = bf16[34,1,64,128]{3,2,1,0:T(8,128)(2,1)} collective-permute-done((bf16[34,1,64,128]{3,2,1,0:T(8,128)(2,1)}, bf16[34,1,64,128]{3,2,1,0:T(8,128)(2,1)}, u32[]{:S(2)}, u32[]{:S(2)}) %collective-permute-start.3) | collective-permute-done | bytes 557088 | tf_op jit(solution)/shard_map/ppermute | solution.py:22
  44.2 17.5 %select_maximum_fusion = bf16[34,18,66,128]{3,2,1,0:T(8,128)(2,1)S(1)} fusion(bf16[34,1,64,128]{3,2,1,0:T(8,128)(2,1)} %collective-permute-done.3, bf16[34,1,64,128]{3,2,1,0:T(8,128)(2,1)S(1)} %collective-permute-done.2, bf16[1,16,64,128]{3,2,1,0:T(8,128)(2,1)S(1)} %collective-permute-done.1, bf16[32,16,64,128]{3,2,1,0:T(8,128)(2,1)} %copy-done, ...), kind=kLoop, calls=%fused_computation.4 | loop fusion | flops 93063168 | bytes 20367360 | tf_op jit(solution)/shard_map/concatenate | solution.py:18
  61.6 9.1 %fusion.8 = (bf16[34,18,64,128]{3,2,1,0:T(8,128)(2,1)}, bf16[34,18,64,128]{3,2,1,0:T(8,128)(2,1)}) fusion(bf16[34,18,66,128]{3,2,1,0:T(8,128)(2,1)S(1)} %select_maximum_fusion), kind=kLoop, calls=%fused_computation.25 | loop fusion | bytes 40108032 | tf_op jit(solution)/shard_map/slice | solution.py:109
  70.7 21.2 %pad_maximum_fusion.x_ref = bf16[34,18,64,384]{3,2,1,0:T(8,128)(2,1)} fusion(bf16[34,18,64,128]{3,2,1,0:T(8,128)(2,1)} %get-tuple-element.6, bf16[34,1,64,128]{3,2,1,0:T(8,128)(2,1)} %collective-permute-done.3, bf16[1,16,64,128]{3,2,1,0:T(8,128)(2,1)S(1)} %collective-permute-done.1, bf16[32,16,64,128]{3,2,1,0:T(8,128)(2,1)} %copy-done, ...), kind=kLoop, calls=%fused_computation.2 | loop fusion | flops 210567168 | bytes 60162048 | tf_op jit(solution)/shard_map/concatenate | solution.py:109
  91.9 42.4 %shard_map.67 = bf16[16,64,4096]{2,1,0:T(8,128)(2,1)} custom-call(s32[32]{0:T(128)S(1)} %pad_add_fusion.table_ref, bf16[34,18,64,384]{3,2,1,0:T(8,128)(2,1)} %pad_maximum_fusion.x_ref, bf16[3,384,192]{2,1,0:T(8,128)(2,1)S(1)} %reshape.47.w_ref, f32[64,1]{1,0:T(8,128)S(1)} %copy.23.b_ref, f32[8,1,4096]{2,1,0:T(1,128)S(1)} %reshape.43.m_ref), custom_call_target="tpu_custom_call" | custom-call | tf_op jit(solution)/shard_map/pallas_call | solution.py:75
  134.3 108.1 %all_to_all.5 = bf16[16,64,4096]{2,1,0:T(8,128)(2,1)} all-to-all(bf16[16,64,4096]{2,1,0:T(8,128)(2,1)} %shard_map.67), channel_id=1, replica_groups=mesh['gx'=8,'gy'=16] {'gy'}, dimensions={0} | all-to-all | bytes 16777216 | tf_op jit(solution)/shard_map/all_to_all | solution.py:125
  242.4 7.9 %copy.29 = bf16[1,16,64,4096]{3,2,1,0:T(8,128)(2,1)} copy(bf16[1,16,64,4096]{3,2,1,0:T(8,128)(2,1)} %bitcast.16) | data formatting | bytes 16777216
  (4 shorter events, 0.1 us)
Async XLA Ops:
  0.0 17.8 %copy-start.2 = (s32[1,1,8,1]{2,3,1,0:T(1,128)S(1)}, s32[1,1,8,1]{2,3,1,0:T(1,128)}, u32[]{:S(2)}) copy-start(s32[1,1,8,1]{2,3,1,0:T(1,128)} %param.9) | copy-start | bytes 100
  8.3 3.4 %copy-start = (bf16[32,16,64,128]{3,2,1,0:T(8,128)(2,1)}, bf16[32,16,64,128]{3,2,1,0:T(8,128)(2,1)S(1)}, u32[]{:S(2)}) copy-start(bf16[32,16,64,128]{3,2,1,0:T(8,128)(2,1)S(1)} %broadcast_multiply_fusion) | copy-start | bytes 25165828
  11.7 20.3 %copy-start.1 = (f32[64]{0:T(128)S(1)}, f32[64]{0:T(128)}, u32[]{:S(2)}) copy-start(f32[64]{0:T(128)} %param.11) | copy-start | bytes 772
  11.8 7.7 %collective-permute-start = (bf16[1,16,64,128]{3,2,1,0:T(8,128)(2,1)S(1)}, bf16[1,16,64,128]{3,2,1,0:T(8,128)(2,1)S(1)}, u32[]{:S(2)}, u32[]{:S(2)}) collective-permute-start(bf16[1,16,64,128]{3,2,1,0:T(8,128)(2,1)S(1)} %get-tuple-element.9), channel_id=1, source_target_pairs={{0,16},{16,32},{32,48},{48,64},{64,80},{80,96},{96,112},{1,17},{17... | collective-permute-start | bytes 786440 | tf_op jit(solution)/shard_map/ppermute | solution.py:20
  13.7 7.5 %collective-permute-start.1 = (bf16[1,16,64,128]{3,2,1,0:T(8,128)(2,1)S(1)}, bf16[1,16,64,128]{3,2,1,0:T(8,128)(2,1)S(1)}, u32[]{:S(2)}, u32[]{:S(2)}) collective-permute-start(bf16[1,16,64,128]{3,2,1,0:T(8,128)(2,1)S(1)} %get-tuple-element.10), channel_id=1, source_target_pairs={{16,0},{32,16},{48,32},{64,48},{80,64},{96,80},{112,96},{17,1},{33... | collective-permute-start | bytes 786440 | tf_op jit(solution)/shard_map/ppermute | solution.py:22
  23.6 15.8 %collective-permute-start.2 = (bf16[34,1,64,128]{3,2,1,0:T(8,128)(2,1)}, bf16[34,1,64,128]{3,2,1,0:T(8,128)(2,1)S(1)}, u32[]{:S(2)}, u32[]{:S(2)}) collective-permute-start(bf16[34,1,64,128]{3,2,1,0:T(8,128)(2,1)} %get-tuple-element.7), channel_id=1, source_target_pairs={{0,1},{1,2},{2,3},{3,4},{4,5},{5,6},{6,7},{7,8},{8,9},{9,10},{10,1... | collective-permute-start | bytes 1671176 | tf_op jit(solution)/shard_map/ppermute | solution.py:20
  27.0 17.2 %collective-permute-start.3 = (bf16[34,1,64,128]{3,2,1,0:T(8,128)(2,1)}, bf16[34,1,64,128]{3,2,1,0:T(8,128)(2,1)}, u32[]{:S(2)}, u32[]{:S(2)}) collective-permute-start(bf16[34,1,64,128]{3,2,1,0:T(8,128)(2,1)} %get-tuple-element.8), channel_id=1, source_target_pairs={{1,0},{2,1},{3,2},{4,3},{5,4},{6,5},{7,6},{8,7},{9,8},{10,9},{11,1... | collective-permute-start | bytes 1671176 | tf_op jit(solution)/shard_map/ppermute | solution.py:22

commit v4 on v3

--- a/solution.py
+++ b/solution.py
@@ -88,6 +88,11 @@
             scratch_shapes=[pltpu.VMEM((3 * C, (EDGE + 2) * EDGE * EDGE), jnp.float32)],
         ),
         compiler_params=pltpu.CompilerParams(vmem_limit_bytes=48 * 1024 * 1024),
+        cost_estimate=pl.CostEstimate(
+            flops=total * 2 * (EDGE + 2) * EDGE * EDGE * 9 * depth * C,
+            bytes_accessed=total * (shifted.dtype.itemsize * (EDGE + 2) * span * EDGE * depth + 2 * C * EDGE**3),
+            transcendentals=0,
+        ),
     )(table, shifted, w9, bias_col, masks)
 
 
@@ -118,11 +123,25 @@
     hit = slots[None, :] == jnp.arange(total, dtype=jnp.int32)[:, None]
     brick_of_slot = jnp.sum(jnp.where(hit, order[None, :], 0), axis=1)
     valid = jnp.any(hit, axis=1).astype(jnp.int32)
-    table = jnp.concatenate([brick_of_slot, valid]).astype(jnp.int32)
+    me = lax.axis_index("gy")
     w9 = weights.transpose(1, 2, 3, 0, 4).reshape(3, 3 * channels_in, 3 * C)
     bias_col = bias.reshape(C, 1).astype(jnp.float32)
-    sending = conv_slots(table, shifted, w9, bias_col, brick_masks, total, bricks_z)
-    decoded = lax.all_to_all(sending, "gy", split_axis=0, concat_axis=0, tiled=True)
+    chunks = 4
+    per_chunk = total // chunks
+    received = []
+    for m in range(chunks):
+        shifts = jnp.arange(m * per_chunk, (m + 1) * per_chunk, dtype=jnp.int32)
+        wanted = lax.rem(me + shifts, total)
+        table = jnp.concatenate([brick_of_slot[wanted], valid[wanted]]).astype(jnp.int32)
+        out = conv_slots(table, shifted, w9, bias_col, brick_masks, per_chunk, bricks_z)
+        for i in range(per_chunk):
+            k = m * per_chunk + i
+            piece = out[i]
+            if k:
+                piece = lax.ppermute(piece, "gy", [(src, (src + k) % groups) for src in range(groups)])
+            received.append(piece)
+    flipped = jnp.stack([received[(-j) % total] for j in range(total)])
+    decoded = jnp.roll(flipped, me, axis=0)
     return decoded[None]
 
 

time: 251 us -> 362 us (1.44)
  the two profiles are of different devices: /device:TPU:8 before, /device:TPU:24 now
where the time goes in v4:
time: 362 us; the launch traced here: 361 us
  waiting for transfers between devices  182 us (50%)
  local copies, waits for them, and re-layouts  54.7 us (15%)
  other arithmetic  49.1 us (14%)
  Pallas kernels  47.3 us (13%)
  starting transfers between devices  28 us (8%)
    ppermute x15, waiting for transfers between devices, per_device(): lax.ppermute(piece, 'gy', [(src, (src + k) % groups) for src in range(gro...  174 us
    pallas_call x4, Pallas kernels, conv_slots(): pl.pallas_call(conv_kernel, out_shape=jax.ShapeDtypeStruct((total, C, EDG...  47.3 us
    unnamed x36, local copies, waits for them, and re-layouts  25.2 us
    concatenate x1, other arithmetic, per_device(): jnp.concatenate([padded[:, :, c:c + extent_z, :] for c in range(3)], axis...  21.2 us
    ppermute x15, starting transfers between devices, per_device(): lax.ppermute(piece, 'gy', [(src, (src + k) % groups) for src in range(gro...  17.7 us
    concatenate x1, other arithmetic, padded_2(): jnp.concatenate([lax.ppermute(tail, axis, [(i, (i + 1) % count) for i in...  17.5 us
    slice x1, local copies, waits for them, and re-layouts, per_device(): padded[:, :, c:c + extent_z, :]  9.03 us
    broadcast_in_dim x1, local copies, waits for them, and re-layouts, per_device(): return decoded[None]  7.89 us
  transfers between devices with their start and end apart: 19, of which 11 were waited for; matrix products, arithmetic and copies ran while one was open for 6% of the time, Pallas kernels for 2%

profile of v4, /device:TPU:24, one launch (start us, length us, event | category | flops | bytes accessed | tf_op | source)
XLA Modules:
  0.0 361.4 jit_solution(8591179721666674737)
XLA Ops:
  0.0 0.8 copy.27
  1.0 1.0 multiply_convert_fusion
  2.0 6.3 %broadcast_multiply_fusion = bf16[32,16,64,128]{3,2,1,0:T(8,128)(2,1)S(1)} fusion(bf16[32,16,64,128]{3,2,1,0:T(8,128)(2,1)} %param.6, bf16[32,16,64]{2,1,0:T(8,128)(2,1)S(1)} %multiply_convert_fusion), kind=kLoop, calls=%fused_computation.20 | loop fusion | flops 4194304 | bytes 16842752 | tf_op jit(solution)/shard_map/mul | solution.py:111
  8.4 1.9 collective-permute-start
  10.3 3.6 %collective-permute-start.1 = (bf16[1,16,64,128]{3,2,1,0:T(8,128)(2,1)S(1)}, bf16[1,16,64,128]{3,2,1,0:T(8,128)(2,1)S(1)}, u32[]{:S(2)}, u32[]{:S(2)}) collective-permute-start(bf16[1,16,64,128]{3,2,1,0:T(8,128)(2,1)S(1)} %get-tuple-element.10), channel_id=1, source_target_pairs={{16,0},{32,16},{48,32},{64,48},{80,64},{96,80},{112,96},{17,1},{33... | collective-permute-start | bytes 786440 | tf_op jit(solution)/shard_map/ppermute | solution.py:22
  18.3 2.4 pad_maximum_fusion.3
  20.7 3.4 collective-permute-start.2
  24.1 1.3 collective-permute-start.3
  27.8 2.4 copy.39
  31.2 4.0 %collective-permute-done.2 = bf16[34,1,64,128]{3,2,1,0:T(8,128)(2,1)S(1)} collective-permute-done((bf16[34,1,64,128]{3,2,1,0:T(8,128)(2,1)}, bf16[34,1,64,128]{3,2,1,0:T(8,128)(2,1)S(1)}, u32[]{:S(2)}, u32[]{:S(2)}) %collective-permute-start.2) | collective-permute-done | bytes 557088 | tf_op jit(solution)/shard_map/ppermute | solution.py:20
  35.2 4.1 %collective-permute-done.3 = bf16[34,1,64,128]{3,2,1,0:T(8,128)(2,1)} collective-permute-done((bf16[34,1,64,128]{3,2,1,0:T(8,128)(2,1)}, bf16[34,1,64,128]{3,2,1,0:T(8,128)(2,1)}, u32[]{:S(2)}, u32[]{:S(2)}) %collective-permute-start.3) | collective-permute-done | bytes 557088 | tf_op jit(solution)/shard_map/ppermute | solution.py:22
  39.4 17.5 %select_maximum_fusion = bf16[34,18,66,128]{3,2,1,0:T(8,128)(2,1)S(1)} fusion(bf16[34,1,64,128]{3,2,1,0:T(8,128)(2,1)} %collective-permute-done.3, bf16[34,1,64,128]{3,2,1,0:T(8,128)(2,1)S(1)} %collective-permute-done.2, bf16[1,16,64,128]{3,2,1,0:T(8,128)(2,1)S(1)} %collective-permute-done.1, bf16[32,16,64,128]{3,2,1,0:T(8,128)(2,1)} %copy-done, ...), kind=kLoop, calls=%fused_computation.12 | loop fusion | flops 93063168 | bytes 20367360 | tf_op jit(solution)/shard_map/concatenate | solution.py:18
  56.8 9.0 %fusion.16 = (bf16[34,18,64,128]{3,2,1,0:T(8,128)(2,1)}, bf16[34,18,64,128]{3,2,1,0:T(8,128)(2,1)}) fusion(bf16[34,18,66,128]{3,2,1,0:T(8,128)(2,1)S(1)} %select_maximum_fusion), kind=kLoop, calls=%fused_computation.108 | loop fusion | bytes 40108032 | tf_op jit(solution)/shard_map/slice | solution.py:114
  65.8 21.2 %pad_maximum_fusion.x_ref = bf16[34,18,64,384]{3,2,1,0:T(8,128)(2,1)} fusion(bf16[34,18,64,128]{3,2,1,0:T(8,128)(2,1)} %get-tuple-element.6, bf16[34,1,64,128]{3,2,1,0:T(8,128)(2,1)} %collective-permute-done.3, bf16[1,16,64,128]{3,2,1,0:T(8,128)(2,1)S(1)} %collective-permute-done.1, bf16[32,16,64,128]{3,2,1,0:T(8,128)(2,1)} %copy-done, ...), kind=kLoop, calls=%fused_computation.10 | loop fusion | flops 210567168 | bytes 60162048 | tf_op jit(solution)/shard_map/concatenate | solution.py:114
  87.0 20.4 %shard_map.67 = bf16[4,64,4096]{2,1,0:T(8,128)(2,1)S(1)} custom-call(s32[8]{0:T(128)S(1)} %pad_add_fusion.table_ref, bf16[34,18,64,384]{3,2,1,0:T(8,128)(2,1)} %pad_maximum_fusion.x_ref, bf16[3,384,192]{2,1,0:T(8,128)(2,1)S(1)} %reshape.256.w_ref, f32[64,1]{1,0:T(8,128)S(1)} %copy.32.b_ref, f32[8,1,4096]{2,1,0:T(1,128)S(1)} %reshape.188.m_ref), custom_call_target="tpu_custom_call" | custom-call | flops 8153726976 | bytes 18022400 | tf_op jit(solution)/shard_map/pallas_call | solution.py:75
  107.5 20.7 %shard_map.70 = bf16[4,64,4096]{2,1,0:T(8,128)(2,1)S(1)} custom-call(s32[8]{0:T(128)S(1)} %pad_add_fusion.3.table_ref, bf16[34,18,64,384]{3,2,1,0:T(8,128)(2,1)} %pad_maximum_fusion.x_ref, bf16[3,384,192]{2,1,0:T(8,128)(2,1)S(1)} %reshape.256.w_ref, f32[64,1]{1,0:T(8,128)S(1)} %copy.32.b_ref, f32[8,1,4096]{2,1,0:T(1,128)S(1)} %reshape.188.m_ref), custom_call_target="tpu_custom_call" | custom-call | flops 8153726976 | bytes 18022400 | tf_op jit(solution)/shard_map/pallas_call | solution.py:75
  128.4 4.5 %collective-permute-start.14 = (bf16[64,4096]{1,0:T(8,128)(2,1)S(1)}, bf16[64,4096]{1,0:T(8,128)(2,1)S(1)}, u32[]{:S(2)}, u32[]{:S(2)}) collective-permute-start(bf16[64,4096]{1,0:T(8,128)(2,1)S(1)} %get-tuple-element.16), channel_id=1, source_target_pairs={{0,5},{1,6},{2,7},{3,8},{4,9},{5,10},{6,11},{7,12},{8,13},{9,14},{... | collective-permute-start | bytes 1572872 | tf_op jit(solution)/shard_map/ppermute | solution.py:141
  133.0 1.6 collective-permute-start.12
  134.6 3.1 shard_map.69
  137.7 3.1 shard_map.68
  141.1 7.5 %collective-permute-start.4 = (bf16[64,4096]{1,0:T(8,128)(2,1)S(1)}, bf16[64,4096]{1,0:T(8,128)(2,1)S(1)}, u32[]{:S(2)}, u32[]{:S(2)}) collective-permute-start(bf16[64,4096]{1,0:T(8,128)(2,1)S(1)} %get-tuple-element.26), channel_id=1, source_target_pairs={{0,15},{1,0},{2,1},{3,2},{4,3},{5,4},{6,5},{7,6},{8,7},{9,8},{10,9... | collective-permute-start | bytes 1572872 | tf_op jit(solution)/shard_map/ppermute | solution.py:141
  148.7 1.0 slice_bitcast_fusion
  149.7 35.1 %collective-permute-done.4 = bf16[64,4096]{1,0:T(8,128)(2,1)S(1)} collective-permute-done((bf16[64,4096]{1,0:T(8,128)(2,1)S(1)}, bf16[64,4096]{1,0:T(8,128)(2,1)S(1)}, u32[]{:S(2)}, u32[]{:S(2)}) %collective-permute-start.4) | collective-permute-done | bytes 524320 | tf_op jit(solution)/shard_map/ppermute | solution.py:141
  184.7 0.8 bitcast_dynamic-update-slice_fusion.28
  185.6 13.4 %collective-permute-done.5 = bf16[64,4096]{1,0:T(8,128)(2,1)S(1)} collective-permute-done((bf16[64,4096]{1,0:T(8,128)(2,1)S(1)}, bf16[64,4096]{1,0:T(8,128)(2,1)S(1)}, u32[]{:S(2)}, u32[]{:S(2)}) %collective-permute-start.5) | collective-permute-done | bytes 524320 | tf_op jit(solution)/shard_map/ppermute | solution.py:141
  199.0 0.8 bitcast_dynamic-update-slice_fusion.26
  199.8 9.6 %collective-permute-done.6 = bf16[64,4096]{1,0:T(8,128)(2,1)S(1)} collective-permute-done((bf16[64,4096]{1,0:T(8,128)(2,1)S(1)}, bf16[64,4096]{1,0:T(8,128)(2,1)S(1)}, u32[]{:S(2)}, u32[]{:S(2)}) %collective-permute-start.6) | collective-permute-done | bytes 524320 | tf_op jit(solution)/shard_map/ppermute | solution.py:141
  209.4 0.8 bitcast_dynamic-update-slice_fusion.24
  210.2 13.9 %collective-permute-done.7 = bf16[64,4096]{1,0:T(8,128)(2,1)S(1)} collective-permute-done((bf16[64,4096]{1,0:T(8,128)(2,1)S(1)}, bf16[64,4096]{1,0:T(8,128)(2,1)S(1)}, u32[]{:S(2)}, u32[]{:S(2)}) %collective-permute-start.7) | collective-permute-done | bytes 524320 | tf_op jit(solution)/shard_map/ppermute | solution.py:141
  224.2 0.8 bitcast_dynamic-update-slice_fusion.22
  225.0 16.0 %collective-permute-done.8 = bf16[64,4096]{1,0:T(8,128)(2,1)S(1)} collective-permute-done((bf16[64,4096]{1,0:T(8,128)(2,1)S(1)}, bf16[64,4096]{1,0:T(8,128)(2,1)S(1)}, u32[]{:S(2)}, u32[]{:S(2)}) %collective-permute-start.8) | collective-permute-done | bytes 524320 | tf_op jit(solution)/shard_map/ppermute | solution.py:141
  241.1 3.9 %collective-permute-start.9 = (bf16[64,4096]{1,0:T(8,128)(2,1)S(1)}, bf16[64,4096]{1,0:T(8,128)(2,1)S(1)}, u32[]{:S(2)}, u32[]{:S(2)}) collective-permute-start(bf16[64,4096]{1,0:T(8,128)(2,1)S(1)} %get-tuple-element.21), channel_id=1, source_target_pairs={{0,10},{1,11},{2,12},{3,13},{4,14},{5,15},{6,0},{7,1},{8,2},{9,3},... | collective-permute-start | bytes 1572872 | tf_op jit(solution)/shard_map/ppermute | solution.py:141
  244.9 0.8 bitcast_dynamic-update-slice_fusion.20
  245.7 12.0 %collective-permute-done.9 = bf16[64,4096]{1,0:T(8,128)(2,1)S(1)} collective-permute-done((bf16[64,4096]{1,0:T(8,128)(2,1)S(1)}, bf16[64,4096]{1,0:T(8,128)(2,1)S(1)}, u32[]{:S(2)}, u32[]{:S(2)}) %collective-permute-start.9) | collective-permute-done | bytes 524320 | tf_op jit(solution)/shard_map/ppermute | solution.py:141
  257.7 0.8 bitcast_dynamic-update-slice_fusion.18
  258.6 10.6 %collective-permute-done.10 = bf16[64,4096]{1,0:T(8,128)(2,1)S(1)} collective-permute-done((bf16[64,4096]{1,0:T(8,128)(2,1)S(1)}, bf16[64,4096]{1,0:T(8,128)(2,1)S(1)}, u32[]{:S(2)}, u32[]{:S(2)}) %collective-permute-start.10) | collective-permute-done | bytes 524320 | tf_op jit(solution)/shard_map/ppermute | solution.py:141
  269.1 0.8 bitcast_dynamic-update-slice_fusion.16
  270.0 43.7 %collective-permute-done.11 = bf16[64,4096]{1,0:T(8,128)(2,1)S(1)} collective-permute-done((bf16[64,4096]{1,0:T(8,128)(2,1)S(1)}, bf16[64,4096]{1,0:T(8,128)(2,1)S(1)}, u32[]{:S(2)}, u32[]{:S(2)}) %collective-permute-start.11) | collective-permute-done | bytes 524320 | tf_op jit(solution)/shard_map/ppermute | solution.py:141
  313.7 0.8 bitcast_dynamic-update-slice_fusion.14
  314.5 0.8 bitcast_dynamic-update-slice_fusion.12
  315.3 0.8 bitcast_dynamic-update-slice_fusion.10
  316.2 0.8 bitcast_dynamic-update-slice_fusion.8
  317.0 0.8 bitcast_dynamic-update-slice_fusion.6
  317.9 19.5 %collective-permute-done.16 = bf16[64,4096]{1,0:T(8,128)(2,1)S(1)} collective-permute-done((bf16[64,4096]{1,0:T(8,128)(2,1)S(1)}, bf16[64,4096]{1,0:T(8,128)(2,1)S(1)}, u32[]{:S(2)}, u32[]{:S(2)}) %collective-permute-start.16) | collective-permute-done | bytes 524320 | tf_op jit(solution)/shard_map/ppermute | solution.py:141
  337.4 0.8 bitcast_dynamic-update-slice_fusion.4
  338.2 0.8 bitcast_dynamic-update-slice_fusion.2
  339.1 0.9 bitcast_dynamic-update-slice_fusion
  339.9 0.9 slice_dynamic-update-slice_fusion.1
  340.8 0.8 bitcast_dynamic-update-slice_fusion.29
  341.7 0.8 bitcast_dynamic-update-slice_fusion.27
  342.5 0.9 bitcast_dynamic-update-slice_fusion.25
  343.4 0.8 bitcast_dynamic-update-slice_fusion.23
  344.2 0.8 bitcast_dynamic-update-slice_fusion.21
  345.0 0.8 bitcast_dynamic-update-slice_fusion.19
  345.9 0.9 bitcast_dynamic-update-slice_fusion.17
  346.7 0.9 bitcast_dynamic-update-slice_fusion.15
  347.6 0.8 bitcast_dynamic-update-slice_fusion.13
  348.5 0.8 bitcast_dynamic-update-slice_fusion.11
  349.3 0.8 bitcast_dynamic-update-slice_fusion.9
  350.1 0.8 bitcast_dynamic-update-slice_fusion.7
  351.0 0.9 bitcast_dynamic-update-slice_fusion.5
  351.8 0.8 bitcast_dynamic-update-slice_fusion.3
  352.6 0.8 bitcast_dynamic-update-slice_fusion.1
  353.5 7.9 %dynamic-slice_bitcast_fusion = bf16[1,16,64,4096]{3,2,1,0:T(8,128)(2,1)} fusion(bf16[32,64,4096]{2,1,0:T(8,128)(2,1)} %bitcast_dynamic-update-slice_fusion.1, s32[]{:T(128)S(6)} %select_n.67), kind=kLoop, calls=%fused_computation.19 | loop fusion | bytes 16777220 | tf_op jit(solution)/shard_map/broadcast_in_dim | solution.py:145
  (61 shorter events, 8.4 us)
Async XLA Ops:
  0.0 14.0 %copy-start.2 = (s32[1,1,8,1]{2,3,1,0:T(1,128)S(1)}, s32[1,1,8,1]{2,3,1,0:T(1,128)}, u32[]{:S(2)}) copy-start(s32[1,1,8,1]{2,3,1,0:T(1,128)} %param.9) | copy-start | bytes 100
  2.0 25.2 %copy-start.1 = (f32[64]{0:T(128)S(1)}, f32[64]{0:T(128)}, u32[]{:S(2)}) copy-start(f32[64]{0:T(128)} %param.11) | copy-start | bytes 772
  8.3 5.8 %copy-start = (bf16[32,16,64,128]{3,2,1,0:T(8,128)(2,1)}, bf16[32,16,64,128]{3,2,1,0:T(8,128)(2,1)S(1)}, u32[]{:S(2)}) copy-start(bf16[32,16,64,128]{3,2,1,0:T(8,128)(2,1)S(1)} %broadcast_multiply_fusion) | copy-start | bytes 25165828
  8.4 9.9 %collective-permute-start = (bf16[1,16,64,128]{3,2,1,0:T(8,128)(2,1)S(1)}, bf16[1,16,64,128]{3,2,1,0:T(8,128)(2,1)S(1)}, u32[]{:S(2)}, u32[]{:S(2)}) collective-permute-start(bf16[1,16,64,128]{3,2,1,0:T(8,128)(2,1)S(1)} %get-tuple-element.9), channel_id=1, source_target_pairs={{0,16},{16,32},{32,48},{48,64},{64,80},{80,96},{96,112},{1,17},{17... | collective-permute-start | bytes 786440 | tf_op jit(solution)/shard_map/ppermute | solution.py:20
  10.3 8.0 %collective-permute-start.1 = (bf16[1,16,64,128]{3,2,1,0:T(8,128)(2,1)S(1)}, bf16[1,16,64,128]{3,2,1,0:T(8,128)(2,1)S(1)}, u32[]{:S(2)}, u32[]{:S(2)}) collective-permute-start(bf16[1,16,64,128]{3,2,1,0:T(8,128)(2,1)S(1)} %get-tuple-element.10), channel_id=1, source_target_pairs={{16,0},{32,16},{48,32},{64,48},{80,64},{96,80},{112,96},{17,1},{33... | collective-permute-start | bytes 786440 | tf_op jit(solution)/shard_map/ppermute | solution.py:22
  20.7 14.5 %collective-permute-start.2 = (bf16[34,1,64,128]{3,2,1,0:T(8,128)(2,1)}, bf16[34,1,64,128]{3,2,1,0:T(8,128)(2,1)S(1)}, u32[]{:S(2)}, u32[]{:S(2)}) collective-permute-start(bf16[34,1,64,128]{3,2,1,0:T(8,128)(2,1)} %get-tuple-element.7), channel_id=1, source_target_pairs={{0,1},{1,2},{2,3},{3,4},{4,5},{5,6},{6,7},{7,8},{8,9},{9,10},{10,1... | collective-permute-start | bytes 1671176 | tf_op jit(solution)/shard_map/ppermute | solution.py:20
  24.1 15.2 %collective-permute-start.3 = (bf16[34,1,64,128]{3,2,1,0:T(8,128)(2,1)}, bf16[34,1,64,128]{3,2,1,0:T(8,128)(2,1)}, u32[]{:S(2)}, u32[]{:S(2)}) collective-permute-start(bf16[34,1,64,128]{3,2,1,0:T(8,128)(2,1)} %get-tuple-element.8), channel_id=1, source_target_pairs={{1,0},{2,1},{3,2},{4,3},{5,4},{6,5},{7,6},{8,7},{9,8},{10,9},{11,1... | collective-permute-start | bytes 1671176 | tf_op jit(solution)/shard_map/ppermute | solution.py:22
  128.4 188.7 %collective-permute-start.15 = (bf16[64,4096]{1,0:T(8,128)(2,1)S(1)}, bf16[64,4096]{1,0:T(8,128)(2,1)S(1)}, u32[]{:S(2)}, u32[]{:S(2)}) collective-permute-start(bf16[64,4096]{1,0:T(8,128)(2,1)S(1)} %get-tuple-element.15), channel_id=1, source_target_pairs={{0,4},{1,5},{2,6},{3,7},{4,8},{5,9},{6,10},{7,11},{8,12},{9,13},{1... | collective-permute-start | bytes 1572872 | tf_op jit(solution)/shard_map/ppermute | solution.py:141
  128.4 187.7 %collective-permute-start.14 = (bf16[64,4096]{1,0:T(8,128)(2,1)S(1)}, bf16[64,4096]{1,0:T(8,128)(2,1)S(1)}, u32[]{:S(2)}, u32[]{:S(2)}) collective-permute-start(bf16[64,4096]{1,0:T(8,128)(2,1)S(1)} %get-tuple-element.16), channel_id=1, source_target_pairs={{0,5},{1,6},{2,7},{3,8},{4,9},{5,10},{6,11},{7,12},{8,13},{9,14},{... | collective-permute-start | bytes 1572872 | tf_op jit(solution)/shard_map/ppermute | solution.py:141
  133.0 182.3 %collective-permute-start.13 = (bf16[64,4096]{1,0:T(8,128)(2,1)S(1)}, bf16[64,4096]{1,0:T(8,128)(2,1)S(1)}, u32[]{:S(2)}, u32[]{:S(2)}) collective-permute-start(bf16[64,4096]{1,0:T(8,128)(2,1)S(1)} %get-tuple-element.17), channel_id=1, source_target_pairs={{0,6},{1,7},{2,8},{3,9},{4,10},{5,11},{6,12},{7,13},{8,14},{9,15},... | collective-permute-start | bytes 1572872 | tf_op jit(solution)/shard_map/ppermute | solution.py:141
  133.0 181.5 %collective-permute-start.12 = (bf16[64,4096]{1,0:T(8,128)(2,1)S(1)}, bf16[64,4096]{1,0:T(8,128)(2,1)S(1)}, u32[]{:S(2)}, u32[]{:S(2)}) collective-permute-start(bf16[64,4096]{1,0:T(8,128)(2,1)S(1)} %get-tuple-element.18), channel_id=1, source_target_pairs={{0,7},{1,8},{2,9},{3,10},{4,11},{5,12},{6,13},{7,14},{8,15},{9,0},... | collective-permute-start | bytes 1572872 | tf_op jit(solution)/shard_map/ppermute | solution.py:141
  141.1 43.6 %collective-permute-start.4 = (bf16[64,4096]{1,0:T(8,128)(2,1)S(1)}, bf16[64,4096]{1,0:T(8,128)(2,1)S(1)}, u32[]{:S(2)}, u32[]{:S(2)}) collective-permute-start(bf16[64,4096]{1,0:T(8,128)(2,1)S(1)} %get-tuple-element.26), channel_id=1, source_target_pairs={{0,15},{1,0},{2,1},{3,2},{4,3},{5,4},{6,5},{7,6},{8,7},{9,8},{10,9... | collective-permute-start | bytes 1572872 | tf_op jit(solution)/shard_map/ppermute | solution.py:141
  184.7 14.3 %collective-permute-start.5 = (bf16[64,4096]{1,0:T(8,128)(2,1)S(1)}, bf16[64,4096]{1,0:T(8,128)(2,1)S(1)}, u32[]{:S(2)}, u32[]{:S(2)}) collective-permute-start(bf16[64,4096]{1,0:T(8,128)(2,1)S(1)} %get-tuple-element.25), channel_id=1, source_target_pairs={{0,14},{1,15},{2,0},{3,1},{4,2},{5,3},{6,4},{7,5},{8,6},{9,7},{10,... | collective-permute-start | bytes 1572872 | tf_op jit(solution)/shard_map/ppermute | solution.py:141
  199.0 10.4 %collective-permute-start.6 = (bf16[64,4096]{1,0:T(8,128)(2,1)S(1)}, bf16[64,4096]{1,0:T(8,128)(2,1)S(1)}, u32[]{:S(2)}, u32[]{:S(2)}) collective-permute-start(bf16[64,4096]{1,0:T(8,128)(2,1)S(1)} %get-tuple-element.24), channel_id=1, source_target_pairs={{0,13},{1,14},{2,15},{3,0},{4,1},{5,2},{6,3},{7,4},{8,5},{9,6},{10... | collective-permute-start | bytes 1572872 | tf_op jit(solution)/shard_map/ppermute | solution.py:141
  209.4 14.8 %collective-permute-start.7 = (bf16[64,4096]{1,0:T(8,128)(2,1)S(1)}, bf16[64,4096]{1,0:T(8,128)(2,1)S(1)}, u32[]{:S(2)}, u32[]{:S(2)}) collective-permute-start(bf16[64,4096]{1,0:T(8,128)(2,1)S(1)} %get-tuple-element.23), channel_id=1, source_target_pairs={{0,12},{1,13},{2,14},{3,15},{4,0},{5,1},{6,2},{7,3},{8,4},{9,5},{1... | collective-permute-start | bytes 1572872 | tf_op jit(solution)/shard_map/ppermute | solution.py:141
  224.2 16.9 %collective-permute-start.8 = (bf16[64,4096]{1,0:T(8,128)(2,1)S(1)}, bf16[64,4096]{1,0:T(8,128)(2,1)S(1)}, u32[]{:S(2)}, u32[]{:S(2)}) collective-permute-start(bf16[64,4096]{1,0:T(8,128)(2,1)S(1)} %get-tuple-element.22), channel_id=1, source_target_pairs={{0,11},{1,12},{2,13},{3,14},{4,15},{5,0},{6,1},{7,2},{8,3},{9,4},{... | collective-permute-start | bytes 1572872 | tf_op jit(solution)/shard_map/ppermute | solution.py:141
  241.1 16.7 %collective-permute-start.9 = (bf16[64,4096]{1,0:T(8,128)(2,1)S(1)}, bf16[64,4096]{1,0:T(8,128)(2,1)S(1)}, u32[]{:S(2)}, u32[]{:S(2)}) collective-permute-start(bf16[64,4096]{1,0:T(8,128)(2,1)S(1)} %get-tuple-element.21), channel_id=1, source_target_pairs={{0,10},{1,11},{2,12},{3,13},{4,14},{5,15},{6,0},{7,1},{8,2},{9,3},... | collective-permute-start | bytes 1572872 | tf_op jit(solution)/shard_map/ppermute | solution.py:141
  257.7 11.4 %collective-permute-start.10 = (bf16[64,4096]{1,0:T(8,128)(2,1)S(1)}, bf16[64,4096]{1,0:T(8,128)(2,1)S(1)}, u32[]{:S(2)}, u32[]{:S(2)}) collective-permute-start(bf16[64,4096]{1,0:T(8,128)(2,1)S(1)} %get-tuple-element.20), channel_id=1, source_target_pairs={{0,9},{1,10},{2,11},{3,12},{4,13},{5,14},{6,15},{7,0},{8,1},{9,2},... | collective-permute-start | bytes 1572872 | tf_op jit(solution)/shard_map/ppermute | solution.py:141
  269.1 44.5 %collective-permute-start.11 = (bf16[64,4096]{1,0:T(8,128)(2,1)S(1)}, bf16[64,4096]{1,0:T(8,128)(2,1)S(1)}, u32[]{:S(2)}, u32[]{:S(2)}) collective-permute-start(bf16[64,4096]{1,0:T(8,128)(2,1)S(1)} %get-tuple-element.19), channel_id=1, source_target_pairs={{0,8},{1,9},{2,10},{3,11},{4,12},{5,13},{6,14},{7,15},{8,0},{9,1},... | collective-permute-start | bytes 1572872 | tf_op jit(solution)/shard_map/ppermute | solution.py:141
  313.7 25.4 %collective-permute-start.18 = (bf16[64,4096]{1,0:T(8,128)(2,1)S(1)}, bf16[64,4096]{1,0:T(8,128)(2,1)S(1)}, u32[]{:S(2)}, u32[]{:S(2)}) collective-permute-start(bf16[64,4096]{1,0:T(8,128)(2,1)S(1)} %get-tuple-element.11), channel_id=1, source_target_pairs={{0,1},{1,2},{2,3},{3,4},{4,5},{5,6},{6,7},{7,8},{8,9},{9,10},{10,1... | collective-permute-start | bytes 1572872 | tf_op jit(solution)/shard_map/ppermute | solution.py:141
  314.5 23.7 %collective-permute-start.17 = (bf16[64,4096]{1,0:T(8,128)(2,1)S(1)}, bf16[64,4096]{1,0:T(8,128)(2,1)S(1)}, u32[]{:S(2)}, u32[]{:S(2)}) collective-permute-start(bf16[64,4096]{1,0:T(8,128)(2,1)S(1)} %get-tuple-element.13), channel_id=1, source_target_pairs={{0,2},{1,3},{2,4},{3,5},{4,6},{5,7},{6,8},{7,9},{8,10},{9,11},{10,... | collective-permute-start | bytes 1572872 | tf_op jit(solution)/shard_map/ppermute | solution.py:141
  315.3 22.1 %collective-permute-start.16 = (bf16[64,4096]{1,0:T(8,128)(2,1)S(1)}, bf16[64,4096]{1,0:T(8,128)(2,1)S(1)}, u32[]{:S(2)}, u32[]{:S(2)}) collective-permute-start(bf16[64,4096]{1,0:T(8,128)(2,1)S(1)} %get-tuple-element.14), channel_id=1, source_target_pairs={{0,3},{1,4},{2,5},{3,6},{4,7},{5,8},{6,9},{7,10},{8,11},{9,12},{10... | collective-permute-start | bytes 1572872 | tf_op jit(solution)/shard_map/ppermute | solution.py:141

commit v5 on v3

--- a/solution.py
+++ b/solution.py
@@ -39,7 +39,9 @@
         for first in range(0, EDGE + 2, group):
             part = jnp.zeros((group * rows, 3 * C), jnp.float32)
             for b in range(3):
-                lhs = x_ref[first:first + group, b:b + EDGE, :, :]
+                lhs = jnp.concatenate(
+                    [x_ref[first:first + group, b:b + EDGE, c:c + EDGE, :] for c in range(3)], axis=-1
+                )
                 lhs = lhs.reshape(group * rows, lhs.shape[-1])
                 part = part + jnp.dot(lhs, w_ref[b], preferred_element_type=jnp.float32)
             part_ref[:, first * rows:(first + group) * rows] = part.T
@@ -63,6 +65,7 @@
 
 def conv_slots(table, shifted, w9, bias_col, masks, total, bricks_z):
     depth = shifted.shape[-1]
+    window = 2 * EDGE
     span = shifted.shape[1]
 
     def brick_of(j, table_ref):
@@ -79,7 +82,7 @@
             num_scalar_prefetch=1,
             grid=(total,),
             in_specs=[
-                pl.BlockSpec((pl.Element(EDGE + 2), pl.Element(span), pl.Element(EDGE), pl.Element(depth)), x_map),
+                pl.BlockSpec((pl.Element(EDGE + 2), pl.Element(span), pl.Element(window), pl.Element(depth)), x_map),
                 pl.BlockSpec(w9.shape, lambda j, t: (0, 0, 0)),
                 pl.BlockSpec(bias_col.shape, lambda j, t: (0, 0)),
                 pl.BlockSpec((1, 1, EDGE**3), lambda j, t: (brick_of(j, t), 0, 0)),
@@ -105,8 +108,7 @@
     live = (voxel_mask * grown).astype(jnp.bfloat16)
     inputs = features * live[..., None]
     padded = padded_2(inputs, (("gx", 0), ("gy", 1)), 1)
-    padded = jnp.pad(padded, ((0, 0), (0, 0), (1, 1), (0, 0)))
-    shifted = jnp.concatenate([padded[:, :, c:c + extent_z, :] for c in range(3)], axis=-1)
+    shifted = jnp.pad(padded, ((0, 0), (0, 0), (1, EDGE - 1), (0, 0)))
     brick_masks = live.astype(jnp.float32).reshape(bricks_x, EDGE, bricks_y, EDGE, bricks_z, EDGE)
     brick_masks = brick_masks.transpose(0, 2, 4, 1, 3, 5).reshape(count, 1, EDGE**3)
     ids = owner.reshape(count)

time: 251 us -> 223 us (0.89)
  other arithmetic: 48.7 us -> 29.3 us
  local copies, waits for them, and re-layouts: 25.5 us -> 16.4 us
    concatenate x1 -> x0, other arithmetic: 21.2 us -> none  [per_device(): jnp.concatenate([padded[:, :, c:c + extent_z, :] for c in range(3)], axis...]
    slice x1 -> x0, local copies, waits for them, and re-layouts: 9.07 us -> none  [per_device(): padded[:, :, c:c + extent_z, :]]
where the time goes in v5:
time: 223 us; the launch traced here: 221 us
  blocking collectives  108 us (48%)
  Pallas kernels  41.9 us (19%)
  other arithmetic  29.3 us (13%)
  local copies, waits for them, and re-layouts  16.4 us (7%)
  waiting for transfers between devices  15.1 us (7%)
  starting transfers between devices  10.3 us (5%)
    all_to_all x1, blocking collectives, per_device(): lax.all_to_all(sending, 'gy', split_axis=0, concat_axis=0, tiled=True)  108 us
    pallas_call x1, Pallas kernels, conv_slots(): pl.pallas_call(conv_kernel, out_shape=jax.ShapeDtypeStruct((total, C, EDG...  41.9 us
    concatenate x1, other arithmetic, padded_2(): jnp.concatenate([lax.ppermute(tail, axis, [(i, (i + 1) % count) for i in...  19.2 us
    unnamed x7, local copies, waits for them, and re-layouts  11.3 us
    ppermute x2, waiting for transfers between devices, padded_2(): lax.ppermute(tail, axis, [(i, (i + 1) % count) for i in range(ends)])  8.6 us
    ppermute x2, waiting for transfers between devices, padded_2(): lax.ppermute(head, axis, [((i + 1) % count, i) for i in range(ends)])  6.51 us
    mul x1, other arithmetic, per_device(): inputs = features * live[..., None]  6.32 us
    ppermute x2, starting transfers between devices, padded_2(): lax.ppermute(tail, axis, [(i, (i + 1) % count) for i in range(ends)])  5.34 us
  transfers between devices with their start and end apart: 4, of which 4 were waited for; matrix products, arithmetic and copies ran while one was open for 2% of the time, Pallas kernels for 0%

profile of v5, /device:TPU:8, one launch (start us, length us, event | category | flops | bytes accessed | tf_op | source)
XLA Modules:
  0.0 220.9 jit_solution(982685857281827604)
XLA Ops:
  0.0 0.0 copy-start.2
  0.0 0.8 copy.18
  0.8 0.1 broadcast_in_dim.36
  0.9 0.1 broadcast_in_dim.37
  0.9 0.1 copy.19
  1.0 1.0 multiply_convert_fusion
  2.0 6.3 %broadcast_multiply_fusion = bf16[32,16,64,128]{3,2,1,0:T(8,128)(2,1)S(1)} fusion(bf16[32,16,64,128]{3,2,1,0:T(8,128)(2,1)} %param.6, bf16[32,16,64]{2,1,0:T(8,128)(2,1)S(1)} %multiply_convert_fusion), kind=kLoop, calls=%fused_computation.10 | loop fusion | flops 4194304 | bytes 16842752 | tf_op jit(solution)/shard_map/mul | solution.py:109
  8.3 0.0 copy-start
  8.3 3.4 %copy-done = bf16[32,16,64,128]{3,2,1,0:T(8,128)(2,1)} copy-done((bf16[32,16,64,128]{3,2,1,0:T(8,128)(2,1)}, bf16[32,16,64,128]{3,2,1,0:T(8,128)(2,1)S(1)}, u32[]{:S(2)}) %copy-start) | copy-done | bytes 8388632
  11.7 0.0 copy-start.1
  11.8 1.9 collective-permute-start
  13.7 3.6 %collective-permute-start.1 = (bf16[1,16,64,128]{3,2,1,0:T(8,128)(2,1)S(1)}, bf16[1,16,64,128]{3,2,1,0:T(8,128)(2,1)S(1)}, u32[]{:S(2)}, u32[]{:S(2)}) collective-permute-start(bf16[1,16,64,128]{3,2,1,0:T(8,128)(2,1)S(1)} %get-tuple-element.8), channel_id=1, source_target_pairs={{16,0},{32,16},{48,32},{64,48},{80,64},{96,80},{112,96},{17,1},{33... | collective-permute-start | bytes 786440 | tf_op jit(solution)/shard_map/ppermute | solution.py:22
  17.4 0.5 reshape.46
  17.8 0.0 copy-done.2
  17.8 0.2 convert_reduce_fusion
  18.0 1.4 collective-permute-done
  19.5 1.8 collective-permute-done.1
  21.2 2.3 %pad_maximum_fusion.2 = (bf16[34,1,64,128]{3,2,1,0:T(8,128)(2,1)}, bf16[34,1,64,128]{3,2,1,0:T(8,128)(2,1)}) fusion(bf16[1,16,64,128]{3,2,1,0:T(8,128)(2,1)S(1)} %collective-permute-done.1, bf16[32,16,64,128]{3,2,1,0:T(8,128)(2,1)} %copy-done, bf16[1,16,64,128]{3,2,1,0:T(8,128)(2,1)S(1)} %collective-permute-done), kind=kLoop, calls=%fused_computation.14 | loop fusion | flops 1114112 | bytes 10027008 | tf_op jit(solution)/shard_map/slice | solution.py:17
  23.6 3.4 %collective-permute-start.2 = (bf16[34,1,64,128]{3,2,1,0:T(8,128)(2,1)}, bf16[34,1,64,128]{3,2,1,0:T(8,128)(2,1)S(1)}, u32[]{:S(2)}, u32[]{:S(2)}) collective-permute-start(bf16[34,1,64,128]{3,2,1,0:T(8,128)(2,1)} %get-tuple-element.5), channel_id=1, source_target_pairs={{0,1},{1,2},{2,3},{3,4},{4,5},{5,6},{6,7},{7,8},{8,9},{9,10},{10,1... | collective-permute-start | bytes 1671176 | tf_op jit(solution)/shard_map/ppermute | solution.py:20
  27.0 1.3 collective-permute-start.3
  28.3 0.1 fusion.6
  28.4 0.1 copy.27
  28.5 0.4 reshape.43.m_ref
  28.9 2.4 %copy.24 = bf16[3,3,128,3,64]{4,3,2,1,0:T(4,128)(2,1)S(1)} copy(bf16[3,3,128,3,64]{2,4,1,0,3:T(8,128)(2,1)} %bitcast.18) | data formatting | bytes 884736 | tf_op jit(solution)/shard_map/reshape | solution.py:124
  31.2 0.7 reshape.47.w_ref
  32.0 0.0 copy-done.1
  32.0 0.1 copy.23.b_ref
  32.1 0.1 select_reduce_fusion
  32.2 0.1 pad_add_fusion.table_ref
  32.3 7.1 %collective-permute-done.2 = bf16[34,1,64,128]{3,2,1,0:T(8,128)(2,1)S(1)} collective-permute-done((bf16[34,1,64,128]{3,2,1,0:T(8,128)(2,1)}, bf16[34,1,64,128]{3,2,1,0:T(8,128)(2,1)S(1)}, u32[]{:S(2)}, u32[]{:S(2)}) %collective-permute-start.2) | collective-permute-done | bytes 557088 | tf_op jit(solution)/shard_map/ppermute | solution.py:20
  39.4 4.8 %collective-permute-done.3 = bf16[34,1,64,128]{3,2,1,0:T(8,128)(2,1)} collective-permute-done((bf16[34,1,64,128]{3,2,1,0:T(8,128)(2,1)}, bf16[34,1,64,128]{3,2,1,0:T(8,128)(2,1)}, u32[]{:S(2)}, u32[]{:S(2)}) %collective-permute-start.3) | collective-permute-done | bytes 557088 | tf_op jit(solution)/shard_map/ppermute | solution.py:22
  44.2 19.2 %select_maximum_fusion.x_ref = bf16[34,18,80,128]{3,2,1,0:T(8,128)(2,1)} fusion(bf16[34,1,64,128]{3,2,1,0:T(8,128)(2,1)} %collective-permute-done.3, bf16[34,1,64,128]{3,2,1,0:T(8,128)(2,1)S(1)} %collective-permute-done.2, bf16[1,16,64,128]{3,2,1,0:T(8,128)(2,1)S(1)} %collective-permute-done.1, bf16[32,16,64,128]{3,2,1,0:T(8,128)(2,1)} %copy-done, ...), kind=kLoop, calls=%fused_computation.3 | loop fusion | flops 112803840 | bytes 22560768 | tf_op jit(solution)/shard_map/concatenate | solution.py:18
  63.4 41.9 %shard_map.67 = bf16[16,64,4096]{2,1,0:T(8,128)(2,1)} custom-call(s32[32]{0:T(128)S(1)} %pad_add_fusion.table_ref, bf16[34,18,80,128]{3,2,1,0:T(8,128)(2,1)} %select_maximum_fusion.x_ref, bf16[3,384,192]{2,1,0:T(8,128)(2,1)S(1)} %reshape.47.w_ref, f32[64,1]{1,0:T(8,128)S(1)} %copy.23.b_ref, f32[8,1,4096]{2,1,0:T(1,128)S(1)} %reshape.43.m_ref), custom_call_target="tpu_custom_call" | custom-call | tf_op jit(solution)/shard_map/pallas_call | solution.py:78
  105.3 107.7 %all_to_all.5 = bf16[16,64,4096]{2,1,0:T(8,128)(2,1)} all-to-all(bf16[16,64,4096]{2,1,0:T(8,128)(2,1)} %shard_map.67), channel_id=1, replica_groups=mesh['gx'=8,'gy'=16] {'gy'}, dimensions={0} | all-to-all | bytes 16777216 | tf_op jit(solution)/shard_map/all_to_all | solution.py:127
  213.0 7.9 %copy.29 = bf16[1,16,64,4096]{3,2,1,0:T(8,128)(2,1)} copy(bf16[1,16,64,4096]{3,2,1,0:T(8,128)(2,1)} %bitcast.16) | data formatting | bytes 16777216
  (4 shorter events, 0.1 us)
Async XLA Ops:
  0.0 17.8 %copy-start.2 = (s32[1,1,8,1]{2,3,1,0:T(1,128)S(1)}, s32[1,1,8,1]{2,3,1,0:T(1,128)}, u32[]{:S(2)}) copy-start(s32[1,1,8,1]{2,3,1,0:T(1,128)} %param.9) | copy-start | bytes 100
  8.3 3.4 %copy-start = (bf16[32,16,64,128]{3,2,1,0:T(8,128)(2,1)}, bf16[32,16,64,128]{3,2,1,0:T(8,128)(2,1)S(1)}, u32[]{:S(2)}) copy-start(bf16[32,16,64,128]{3,2,1,0:T(8,128)(2,1)S(1)} %broadcast_multiply_fusion) | copy-start | bytes 25165828
  11.7 20.2 %copy-start.1 = (f32[64]{0:T(128)S(1)}, f32[64]{0:T(128)}, u32[]{:S(2)}) copy-start(f32[64]{0:T(128)} %param.11) | copy-start | bytes 772
  11.8 7.7 %collective-permute-start = (bf16[1,16,64,128]{3,2,1,0:T(8,128)(2,1)S(1)}, bf16[1,16,64,128]{3,2,1,0:T(8,128)(2,1)S(1)}, u32[]{:S(2)}, u32[]{:S(2)}) collective-permute-start(bf16[1,16,64,128]{3,2,1,0:T(8,128)(2,1)S(1)} %get-tuple-element.7), channel_id=1, source_target_pairs={{0,16},{16,32},{32,48},{48,64},{64,80},{80,96},{96,112},{1,17},{17... | collective-permute-start | bytes 786440 | tf_op jit(solution)/shard_map/ppermute | solution.py:20
  13.7 7.5 %collective-permute-start.1 = (bf16[1,16,64,128]{3,2,1,0:T(8,128)(2,1)S(1)}, bf16[1,16,64,128]{3,2,1,0:T(8,128)(2,1)S(1)}, u32[]{:S(2)}, u32[]{:S(2)}) collective-permute-start(bf16[1,16,64,128]{3,2,1,0:T(8,128)(2,1)S(1)} %get-tuple-element.8), channel_id=1, source_target_pairs={{16,0},{32,16},{48,32},{64,48},{80,64},{96,80},{112,96},{17,1},{33... | collective-permute-start | bytes 786440 | tf_op jit(solution)/shard_map/ppermute | solution.py:22
  23.6 15.8 %collective-permute-start.2 = (bf16[34,1,64,128]{3,2,1,0:T(8,128)(2,1)}, bf16[34,1,64,128]{3,2,1,0:T(8,128)(2,1)S(1)}, u32[]{:S(2)}, u32[]{:S(2)}) collective-permute-start(bf16[34,1,64,128]{3,2,1,0:T(8,128)(2,1)} %get-tuple-element.5), channel_id=1, source_target_pairs={{0,1},{1,2},{2,3},{3,4},{4,5},{5,6},{6,7},{7,8},{8,9},{9,10},{10,1... | collective-permute-start | bytes 1671176 | tf_op jit(solution)/shard_map/ppermute | solution.py:20
  27.0 17.2 %collective-permute-start.3 = (bf16[34,1,64,128]{3,2,1,0:T(8,128)(2,1)}, bf16[34,1,64,128]{3,2,1,0:T(8,128)(2,1)}, u32[]{:S(2)}, u32[]{:S(2)}) collective-permute-start(bf16[34,1,64,128]{3,2,1,0:T(8,128)(2,1)} %get-tuple-element.6), channel_id=1, source_target_pairs={{1,0},{2,1},{3,2},{4,3},{5,4},{6,5},{7,6},{8,7},{9,8},{10,9},{11,1... | collective-permute-start | bytes 1671176 | tf_op jit(solution)/shard_map/ppermute | solution.py:22

commit v6 on v5

--- a/solution.py
+++ b/solution.py
@@ -9,21 +9,42 @@
 EDGE = 16
 
 
-def padded_2(cells, sides, width):
-    for axis, dim in sides:
-        count = lax.axis_size(axis)
-        ends = count - 1
-        head = lax.slice_in_dim(cells, 0, width, axis=dim)
-        tail = lax.slice_in_dim(cells, cells.shape[dim] - width, cells.shape[dim], axis=dim)
-        cells = jnp.concatenate(
-            [
-                lax.ppermute(tail, axis, [(i, (i + 1) % count) for i in range(ends)]),
-                cells,
-                lax.ppermute(head, axis, [((i + 1) % count, i) for i in range(ends)]),
-            ],
-            axis=dim,
-        )
-    return cells
+def shift(piece, axes, steps):
+    sizes = [lax.axis_size(axis) for axis in axes]
+    total = 1
+    for size in sizes:
+        total *= size
+    pairs = []
+    for source in range(total):
+        place = []
+        rest = source
+        for size in reversed(sizes):
+            place.append(rest % size)
+            rest //= size
+        place = place[::-1]
+        moved = [p + d for p, d in zip(place, steps)]
+        if all(0 <= m < size for m, size in zip(moved, sizes)):
+            target = 0
+            for m, size in zip(moved, sizes):
+                target = target * size + m
+            pairs.append((source, target))
+    return lax.ppermute(piece, axes if len(axes) > 1 else axes[0], pairs)
+
+
+def padded_2(cells):
+    both = ("gx", "gy")
+    up = shift(cells[-1:], ("gx",), (1,))
+    down = shift(cells[:1], ("gx",), (-1,))
+    left = shift(cells[:, -1:], ("gy",), (1,))
+    right = shift(cells[:, :1], ("gy",), (-1,))
+    up_left = shift(cells[-1:, -1:], both, (1, 1))
+    up_right = shift(cells[-1:, :1], both, (1, -1))
+    down_left = shift(cells[:1, -1:], both, (-1, 1))
+    down_right = shift(cells[:1, :1], both, (-1, -1))
+    top = jnp.concatenate([up_left, up, up_right], axis=1)
+    middle = jnp.concatenate([left, cells, right], axis=1)
+    bottom = jnp.concatenate([down_left, down, down_right], axis=1)
+    return jnp.concatenate([top, middle, bottom], axis=0)
 
 
 def conv_kernel(table_ref, x_ref, w_ref, b_ref, m_ref, o_ref, part_ref):
@@ -107,7 +128,7 @@
     grown = jnp.repeat(grown, EDGE, axis=2)
     live = (voxel_mask * grown).astype(jnp.bfloat16)
     inputs = features * live[..., None]
-    padded = padded_2(inputs, (("gx", 0), ("gy", 1)), 1)
+    padded = padded_2(inputs)
     shifted = jnp.pad(padded, ((0, 0), (0, 0), (1, EDGE - 1), (0, 0)))
     brick_masks = live.astype(jnp.float32).reshape(bricks_x, EDGE, bricks_y, EDGE, bricks_z, EDGE)
     brick_masks = brick_masks.transpose(0, 2, 4, 1, 3, 5).reshape(count, 1, EDGE**3)

time: 223 us -> 233 us (1.045)
  waiting for transfers between devices: 15.1 us -> 1.79 us
  starting transfers between devices: 10.3 us -> 22.1 us
  other arithmetic: 29.3 us -> 37 us
  blocking collectives: 108 us -> 111 us
    ppermute x4 -> x8, waiting for transfers between devices: 15.1 us -> 1.79 us  [shift(): return lax.ppermute(piece, axes if len(axes) > 1 else axes[0], pairs)]
    ppermute x4 -> x8, starting transfers between devices: 10.3 us -> 22.1 us  [shift(): return lax.ppermute(piece, axes if len(axes) > 1 else axes[0], pairs)]
    concatenate x1, other arithmetic: 19.2 us -> 29.2 us  [padded_2(): return jnp.concatenate([top, middle, bottom], axis=0)]
    unnamed x7, local copies, waits for them, and re-layouts: 11.3 us -> 7.9 us
    all_to_all x1, blocking collectives: 108 us -> 111 us  [per_device(): lax.all_to_all(sending, 'gy', split_axis=0, concat_axis=0, tiled=True)]
    slice x1 -> x0, other arithmetic: 2.34 us -> none  [padded_2(): lax.slice_in_dim(cells, cells.shape[dim] - width, cells.shape[dim], axis=...]
  transfers between devices with their start and end apart: 4 -> 8, of which waited for: 4 -> 2; matrix products, arithmetic and copies ran while one was open for 2% -> 3% of each run, Pallas kernels for 0% -> 0%
where the time goes in v6:
time: 233 us; the launch traced here: 229 us
  blocking collectives  111 us (48%)
  Pallas kernels  42.1 us (18%)
  other arithmetic  37 us (16%)
  starting transfers between devices  22.1 us (9%)
  local copies, waits for them, and re-layouts  14.9 us (6%)
    all_to_all x1, blocking collectives, per_device(): lax.all_to_all(sending, 'gy', split_axis=0, concat_axis=0, tiled=True)  111 us
    pallas_call x1, Pallas kernels, conv_slots(): pl.pallas_call(conv_kernel, out_shape=jax.ShapeDtypeStruct((total, C, EDG...  42.1 us
    concatenate x1, other arithmetic, padded_2(): return jnp.concatenate([top, middle, bottom], axis=0)  29.2 us
    ppermute x8, starting transfers between devices, shift(): return lax.ppermute(piece, axes if len(axes) > 1 else axes[0], pairs)  22.1 us
    unnamed x7, local copies, waits for them, and re-layouts  7.9 us
    mul x1, other arithmetic, per_device(): inputs = features * live[..., None]  6.32 us
  transfers between devices with their start and end apart: 8, of which 2 were waited for; matrix products, arithmetic and copies ran while one was open for 3% of the time, Pallas kernels for 0%

profile of v6, /device:TPU:8, one launch (start us, length us, event | category | flops | bytes accessed | tf_op | source)
XLA Modules:
  0.0 228.7 jit_solution(2763734752116952490)
XLA Ops:
  0.0 0.0 copy-start.2
  0.0 0.8 copy.18
  0.8 0.1 broadcast_in_dim.36
  0.9 0.1 broadcast_in_dim.37
  0.9 0.1 copy.19
  1.0 1.0 multiply_convert_fusion
  2.0 0.0 copy-start.1
  2.0 6.3 %broadcast_multiply_fusion = bf16[32,16,64,128]{3,2,1,0:T(8,128)(2,1)S(1)} fusion(bf16[32,16,64,128]{3,2,1,0:T(8,128)(2,1)} %param.6, bf16[32,16,64]{2,1,0:T(8,128)(2,1)S(1)} %multiply_convert_fusion), kind=kLoop, calls=%fused_computation.13 | loop fusion | flops 4194304 | bytes 16842752 | tf_op jit(solution)/shard_map/mul | solution.py:130
  8.4 0.0 copy-start
  8.4 2.8 %collective-permute-start = (bf16[1,1,64,128]{3,2,1,0:T(8,128)(2,1)S(1)}, bf16[1,1,64,128]{3,2,1,0:T(8,128)(2,1)S(1)}, u32[]{:S(2)}, u32[]{:S(2)}) collective-permute-start(bf16[1,1,64,128]{3,2,1,0:T(8,128)(2,1)S(1)} %get-tuple-element.5), channel_id=1, source_target_pairs={{0,17},{1,18},{2,19},{3,20},{4,21},{5,22},{6,23},{7,24},{8,25},{9,... | collective-permute-start | bytes 49160 | tf_op jit(solution)/shard_map/ppermute | solution.py:31
  11.2 1.3 collective-permute-start.2
  12.5 1.1 fusion.10
  13.6 5.9 %collective-permute-start.3 = (bf16[32,1,64,128]{3,2,1,0:T(8,128)(2,1)}, bf16[32,1,64,128]{3,2,1,0:T(8,128)(2,1)S(1)}, u32[]{:S(2)}, u32[]{:S(2)}) collective-permute-start(bf16[32,1,64,128]{3,2,1,0:T(8,128)(2,1)} %get-tuple-element.11), channel_id=1, source_target_pairs={{0,1},{1,2},{2,3},{3,4},{4,5},{5,6},{6,7},{7,8},{8,9},{9,10},{10,1... | collective-permute-start | bytes 1572872 | tf_op jit(solution)/shard_map/ppermute | solution.py:31
  19.4 1.3 collective-permute-start.4
  20.7 0.8 fusion.9
  21.6 1.9 collective-permute-start.1
  23.5 0.0 copy-done.2
  23.5 0.2 convert_reduce_fusion
  23.7 0.0 collective-permute-done
  23.7 3.6 %collective-permute-start.6 = (bf16[1,16,64,128]{3,2,1,0:T(8,128)(2,1)}, bf16[1,16,64,128]{3,2,1,0:T(8,128)(2,1)}, u32[]{:S(2)}, u32[]{:S(2)}) collective-permute-start(bf16[1,16,64,128]{3,2,1,0:T(8,128)(2,1)} %get-tuple-element.10), channel_id=1, source_target_pairs={{16,0},{32,16},{48,32},{64,48},{80,64},{96,80},{112,96},{17,1},{33... | collective-permute-start | bytes 786440 | tf_op jit(solution)/shard_map/ppermute | solution.py:31
  27.4 0.1 fusion.6
  27.4 0.0 collective-permute-done.2
  27.5 4.0 %collective-permute-start.5 = (bf16[1,1,64,128]{3,2,1,0:T(8,128)(2,1)S(1)}, bf16[1,1,64,128]{3,2,1,0:T(8,128)(2,1)S(1)}, u32[]{:S(2)}, u32[]{:S(2)}) collective-permute-start(bf16[1,1,64,128]{3,2,1,0:T(8,128)(2,1)S(1)} %get-tuple-element.7), channel_id=1, source_target_pairs={{16,1},{17,2},{18,3},{19,4},{20,5},{21,6},{22,7},{23,8},{24,9},{25... | collective-permute-start | bytes 49160 | tf_op jit(solution)/shard_map/ppermute | solution.py:31
  31.4 0.1 select_reduce_fusion
  31.5 1.3 collective-permute-done.5
  32.9 0.0 copy-done
  32.9 1.3 collective-permute-start.7
  34.2 0.1 pad_add_fusion.table_ref
  34.2 0.5 reshape.46
  34.7 0.1 copy.27
  34.8 0.4 reshape.43.m_ref
  35.2 2.3 %copy.24 = bf16[3,3,128,3,64]{4,3,2,1,0:T(4,128)(2,1)S(1)} copy(bf16[3,3,128,3,64]{2,4,1,0,3:T(8,128)(2,1)} %bitcast.18) | data formatting | bytes 884736 | tf_op jit(solution)/shard_map/reshape | solution.py:145
  37.6 0.7 reshape.47.w_ref
  38.3 0.0 copy-done.1
  38.3 0.1 copy.23.b_ref
  38.4 0.4 collective-permute-done.7
  38.8 0.0 collective-permute-done.1
  38.8 0.0 collective-permute-done.6
  38.8 0.0 collective-permute-done.3
  38.8 0.0 collective-permute-done.4
  38.9 29.2 %fusion.1.x_ref = bf16[34,18,80,128]{3,2,1,0:T(8,128)(2,1)} fusion(bf16[1,1,64,128]{3,2,1,0:T(8,128)(2,1)S(1)} %collective-permute-done.7, bf16[1,16,64,128]{3,2,1,0:T(8,128)(2,1)} %collective-permute-done.6, bf16[1,1,64,128]{3,2,1,0:T(8,128)(2,1)S(1)} %collective-permute-done.5, bf16[32,1,64,128]{3,2,1,0:T(8,128)(2,1)S(1)} %collective-permute-done.4, ...), kind=kLoop, calls=%fused_computation.4 | loop fusion | flops 188006400 | bytes 22560768 | tf_op jit(solution)/shard_map/concatenate | solution.py:47
  68.1 42.1 %shard_map.67 = bf16[16,64,4096]{2,1,0:T(8,128)(2,1)} custom-call(s32[32]{0:T(128)S(1)} %pad_add_fusion.table_ref, bf16[34,18,80,128]{3,2,1,0:T(8,128)(2,1)} %fusion.1.x_ref, bf16[3,384,192]{2,1,0:T(8,128)(2,1)S(1)} %reshape.47.w_ref, f32[64,1]{1,0:T(8,128)S(1)} %copy.23.b_ref, f32[8,1,4096]{2,1,0:T(1,128)S(1)} %reshape.43.m_ref), custom_call_target="tpu_custom_call" | custom-call | tf_op jit(solution)/shard_map/pallas_call | solution.py:99
  110.2 110.7 %all_to_all.5 = bf16[16,64,4096]{2,1,0:T(8,128)(2,1)} all-to-all(bf16[16,64,4096]{2,1,0:T(8,128)(2,1)} %shard_map.67), channel_id=1, replica_groups=mesh['gx'=8,'gy'=16] {'gy'}, dimensions={0} | all-to-all | bytes 16777216 | tf_op jit(solution)/shard_map/all_to_all | solution.py:148
  220.8 7.9 %copy.29 = bf16[1,16,64,4096]{3,2,1,0:T(8,128)(2,1)} copy(bf16[1,16,64,4096]{3,2,1,0:T(8,128)(2,1)} %bitcast.16) | data formatting | bytes 16777216
  (4 shorter events, 0.0 us)
Async XLA Ops:
  0.0 23.5 %copy-start.2 = (s32[1,1,8,1]{2,3,1,0:T(1,128)S(1)}, s32[1,1,8,1]{2,3,1,0:T(1,128)}, u32[]{:S(2)}) copy-start(s32[1,1,8,1]{2,3,1,0:T(1,128)} %param.9) | copy-start | bytes 100
  2.0 36.3 %copy-start.1 = (f32[64]{0:T(128)S(1)}, f32[64]{0:T(128)}, u32[]{:S(2)}) copy-start(f32[64]{0:T(128)} %param.11) | copy-start | bytes 772
  8.4 24.5 %copy-start = (bf16[32,16,64,128]{3,2,1,0:T(8,128)(2,1)}, bf16[32,16,64,128]{3,2,1,0:T(8,128)(2,1)S(1)}, u32[]{:S(2)}) copy-start(bf16[32,16,64,128]{3,2,1,0:T(8,128)(2,1)S(1)} %broadcast_multiply_fusion) | copy-start | bytes 25165828
  8.4 15.3 %collective-permute-start = (bf16[1,1,64,128]{3,2,1,0:T(8,128)(2,1)S(1)}, bf16[1,1,64,128]{3,2,1,0:T(8,128)(2,1)S(1)}, u32[]{:S(2)}, u32[]{:S(2)}) collective-permute-start(bf16[1,1,64,128]{3,2,1,0:T(8,128)(2,1)S(1)} %get-tuple-element.5), channel_id=1, source_target_pairs={{0,17},{1,18},{2,19},{3,20},{4,21},{5,22},{6,23},{7,24},{8,25},{9,... | collective-permute-start | bytes 49160 | tf_op jit(solution)/shard_map/ppermute | solution.py:31
  11.2 16.2 %collective-permute-start.2 = (bf16[1,1,64,128]{3,2,1,0:T(8,128)(2,1)S(1)}, bf16[1,1,64,128]{3,2,1,0:T(8,128)(2,1)S(1)}, u32[]{:S(2)}, u32[]{:S(2)}) collective-permute-start(bf16[1,1,64,128]{3,2,1,0:T(8,128)(2,1)S(1)} %get-tuple-element.8), channel_id=1, source_target_pairs={{1,16},{2,17},{3,18},{4,19},{5,20},{6,21},{7,22},{8,23},{9,24},{10... | collective-permute-start | bytes 49160 | tf_op jit(solution)/shard_map/ppermute | solution.py:31
  13.6 25.3 %collective-permute-start.3 = (bf16[32,1,64,128]{3,2,1,0:T(8,128)(2,1)}, bf16[32,1,64,128]{3,2,1,0:T(8,128)(2,1)S(1)}, u32[]{:S(2)}, u32[]{:S(2)}) collective-permute-start(bf16[32,1,64,128]{3,2,1,0:T(8,128)(2,1)} %get-tuple-element.11), channel_id=1, source_target_pairs={{0,1},{1,2},{2,3},{3,4},{4,5},{5,6},{6,7},{7,8},{8,9},{9,10},{10,1... | collective-permute-start | bytes 1572872 | tf_op jit(solution)/shard_map/ppermute | solution.py:31
  19.4 19.4 %collective-permute-start.4 = (bf16[32,1,64,128]{3,2,1,0:T(8,128)(2,1)}, bf16[32,1,64,128]{3,2,1,0:T(8,128)(2,1)S(1)}, u32[]{:S(2)}, u32[]{:S(2)}) collective-permute-start(bf16[32,1,64,128]{3,2,1,0:T(8,128)(2,1)} %get-tuple-element.12), channel_id=1, source_target_pairs={{1,0},{2,1},{3,2},{4,3},{5,4},{6,5},{7,6},{8,7},{9,8},{10,9},{11,1... | collective-permute-start | bytes 1572872 | tf_op jit(solution)/shard_map/ppermute | solution.py:31
  21.6 17.2 %collective-permute-start.1 = (bf16[1,16,64,128]{3,2,1,0:T(8,128)(2,1)}, bf16[1,16,64,128]{3,2,1,0:T(8,128)(2,1)S(1)}, u32[]{:S(2)}, u32[]{:S(2)}) collective-permute-start(bf16[1,16,64,128]{3,2,1,0:T(8,128)(2,1)} %get-tuple-element.9), channel_id=1, source_target_pairs={{0,16},{16,32},{32,48},{48,64},{64,80},{80,96},{96,112},{1,17},{17... | collective-permute-start | bytes 786440 | tf_op jit(solution)/shard_map/ppermute | solution.py:31
  23.7 15.1 %collective-permute-start.6 = (bf16[1,16,64,128]{3,2,1,0:T(8,128)(2,1)}, bf16[1,16,64,128]{3,2,1,0:T(8,128)(2,1)}, u32[]{:S(2)}, u32[]{:S(2)}) collective-permute-start(bf16[1,16,64,128]{3,2,1,0:T(8,128)(2,1)} %get-tuple-element.10), channel_id=1, source_target_pairs={{16,0},{32,16},{48,32},{64,48},{80,64},{96,80},{112,96},{17,1},{33... | collective-permute-start | bytes 786440 | tf_op jit(solution)/shard_map/ppermute | solution.py:31
  27.5 5.4 %collective-permute-start.5 = (bf16[1,1,64,128]{3,2,1,0:T(8,128)(2,1)S(1)}, bf16[1,1,64,128]{3,2,1,0:T(8,128)(2,1)S(1)}, u32[]{:S(2)}, u32[]{:S(2)}) collective-permute-start(bf16[1,1,64,128]{3,2,1,0:T(8,128)(2,1)S(1)} %get-tuple-element.7), channel_id=1, source_target_pairs={{16,1},{17,2},{18,3},{19,4},{20,5},{21,6},{22,7},{23,8},{24,9},{25... | collective-permute-start | bytes 49160 | tf_op jit(solution)/shard_map/ppermute | solution.py:31
  32.9 6.0 %collective-permute-start.7 = (bf16[1,1,64,128]{3,2,1,0:T(8,128)(2,1)S(1)}, bf16[1,1,64,128]{3,2,1,0:T(8,128)(2,1)S(1)}, u32[]{:S(2)}, u32[]{:S(2)}) collective-permute-start(bf16[1,1,64,128]{3,2,1,0:T(8,128)(2,1)S(1)} %get-tuple-element.6), channel_id=1, source_target_pairs={{17,0},{18,1},{19,2},{20,3},{21,4},{22,5},{23,6},{24,7},{25,8},{26... | collective-permute-start | bytes 49160 | tf_op jit(solution)/shard_map/ppermute | solution.py:31

commit v7 on v5

--- a/solution.py
+++ b/solution.py
@@ -31,7 +31,7 @@
     slots = pl.num_programs(0)
     valid = table_ref[slots + slot]
     rows = EDGE * EDGE
-    group = 6
+    group = 9
     chunk = 4 * rows
 
     @pl.when(valid > 0)

time: 223 us -> 226 us (1.013)
  Pallas kernels: 41.9 us -> 46.7 us
    pallas_call x1, Pallas kernels: 41.9 us -> 46.7 us  [conv_slots(): pl.pallas_call(conv_kernel, out_shape=jax.ShapeDtypeStruct((total, C, EDG...]
where the time goes in v7:
time: 226 us; the launch traced here: 225 us
  blocking collectives  107 us (47%)
  Pallas kernels  46.7 us (21%)
  other arithmetic  29.3 us (13%)
  local copies, waits for them, and re-layouts  16.4 us (7%)
  waiting for transfers between devices  15.1 us (7%)
  starting transfers between devices  10.3 us (5%)
    all_to_all x1, blocking collectives, per_device(): lax.all_to_all(sending, 'gy', split_axis=0, concat_axis=0, tiled=True)  107 us
    pallas_call x1, Pallas kernels, conv_slots(): pl.pallas_call(conv_kernel, out_shape=jax.ShapeDtypeStruct((total, C, EDG...  46.7 us
    concatenate x1, other arithmetic, padded_2(): jnp.concatenate([lax.ppermute(tail, axis, [(i, (i + 1) % count) for i in...  19.2 us
    unnamed x7, local copies, waits for them, and re-layouts  11.3 us
    ppermute x2, waiting for transfers between devices, padded_2(): lax.ppermute(tail, axis, [(i, (i + 1) % count) for i in range(ends)])  8.6 us
    ppermute x2, waiting for transfers between devices, padded_2(): lax.ppermute(head, axis, [((i + 1) % count, i) for i in range(ends)])  6.51 us
    mul x1, other arithmetic, per_device(): inputs = features * live[..., None]  6.32 us
    ppermute x2, starting transfers between devices, padded_2(): lax.ppermute(tail, axis, [(i, (i + 1) % count) for i in range(ends)])  5.34 us
  transfers between devices with their start and end apart: 4, of which 4 were waited for; matrix products, arithmetic and copies ran while one was open for 2% of the time, Pallas kernels for 0%

profile of v7, /device:TPU:8, one launch (start us, length us, event | category | flops | bytes accessed | tf_op | source)
XLA Modules:
  0.0 225.3 jit_solution(715278914227906360)
XLA Ops:
  0.0 0.0 copy-start.2
  0.0 0.8 copy.18
  0.8 0.1 broadcast_in_dim.36
  0.9 0.1 broadcast_in_dim.37
  0.9 0.1 copy.19
  1.0 1.0 multiply_convert_fusion
  2.0 6.3 %broadcast_multiply_fusion = bf16[32,16,64,128]{3,2,1,0:T(8,128)(2,1)S(1)} fusion(bf16[32,16,64,128]{3,2,1,0:T(8,128)(2,1)} %param.6, bf16[32,16,64]{2,1,0:T(8,128)(2,1)S(1)} %multiply_convert_fusion), kind=kLoop, calls=%fused_computation.10 | loop fusion | flops 4194304 | bytes 16842752 | tf_op jit(solution)/shard_map/mul | solution.py:109
  8.3 0.0 copy-start
  8.3 3.4 %copy-done = bf16[32,16,64,128]{3,2,1,0:T(8,128)(2,1)} copy-done((bf16[32,16,64,128]{3,2,1,0:T(8,128)(2,1)}, bf16[32,16,64,128]{3,2,1,0:T(8,128)(2,1)S(1)}, u32[]{:S(2)}) %copy-start) | copy-done | bytes 8388632
  11.7 0.0 copy-start.1
  11.8 1.9 collective-permute-start
  13.7 3.6 %collective-permute-start.1 = (bf16[1,16,64,128]{3,2,1,0:T(8,128)(2,1)S(1)}, bf16[1,16,64,128]{3,2,1,0:T(8,128)(2,1)S(1)}, u32[]{:S(2)}, u32[]{:S(2)}) collective-permute-start(bf16[1,16,64,128]{3,2,1,0:T(8,128)(2,1)S(1)} %get-tuple-element.8), channel_id=1, source_target_pairs={{16,0},{32,16},{48,32},{64,48},{80,64},{96,80},{112,96},{17,1},{33... | collective-permute-start | bytes 786440 | tf_op jit(solution)/shard_map/ppermute | solution.py:22
  17.4 0.5 reshape.46
  17.8 0.0 copy-done.2
  17.8 0.2 convert_reduce_fusion
  18.0 1.4 collective-permute-done
  19.5 1.8 collective-permute-done.1
  21.2 2.3 %pad_maximum_fusion.2 = (bf16[34,1,64,128]{3,2,1,0:T(8,128)(2,1)}, bf16[34,1,64,128]{3,2,1,0:T(8,128)(2,1)}) fusion(bf16[1,16,64,128]{3,2,1,0:T(8,128)(2,1)S(1)} %collective-permute-done.1, bf16[32,16,64,128]{3,2,1,0:T(8,128)(2,1)} %copy-done, bf16[1,16,64,128]{3,2,1,0:T(8,128)(2,1)S(1)} %collective-permute-done), kind=kLoop, calls=%fused_computation.14 | loop fusion | flops 1114112 | bytes 10027008 | tf_op jit(solution)/shard_map/slice | solution.py:17
  23.6 3.4 %collective-permute-start.2 = (bf16[34,1,64,128]{3,2,1,0:T(8,128)(2,1)}, bf16[34,1,64,128]{3,2,1,0:T(8,128)(2,1)S(1)}, u32[]{:S(2)}, u32[]{:S(2)}) collective-permute-start(bf16[34,1,64,128]{3,2,1,0:T(8,128)(2,1)} %get-tuple-element.5), channel_id=1, source_target_pairs={{0,1},{1,2},{2,3},{3,4},{4,5},{5,6},{6,7},{7,8},{8,9},{9,10},{10,1... | collective-permute-start | bytes 1671176 | tf_op jit(solution)/shard_map/ppermute | solution.py:20
  27.0 1.3 collective-permute-start.3
  28.3 0.1 fusion.6
  28.4 0.1 copy.27
  28.5 0.4 reshape.43.m_ref
  28.9 2.4 %copy.24 = bf16[3,3,128,3,64]{4,3,2,1,0:T(4,128)(2,1)S(1)} copy(bf16[3,3,128,3,64]{2,4,1,0,3:T(8,128)(2,1)} %bitcast.18) | data formatting | bytes 884736 | tf_op jit(solution)/shard_map/reshape | solution.py:124
  31.2 0.7 reshape.47.w_ref
  32.0 0.0 copy-done.1
  32.0 0.1 copy.23.b_ref
  32.1 0.1 select_reduce_fusion
  32.2 0.1 pad_add_fusion.table_ref
  32.3 7.1 %collective-permute-done.2 = bf16[34,1,64,128]{3,2,1,0:T(8,128)(2,1)S(1)} collective-permute-done((bf16[34,1,64,128]{3,2,1,0:T(8,128)(2,1)}, bf16[34,1,64,128]{3,2,1,0:T(8,128)(2,1)S(1)}, u32[]{:S(2)}, u32[]{:S(2)}) %collective-permute-start.2) | collective-permute-done | bytes 557088 | tf_op jit(solution)/shard_map/ppermute | solution.py:20
  39.4 4.8 %collective-permute-done.3 = bf16[34,1,64,128]{3,2,1,0:T(8,128)(2,1)} collective-permute-done((bf16[34,1,64,128]{3,2,1,0:T(8,128)(2,1)}, bf16[34,1,64,128]{3,2,1,0:T(8,128)(2,1)}, u32[]{:S(2)}, u32[]{:S(2)}) %collective-permute-start.3) | collective-permute-done | bytes 557088 | tf_op jit(solution)/shard_map/ppermute | solution.py:22
  44.2 19.2 %select_maximum_fusion.x_ref = bf16[34,18,80,128]{3,2,1,0:T(8,128)(2,1)} fusion(bf16[34,1,64,128]{3,2,1,0:T(8,128)(2,1)} %collective-permute-done.3, bf16[34,1,64,128]{3,2,1,0:T(8,128)(2,1)S(1)} %collective-permute-done.2, bf16[1,16,64,128]{3,2,1,0:T(8,128)(2,1)S(1)} %collective-permute-done.1, bf16[32,16,64,128]{3,2,1,0:T(8,128)(2,1)} %copy-done, ...), kind=kLoop, calls=%fused_computation.3 | loop fusion | flops 112803840 | bytes 22560768 | tf_op jit(solution)/shard_map/concatenate | solution.py:18
  63.4 46.7 %shard_map.67 = bf16[16,64,4096]{2,1,0:T(8,128)(2,1)} custom-call(s32[32]{0:T(128)S(1)} %pad_add_fusion.table_ref, bf16[34,18,80,128]{3,2,1,0:T(8,128)(2,1)} %select_maximum_fusion.x_ref, bf16[3,384,192]{2,1,0:T(8,128)(2,1)S(1)} %reshape.47.w_ref, f32[64,1]{1,0:T(8,128)S(1)} %copy.23.b_ref, f32[8,1,4096]{2,1,0:T(1,128)S(1)} %reshape.43.m_ref), custom_call_target="tpu_custom_call" | custom-call | tf_op jit(solution)/shard_map/pallas_call | solution.py:78
  110.1 107.3 %all_to_all.5 = bf16[16,64,4096]{2,1,0:T(8,128)(2,1)} all-to-all(bf16[16,64,4096]{2,1,0:T(8,128)(2,1)} %shard_map.67), channel_id=1, replica_groups=mesh['gx'=8,'gy'=16] {'gy'}, dimensions={0} | all-to-all | bytes 16777216 | tf_op jit(solution)/shard_map/all_to_all | solution.py:127
  217.4 7.9 %copy.29 = bf16[1,16,64,4096]{3,2,1,0:T(8,128)(2,1)} copy(bf16[1,16,64,4096]{3,2,1,0:T(8,128)(2,1)} %bitcast.16) | data formatting | bytes 16777216
  (4 shorter events, 0.1 us)
Async XLA Ops:
  0.0 17.8 %copy-start.2 = (s32[1,1,8,1]{2,3,1,0:T(1,128)S(1)}, s32[1,1,8,1]{2,3,1,0:T(1,128)}, u32[]{:S(2)}) copy-start(s32[1,1,8,1]{2,3,1,0:T(1,128)} %param.9) | copy-start | bytes 100
  8.3 3.4 %copy-start = (bf16[32,16,64,128]{3,2,1,0:T(8,128)(2,1)}, bf16[32,16,64,128]{3,2,1,0:T(8,128)(2,1)S(1)}, u32[]{:S(2)}) copy-start(bf16[32,16,64,128]{3,2,1,0:T(8,128)(2,1)S(1)} %broadcast_multiply_fusion) | copy-start | bytes 25165828
  11.7 20.2 %copy-start.1 = (f32[64]{0:T(128)S(1)}, f32[64]{0:T(128)}, u32[]{:S(2)}) copy-start(f32[64]{0:T(128)} %param.11) | copy-start | bytes 772
  11.8 7.7 %collective-permute-start = (bf16[1,16,64,128]{3,2,1,0:T(8,128)(2,1)S(1)}, bf16[1,16,64,128]{3,2,1,0:T(8,128)(2,1)S(1)}, u32[]{:S(2)}, u32[]{:S(2)}) collective-permute-start(bf16[1,16,64,128]{3,2,1,0:T(8,128)(2,1)S(1)} %get-tuple-element.7), channel_id=1, source_target_pairs={{0,16},{16,32},{32,48},{48,64},{64,80},{80,96},{96,112},{1,17},{17... | collective-permute-start | bytes 786440 | tf_op jit(solution)/shard_map/ppermute | solution.py:20
  13.7 7.5 %collective-permute-start.1 = (bf16[1,16,64,128]{3,2,1,0:T(8,128)(2,1)S(1)}, bf16[1,16,64,128]{3,2,1,0:T(8,128)(2,1)S(1)}, u32[]{:S(2)}, u32[]{:S(2)}) collective-permute-start(bf16[1,16,64,128]{3,2,1,0:T(8,128)(2,1)S(1)} %get-tuple-element.8), channel_id=1, source_target_pairs={{16,0},{32,16},{48,32},{64,48},{80,64},{96,80},{112,96},{17,1},{33... | collective-permute-start | bytes 786440 | tf_op jit(solution)/shard_map/ppermute | solution.py:22
  23.6 15.8 %collective-permute-start.2 = (bf16[34,1,64,128]{3,2,1,0:T(8,128)(2,1)}, bf16[34,1,64,128]{3,2,1,0:T(8,128)(2,1)S(1)}, u32[]{:S(2)}, u32[]{:S(2)}) collective-permute-start(bf16[34,1,64,128]{3,2,1,0:T(8,128)(2,1)} %get-tuple-element.5), channel_id=1, source_target_pairs={{0,1},{1,2},{2,3},{3,4},{4,5},{5,6},{6,7},{7,8},{8,9},{9,10},{10,1... | collective-permute-start | bytes 1671176 | tf_op jit(solution)/shard_map/ppermute | solution.py:20
  27.0 17.2 %collective-permute-start.3 = (bf16[34,1,64,128]{3,2,1,0:T(8,128)(2,1)}, bf16[34,1,64,128]{3,2,1,0:T(8,128)(2,1)}, u32[]{:S(2)}, u32[]{:S(2)}) collective-permute-start(bf16[34,1,64,128]{3,2,1,0:T(8,128)(2,1)} %get-tuple-element.6), channel_id=1, source_target_pairs={{1,0},{2,1},{3,2},{4,3},{5,4},{6,5},{7,6},{8,7},{9,8},{10,9},{11,1... | collective-permute-start | bytes 1671176 | tf_op jit(solution)/shard_map/ppermute | solution.py:22

commit v8 on v5

--- a/solution.py
+++ b/solution.py
@@ -120,7 +120,10 @@
     hit = slots[None, :] == jnp.arange(total, dtype=jnp.int32)[:, None]
     brick_of_slot = jnp.sum(jnp.where(hit, order[None, :], 0), axis=1)
     valid = jnp.any(hit, axis=1).astype(jnp.int32)
-    table = jnp.concatenate([brick_of_slot, valid]).astype(jnp.int32)
+    seen = lax.cummax(jnp.where(valid > 0, jnp.arange(total, dtype=jnp.int32), -1))
+    first = jnp.argmax(valid)
+    held = jnp.where(seen >= 0, brick_of_slot[jnp.maximum(seen, 0)], brick_of_slot[first])
+    table = jnp.concatenate([held, valid]).astype(jnp.int32)
     w9 = weights.transpose(1, 2, 3, 0, 4).reshape(3, 3 * channels_in, 3 * C)
     bias_col = bias.reshape(C, 1).astype(jnp.float32)
     sending = conv_slots(table, shifted, w9, bias_col, brick_masks, total, bricks_z)

time: 223 us -> 221 us (level)
  waiting for transfers between devices: 15.1 us -> 11 us
    ppermute x2, waiting for transfers between devices: 8.6 us -> 6.21 us  [padded_2(): lax.ppermute(tail, axis, [(i, (i + 1) % count) for i in range(ends)])]
  transfers between devices with their start and end apart: 4 -> 4, of which waited for: 4 -> 2; matrix products, arithmetic and copies ran while one was open for 2% -> 3% of each run, Pallas kernels for 0% -> 0%
where the time goes in v8:
time: 221 us; the launch traced here: 220 us
  blocking collectives  107 us (48%)
  Pallas kernels  41.9 us (19%)
  other arithmetic  30.9 us (14%)
  local copies, waits for them, and re-layouts  17.8 us (8%)
  waiting for transfers between devices  11 us (5%)
  starting transfers between devices  10.3 us (5%)
    all_to_all x1, blocking collectives, per_device(): lax.all_to_all(sending, 'gy', split_axis=0, concat_axis=0, tiled=True)  107 us
    pallas_call x1, Pallas kernels, conv_slots(): pl.pallas_call(conv_kernel, out_shape=jax.ShapeDtypeStruct((total, C, EDG...  41.9 us
    concatenate x1, other arithmetic, padded_2(): jnp.concatenate([lax.ppermute(tail, axis, [(i, (i + 1) % count) for i in...  19.2 us
    unnamed x7, local copies, waits for them, and re-layouts  11.3 us
    mul x1, other arithmetic, per_device(): inputs = features * live[..., None]  6.32 us
    ppermute x2, waiting for transfers between devices, padded_2(): lax.ppermute(tail, axis, [(i, (i + 1) % count) for i in range(ends)])  6.21 us
    ppermute x2, starting transfers between devices, padded_2(): lax.ppermute(tail, axis, [(i, (i + 1) % count) for i in range(ends)])  5.34 us
    ppermute x2, starting transfers between devices, padded_2(): lax.ppermute(head, axis, [((i + 1) % count, i) for i in range(ends)])  4.93 us
  transfers between devices with their start and end apart: 4, of which 2 were waited for; matrix products, arithmetic and copies ran while one was open for 3% of the time, Pallas kernels for 0%

profile of v8, /device:TPU:8, one launch (start us, length us, event | category | flops | bytes accessed | tf_op | source)
XLA Modules:
  0.0 220.2 jit_solution(17050212151454299951)
XLA Ops:
  0.0 0.0 copy-start.2
  0.0 0.8 copy.21
  0.8 0.1 broadcast_in_dim.47
  0.9 0.1 broadcast_in_dim.48
  0.9 0.1 copy.22
  1.0 1.0 multiply_convert_fusion
  2.0 6.3 %broadcast_multiply_fusion = bf16[32,16,64,128]{3,2,1,0:T(8,128)(2,1)S(1)} fusion(bf16[32,16,64,128]{3,2,1,0:T(8,128)(2,1)} %param.6, bf16[32,16,64]{2,1,0:T(8,128)(2,1)S(1)} %multiply_convert_fusion), kind=kLoop, calls=%fused_computation.11 | loop fusion | flops 4194304 | bytes 16842752 | tf_op jit(solution)/shard_map/mul | solution.py:109
  8.3 0.0 copy-start
  8.4 3.4 %copy-done = bf16[32,16,64,128]{3,2,1,0:T(8,128)(2,1)} copy-done((bf16[32,16,64,128]{3,2,1,0:T(8,128)(2,1)}, bf16[32,16,64,128]{3,2,1,0:T(8,128)(2,1)S(1)}, u32[]{:S(2)}) %copy-start) | copy-done | bytes 8388632
  11.7 0.0 copy-start.1
  11.8 1.9 collective-permute-start
  13.7 3.6 %collective-permute-start.1 = (bf16[1,16,64,128]{3,2,1,0:T(8,128)(2,1)S(1)}, bf16[1,16,64,128]{3,2,1,0:T(8,128)(2,1)S(1)}, u32[]{:S(2)}, u32[]{:S(2)}) collective-permute-start(bf16[1,16,64,128]{3,2,1,0:T(8,128)(2,1)S(1)} %get-tuple-element.10), channel_id=1, source_target_pairs={{16,0},{32,16},{48,32},{64,48},{80,64},{96,80},{112,96},{17,1},{33... | collective-permute-start | bytes 786440 | tf_op jit(solution)/shard_map/ppermute | solution.py:22
  17.4 0.0 copy-done.2
  17.4 0.2 convert_reduce_fusion
  17.6 0.1 fusion.6
  17.6 0.7 iota_reduce_fusion
  18.4 0.5 reshape.76
  20.0 0.1 copy.20
  20.6 0.1 select_reduce_fusion
  20.7 0.6 dynamic_slice.3
  21.3 0.1 maximum_reduce_fusion
  21.4 0.0 collective-permute-done
  21.4 0.0 collective-permute-done.1
  21.4 2.3 %pad_maximum_fusion.2 = (bf16[34,1,64,128]{3,2,1,0:T(8,128)(2,1)}, bf16[34,1,64,128]{3,2,1,0:T(8,128)(2,1)}) fusion(bf16[1,16,64,128]{3,2,1,0:T(8,128)(2,1)S(1)} %collective-permute-done.1, bf16[32,16,64,128]{3,2,1,0:T(8,128)(2,1)} %copy-done, bf16[1,16,64,128]{3,2,1,0:T(8,128)(2,1)S(1)} %collective-permute-done), kind=kLoop, calls=%fused_computation.15 | loop fusion | flops 1114112 | bytes 10027008 | tf_op jit(solution)/shard_map/slice | solution.py:17
  23.8 3.4 %collective-permute-start.2 = (bf16[34,1,64,128]{3,2,1,0:T(8,128)(2,1)}, bf16[34,1,64,128]{3,2,1,0:T(8,128)(2,1)S(1)}, u32[]{:S(2)}, u32[]{:S(2)}) collective-permute-start(bf16[34,1,64,128]{3,2,1,0:T(8,128)(2,1)} %get-tuple-element.7), channel_id=1, source_target_pairs={{0,1},{1,2},{2,3},{3,4},{4,5},{5,6},{6,7},{7,8},{8,9},{9,10},{10,1... | collective-permute-start | bytes 1671176 | tf_op jit(solution)/shard_map/ppermute | solution.py:20
  27.2 1.3 collective-permute-start.3
  28.5 0.7 gather_fusion
  29.2 0.1 copy.30
  29.3 0.4 reshape.73.m_ref
  29.7 2.4 %copy.27 = bf16[3,3,128,3,64]{4,3,2,1,0:T(4,128)(2,1)S(1)} copy(bf16[3,3,128,3,64]{2,4,1,0,3:T(8,128)(2,1)} %bitcast.21) | data formatting | bytes 884736 | tf_op jit(solution)/shard_map/reshape | solution.py:127
  32.0 0.7 reshape.85.w_ref
  32.8 0.0 copy-done.1
  32.8 0.1 copy.26.b_ref
  32.9 0.1 compare_reduce_fusion
  33.0 0.6 broadcast_select_fusion
  33.6 0.1 pad_add_fusion.table_ref
  33.7 6.2 %collective-permute-done.2 = bf16[34,1,64,128]{3,2,1,0:T(8,128)(2,1)S(1)} collective-permute-done((bf16[34,1,64,128]{3,2,1,0:T(8,128)(2,1)}, bf16[34,1,64,128]{3,2,1,0:T(8,128)(2,1)S(1)}, u32[]{:S(2)}, u32[]{:S(2)}) %collective-permute-start.2) | collective-permute-done | bytes 557088 | tf_op jit(solution)/shard_map/ppermute | solution.py:20
  39.9 4.7 %collective-permute-done.3 = bf16[34,1,64,128]{3,2,1,0:T(8,128)(2,1)} collective-permute-done((bf16[34,1,64,128]{3,2,1,0:T(8,128)(2,1)}, bf16[34,1,64,128]{3,2,1,0:T(8,128)(2,1)}, u32[]{:S(2)}, u32[]{:S(2)}) %collective-permute-start.3) | collective-permute-done | bytes 557088 | tf_op jit(solution)/shard_map/ppermute | solution.py:22
  44.6 19.2 %select_maximum_fusion.x_ref = bf16[34,18,80,128]{3,2,1,0:T(8,128)(2,1)} fusion(bf16[34,1,64,128]{3,2,1,0:T(8,128)(2,1)} %collective-permute-done.3, bf16[34,1,64,128]{3,2,1,0:T(8,128)(2,1)S(1)} %collective-permute-done.2, bf16[1,16,64,128]{3,2,1,0:T(8,128)(2,1)S(1)} %collective-permute-done.1, bf16[32,16,64,128]{3,2,1,0:T(8,128)(2,1)} %copy-done, ...), kind=kLoop, calls=%fused_computation.4 | loop fusion | flops 112803840 | bytes 22560768 | tf_op jit(solution)/shard_map/concatenate | solution.py:18
  63.8 41.9 %shard_map.67 = bf16[16,64,4096]{2,1,0:T(8,128)(2,1)} custom-call(s32[32]{0:T(128)S(1)} %pad_add_fusion.table_ref, bf16[34,18,80,128]{3,2,1,0:T(8,128)(2,1)} %select_maximum_fusion.x_ref, bf16[3,384,192]{2,1,0:T(8,128)(2,1)S(1)} %reshape.85.w_ref, f32[64,1]{1,0:T(8,128)S(1)} %copy.26.b_ref, f32[8,1,4096]{2,1,0:T(1,128)S(1)} %reshape.73.m_ref), custom_call_target="tpu_custom_call" | custom-call | tf_op jit(solution)/shard_map/pallas_call | solution.py:78
  105.7 106.6 %all_to_all.5 = bf16[16,64,4096]{2,1,0:T(8,128)(2,1)} all-to-all(bf16[16,64,4096]{2,1,0:T(8,128)(2,1)} %shard_map.67), channel_id=1, replica_groups=mesh['gx'=8,'gy'=16] {'gy'}, dimensions={0} | all-to-all | bytes 16777216 | tf_op jit(solution)/shard_map/all_to_all | solution.py:130
  212.3 7.9 %copy.32 = bf16[1,16,64,4096]{3,2,1,0:T(8,128)(2,1)} copy(bf16[1,16,64,4096]{3,2,1,0:T(8,128)(2,1)} %bitcast.19) | data formatting | bytes 16777216
  (7 shorter events, 0.1 us)
Async XLA Ops:
  0.0 17.4 %copy-start.2 = (s32[1,1,8,1]{2,3,1,0:T(1,128)S(1)}, s32[1,1,8,1]{2,3,1,0:T(1,128)}, u32[]{:S(2)}) copy-start(s32[1,1,8,1]{2,3,1,0:T(1,128)} %param.9) | copy-start | bytes 100
  8.3 3.4 %copy-start = (bf16[32,16,64,128]{3,2,1,0:T(8,128)(2,1)}, bf16[32,16,64,128]{3,2,1,0:T(8,128)(2,1)S(1)}, u32[]{:S(2)}) copy-start(bf16[32,16,64,128]{3,2,1,0:T(8,128)(2,1)S(1)} %broadcast_multiply_fusion) | copy-start | bytes 25165828
  11.7 21.0 %copy-start.1 = (f32[64]{0:T(128)S(1)}, f32[64]{0:T(128)}, u32[]{:S(2)}) copy-start(f32[64]{0:T(128)} %param.11) | copy-start | bytes 772
  11.8 9.6 %collective-permute-start = (bf16[1,16,64,128]{3,2,1,0:T(8,128)(2,1)S(1)}, bf16[1,16,64,128]{3,2,1,0:T(8,128)(2,1)S(1)}, u32[]{:S(2)}, u32[]{:S(2)}) collective-permute-start(bf16[1,16,64,128]{3,2,1,0:T(8,128)(2,1)S(1)} %get-tuple-element.9), channel_id=1, source_target_pairs={{0,16},{16,32},{32,48},{48,64},{64,80},{80,96},{96,112},{1,17},{17... | collective-permute-start | bytes 786440 | tf_op jit(solution)/shard_map/ppermute | solution.py:20
  13.7 7.7 %collective-permute-start.1 = (bf16[1,16,64,128]{3,2,1,0:T(8,128)(2,1)S(1)}, bf16[1,16,64,128]{3,2,1,0:T(8,128)(2,1)S(1)}, u32[]{:S(2)}, u32[]{:S(2)}) collective-permute-start(bf16[1,16,64,128]{3,2,1,0:T(8,128)(2,1)S(1)} %get-tuple-element.10), channel_id=1, source_target_pairs={{16,0},{32,16},{48,32},{64,48},{80,64},{96,80},{112,96},{17,1},{33... | collective-permute-start | bytes 786440 | tf_op jit(solution)/shard_map/ppermute | solution.py:22
  23.8 16.1 %collective-permute-start.2 = (bf16[34,1,64,128]{3,2,1,0:T(8,128)(2,1)}, bf16[34,1,64,128]{3,2,1,0:T(8,128)(2,1)S(1)}, u32[]{:S(2)}, u32[]{:S(2)}) collective-permute-start(bf16[34,1,64,128]{3,2,1,0:T(8,128)(2,1)} %get-tuple-element.7), channel_id=1, source_target_pairs={{0,1},{1,2},{2,3},{3,4},{4,5},{5,6},{6,7},{7,8},{8,9},{9,10},{10,1... | collective-permute-start | bytes 1671176 | tf_op jit(solution)/shard_map/ppermute | solution.py:20
  27.2 17.4 %collective-permute-start.3 = (bf16[34,1,64,128]{3,2,1,0:T(8,128)(2,1)}, bf16[34,1,64,128]{3,2,1,0:T(8,128)(2,1)}, u32[]{:S(2)}, u32[]{:S(2)}) collective-permute-start(bf16[34,1,64,128]{3,2,1,0:T(8,128)(2,1)} %get-tuple-element.8), channel_id=1, source_target_pairs={{1,0},{2,1},{3,2},{4,3},{5,4},{6,5},{7,6},{8,7},{9,8},{10,9},{11,1... | collective-permute-start | bytes 1671176 | tf_op jit(solution)/shard_map/ppermute | solution.py:22

commit v9 on v7

--- a/solution.py
+++ b/solution.py
@@ -31,7 +31,7 @@
     slots = pl.num_programs(0)
     valid = table_ref[slots + slot]
     rows = EDGE * EDGE
-    group = 9
+    group = 3
     chunk = 4 * rows
 
     @pl.when(valid > 0)

time: 226 us -> 222 us (0.982)
  Pallas kernels: 46.7 us -> 42.9 us
    pallas_call x1, Pallas kernels: 46.7 us -> 42.9 us  [conv_slots(): pl.pallas_call(conv_kernel, out_shape=jax.ShapeDtypeStruct((total, C, EDG...]
where the time goes in v9:
time: 222 us; the launch traced here: 220 us
  blocking collectives  106 us (48%)
  Pallas kernels  42.9 us (19%)
  other arithmetic  29.3 us (13%)
  local copies, waits for them, and re-layouts  16.4 us (7%)
  waiting for transfers between devices  15.1 us (7%)
  starting transfers between devices  10.3 us (5%)
    all_to_all x1, blocking collectives, per_device(): lax.all_to_all(sending, 'gy', split_axis=0, concat_axis=0, tiled=True)  106 us
    pallas_call x1, Pallas kernels, conv_slots(): pl.pallas_call(conv_kernel, out_shape=jax.ShapeDtypeStruct((total, C, EDG...  42.9 us
    concatenate x1, other arithmetic, padded_2(): jnp.concatenate([lax.ppermute(tail, axis, [(i, (i + 1) % count) for i in...  19.2 us
    unnamed x7, local copies, waits for them, and re-layouts  11.3 us
    ppermute x2, waiting for transfers between devices, padded_2(): lax.ppermute(tail, axis, [(i, (i + 1) % count) for i in range(ends)])  8.6 us
    ppermute x2, waiting for transfers between devices, padded_2(): lax.ppermute(head, axis, [((i + 1) % count, i) for i in range(ends)])  6.51 us
    mul x1, other arithmetic, per_device(): inputs = features * live[..., None]  6.32 us
    ppermute x2, starting transfers between devices, padded_2(): lax.ppermute(tail, axis, [(i, (i + 1) % count) for i in range(ends)])  5.34 us
  transfers between devices with their start and end apart: 4, of which 4 were waited for; matrix products, arithmetic and copies ran while one was open for 2% of the time, Pallas kernels for 0%

profile of v9, /device:TPU:8, one launch (start us, length us, event | category | flops | bytes accessed | tf_op | source)
XLA Modules:
  0.0 220.2 jit_solution(12539929213153484790)
XLA Ops:
  0.0 0.0 copy-start.2
  0.0 0.8 copy.18
  0.8 0.1 broadcast_in_dim.36
  0.9 0.1 broadcast_in_dim.37
  0.9 0.1 copy.19
  1.0 1.0 multiply_convert_fusion
  2.0 6.3 %broadcast_multiply_fusion = bf16[32,16,64,128]{3,2,1,0:T(8,128)(2,1)S(1)} fusion(bf16[32,16,64,128]{3,2,1,0:T(8,128)(2,1)} %param.6, bf16[32,16,64]{2,1,0:T(8,128)(2,1)S(1)} %multiply_convert_fusion), kind=kLoop, calls=%fused_computation.10 | loop fusion | flops 4194304 | bytes 16842752 | tf_op jit(solution)/shard_map/mul | solution.py:109
  8.3 0.0 copy-start
  8.3 3.4 %copy-done = bf16[32,16,64,128]{3,2,1,0:T(8,128)(2,1)} copy-done((bf16[32,16,64,128]{3,2,1,0:T(8,128)(2,1)}, bf16[32,16,64,128]{3,2,1,0:T(8,128)(2,1)S(1)}, u32[]{:S(2)}) %copy-start) | copy-done | bytes 8388632
  11.7 0.0 copy-start.1
  11.8 1.9 collective-permute-start
  13.7 3.6 %collective-permute-start.1 = (bf16[1,16,64,128]{3,2,1,0:T(8,128)(2,1)S(1)}, bf16[1,16,64,128]{3,2,1,0:T(8,128)(2,1)S(1)}, u32[]{:S(2)}, u32[]{:S(2)}) collective-permute-start(bf16[1,16,64,128]{3,2,1,0:T(8,128)(2,1)S(1)} %get-tuple-element.8), channel_id=1, source_target_pairs={{16,0},{32,16},{48,32},{64,48},{80,64},{96,80},{112,96},{17,1},{33... | collective-permute-start | bytes 786440 | tf_op jit(solution)/shard_map/ppermute | solution.py:22
  17.4 0.5 reshape.46
  17.8 0.0 copy-done.2
  17.8 0.2 convert_reduce_fusion
  18.0 1.4 collective-permute-done
  19.5 1.8 collective-permute-done.1
  21.2 2.3 %pad_maximum_fusion.2 = (bf16[34,1,64,128]{3,2,1,0:T(8,128)(2,1)}, bf16[34,1,64,128]{3,2,1,0:T(8,128)(2,1)}) fusion(bf16[1,16,64,128]{3,2,1,0:T(8,128)(2,1)S(1)} %collective-permute-done.1, bf16[32,16,64,128]{3,2,1,0:T(8,128)(2,1)} %copy-done, bf16[1,16,64,128]{3,2,1,0:T(8,128)(2,1)S(1)} %collective-permute-done), kind=kLoop, calls=%fused_computation.14 | loop fusion | flops 1114112 | bytes 10027008 | tf_op jit(solution)/shard_map/slice | solution.py:17
  23.6 3.4 %collective-permute-start.2 = (bf16[34,1,64,128]{3,2,1,0:T(8,128)(2,1)}, bf16[34,1,64,128]{3,2,1,0:T(8,128)(2,1)S(1)}, u32[]{:S(2)}, u32[]{:S(2)}) collective-permute-start(bf16[34,1,64,128]{3,2,1,0:T(8,128)(2,1)} %get-tuple-element.5), channel_id=1, source_target_pairs={{0,1},{1,2},{2,3},{3,4},{4,5},{5,6},{6,7},{7,8},{8,9},{9,10},{10,1... | collective-permute-start | bytes 1671176 | tf_op jit(solution)/shard_map/ppermute | solution.py:20
  27.0 1.3 collective-permute-start.3
  28.3 0.1 fusion.6
  28.4 0.1 copy.27
  28.5 0.4 reshape.43.m_ref
  28.9 2.4 %copy.24 = bf16[3,3,128,3,64]{4,3,2,1,0:T(4,128)(2,1)S(1)} copy(bf16[3,3,128,3,64]{2,4,1,0,3:T(8,128)(2,1)} %bitcast.18) | data formatting | bytes 884736 | tf_op jit(solution)/shard_map/reshape | solution.py:124
  31.2 0.7 reshape.47.w_ref
  32.0 0.0 copy-done.1
  32.0 0.1 copy.23.b_ref
  32.1 0.1 select_reduce_fusion
  32.2 0.1 pad_add_fusion.table_ref
  32.3 7.1 %collective-permute-done.2 = bf16[34,1,64,128]{3,2,1,0:T(8,128)(2,1)S(1)} collective-permute-done((bf16[34,1,64,128]{3,2,1,0:T(8,128)(2,1)}, bf16[34,1,64,128]{3,2,1,0:T(8,128)(2,1)S(1)}, u32[]{:S(2)}, u32[]{:S(2)}) %collective-permute-start.2) | collective-permute-done | bytes 557088 | tf_op jit(solution)/shard_map/ppermute | solution.py:20
  39.4 4.8 %collective-permute-done.3 = bf16[34,1,64,128]{3,2,1,0:T(8,128)(2,1)} collective-permute-done((bf16[34,1,64,128]{3,2,1,0:T(8,128)(2,1)}, bf16[34,1,64,128]{3,2,1,0:T(8,128)(2,1)}, u32[]{:S(2)}, u32[]{:S(2)}) %collective-permute-start.3) | collective-permute-done | bytes 557088 | tf_op jit(solution)/shard_map/ppermute | solution.py:22
  44.2 19.2 %select_maximum_fusion.x_ref = bf16[34,18,80,128]{3,2,1,0:T(8,128)(2,1)} fusion(bf16[34,1,64,128]{3,2,1,0:T(8,128)(2,1)} %collective-permute-done.3, bf16[34,1,64,128]{3,2,1,0:T(8,128)(2,1)S(1)} %collective-permute-done.2, bf16[1,16,64,128]{3,2,1,0:T(8,128)(2,1)S(1)} %collective-permute-done.1, bf16[32,16,64,128]{3,2,1,0:T(8,128)(2,1)} %copy-done, ...), kind=kLoop, calls=%fused_computation.3 | loop fusion | flops 112803840 | bytes 22560768 | tf_op jit(solution)/shard_map/concatenate | solution.py:18
  63.4 42.9 %shard_map.67 = bf16[16,64,4096]{2,1,0:T(8,128)(2,1)} custom-call(s32[32]{0:T(128)S(1)} %pad_add_fusion.table_ref, bf16[34,18,80,128]{3,2,1,0:T(8,128)(2,1)} %select_maximum_fusion.x_ref, bf16[3,384,192]{2,1,0:T(8,128)(2,1)S(1)} %reshape.47.w_ref, f32[64,1]{1,0:T(8,128)S(1)} %copy.23.b_ref, f32[8,1,4096]{2,1,0:T(1,128)S(1)} %reshape.43.m_ref), custom_call_target="tpu_custom_call" | custom-call | tf_op jit(solution)/shard_map/pallas_call | solution.py:78
  106.3 106.1 %all_to_all.5 = bf16[16,64,4096]{2,1,0:T(8,128)(2,1)} all-to-all(bf16[16,64,4096]{2,1,0:T(8,128)(2,1)} %shard_map.67), channel_id=1, replica_groups=mesh['gx'=8,'gy'=16] {'gy'}, dimensions={0} | all-to-all | bytes 16777216 | tf_op jit(solution)/shard_map/all_to_all | solution.py:127
  212.4 7.9 %copy.29 = bf16[1,16,64,4096]{3,2,1,0:T(8,128)(2,1)} copy(bf16[1,16,64,4096]{3,2,1,0:T(8,128)(2,1)} %bitcast.16) | data formatting | bytes 16777216
  (4 shorter events, 0.1 us)
Async XLA Ops:
  0.0 17.8 %copy-start.2 = (s32[1,1,8,1]{2,3,1,0:T(1,128)S(1)}, s32[1,1,8,1]{2,3,1,0:T(1,128)}, u32[]{:S(2)}) copy-start(s32[1,1,8,1]{2,3,1,0:T(1,128)} %param.9) | copy-start | bytes 100
  8.3 3.4 %copy-start = (bf16[32,16,64,128]{3,2,1,0:T(8,128)(2,1)}, bf16[32,16,64,128]{3,2,1,0:T(8,128)(2,1)S(1)}, u32[]{:S(2)}) copy-start(bf16[32,16,64,128]{3,2,1,0:T(8,128)(2,1)S(1)} %broadcast_multiply_fusion) | copy-start | bytes 25165828
  11.7 20.2 %copy-start.1 = (f32[64]{0:T(128)S(1)}, f32[64]{0:T(128)}, u32[]{:S(2)}) copy-start(f32[64]{0:T(128)} %param.11) | copy-start | bytes 772
  11.8 7.7 %collective-permute-start = (bf16[1,16,64,128]{3,2,1,0:T(8,128)(2,1)S(1)}, bf16[1,16,64,128]{3,2,1,0:T(8,128)(2,1)S(1)}, u32[]{:S(2)}, u32[]{:S(2)}) collective-permute-start(bf16[1,16,64,128]{3,2,1,0:T(8,128)(2,1)S(1)} %get-tuple-element.7), channel_id=1, source_target_pairs={{0,16},{16,32},{32,48},{48,64},{64,80},{80,96},{96,112},{1,17},{17... | collective-permute-start | bytes 786440 | tf_op jit(solution)/shard_map/ppermute | solution.py:20
  13.7 7.5 %collective-permute-start.1 = (bf16[1,16,64,128]{3,2,1,0:T(8,128)(2,1)S(1)}, bf16[1,16,64,128]{3,2,1,0:T(8,128)(2,1)S(1)}, u32[]{:S(2)}, u32[]{:S(2)}) collective-permute-start(bf16[1,16,64,128]{3,2,1,0:T(8,128)(2,1)S(1)} %get-tuple-element.8), channel_id=1, source_target_pairs={{16,0},{32,16},{48,32},{64,48},{80,64},{96,80},{112,96},{17,1},{33... | collective-permute-start | bytes 786440 | tf_op jit(solution)/shard_map/ppermute | solution.py:22
  23.6 15.8 %collective-permute-start.2 = (bf16[34,1,64,128]{3,2,1,0:T(8,128)(2,1)}, bf16[34,1,64,128]{3,2,1,0:T(8,128)(2,1)S(1)}, u32[]{:S(2)}, u32[]{:S(2)}) collective-permute-start(bf16[34,1,64,128]{3,2,1,0:T(8,128)(2,1)} %get-tuple-element.5), channel_id=1, source_target_pairs={{0,1},{1,2},{2,3},{3,4},{4,5},{5,6},{6,7},{7,8},{8,9},{9,10},{10,1... | collective-permute-start | bytes 1671176 | tf_op jit(solution)/shard_map/ppermute | solution.py:20
  27.0 17.2 %collective-permute-start.3 = (bf16[34,1,64,128]{3,2,1,0:T(8,128)(2,1)}, bf16[34,1,64,128]{3,2,1,0:T(8,128)(2,1)}, u32[]{:S(2)}, u32[]{:S(2)}) collective-permute-start(bf16[34,1,64,128]{3,2,1,0:T(8,128)(2,1)} %get-tuple-element.6), channel_id=1, source_target_pairs={{1,0},{2,1},{3,2},{4,3},{5,4},{6,5},{7,6},{8,7},{9,8},{10,9},{11,1... | collective-permute-start | bytes 1671176 | tf_op jit(solution)/shard_map/ppermute | solution.py:22

commit v10 on v5

--- a/solution.py
+++ b/solution.py
@@ -1,4 +1,5 @@
 import jax
+import numpy as np
 import jax.numpy as jnp
 from jax import lax
 from jax.sharding import PartitionSpec as P
@@ -106,8 +107,20 @@
     grown = jnp.repeat(grown, EDGE, axis=1)
     grown = jnp.repeat(grown, EDGE, axis=2)
     live = (voxel_mask * grown).astype(jnp.bfloat16)
-    inputs = features * live[..., None]
-    padded = padded_2(inputs, (("gx", 0), ("gy", 1)), 1)
+    def masked(index):
+        edge = features[index].astype(jnp.float32) * live[index].astype(jnp.float32)[..., None]
+        return edge.astype(features.dtype)
+
+    rows_x = lax.axis_size("gx")
+    cols_y = lax.axis_size("gy")
+    up = lax.ppermute(masked(np.s_[-1:]), "gx", [(i, i + 1) for i in range(rows_x - 1)])
+    down = lax.ppermute(masked(np.s_[:1]), "gx", [(i + 1, i) for i in range(rows_x - 1)])
+    extended = jnp.concatenate([up, features * live[..., None], down], axis=0)
+    col_tail = jnp.concatenate([up[:, -1:], masked(np.s_[:, -1:]), down[:, -1:]], axis=0)
+    col_head = jnp.concatenate([up[:, :1], masked(np.s_[:, :1]), down[:, :1]], axis=0)
+    left = lax.ppermute(col_tail, "gy", [(i, i + 1) for i in range(cols_y - 1)])
+    right = lax.ppermute(col_head, "gy", [(i + 1, i) for i in range(cols_y - 1)])
+    padded = jnp.concatenate([left, extended, right], axis=1)
     shifted = jnp.pad(padded, ((0, 0), (0, 0), (1, EDGE - 1), (0, 0)))
     brick_masks = live.astype(jnp.float32).reshape(bricks_x, EDGE, bricks_y, EDGE, bricks_z, EDGE)
     brick_masks = brick_masks.transpose(0, 2, 4, 1, 3, 5).reshape(count, 1, EDGE**3)

time: 223 us -> 219 us (0.982)
  other arithmetic: 29.3 us -> 33.6 us
  local copies, waits for them, and re-layouts: 16.4 us -> 13.8 us
  waiting for transfers between devices: 15.1 us -> 12.8 us
    convert_element_type x0 -> x2, other arithmetic: none -> 3.94 us  [masked(): return edge.astype(features.dtype)]
    unnamed x7, local copies, waits for them, and re-layouts: 11.3 us -> 7.9 us
    slice x1 -> x0, other arithmetic: 2.34 us -> none  [padded_2(): lax.slice_in_dim(cells, cells.shape[dim] - width, cells.shape[dim], axis=...]
    ppermute x4, waiting for transfers between devices: 15.1 us -> 12.8 us  [the longest x1 7.43 us: per_device(): left = lax.ppermute(col_tail, 'gy', [(i, i + 1) for i in range(cols_y - 1)])]
    mul x1 -> x3, other arithmetic: 6.32 us -> 8.58 us  [the longest x1 8.55 us: per_device(): extended = jnp.concatenate([up, features * live[..., None], down], axis=0)]
    concatenate x1 -> x3, other arithmetic: 19.2 us -> 19.6 us  [the longest x1 17.9 us: per_device(): padded = jnp.concatenate([left, extended, right], axis=1)]
  transfers between devices with their start and end apart: 4 -> 4, of which waited for: 4 -> 2; matrix products, arithmetic and copies ran while one was open for 2% -> 7% of each run, Pallas kernels for 0% -> 0%
where the time goes in v10:
time: 219 us; the launch traced here: 218 us
  blocking collectives  107 us (49%)
  Pallas kernels  41.9 us (19%)
  other arithmetic  33.6 us (15%)
  local copies, waits for them, and re-layouts  13.8 us (6%)
  waiting for transfers between devices  12.8 us (6%)
  starting transfers between devices  9.01 us (4%)
    all_to_all x1, blocking collectives, per_device(): lax.all_to_all(sending, 'gy', split_axis=0, concat_axis=0, tiled=True)  107 us
    pallas_call x1, Pallas kernels, conv_slots(): pl.pallas_call(conv_kernel, out_shape=jax.ShapeDtypeStruct((total, C, EDG...  41.9 us
    concatenate x1, other arithmetic, per_device(): padded = jnp.concatenate([left, extended, right], axis=1)  17.9 us
    mul x1, other arithmetic, per_device(): extended = jnp.concatenate([up, features * live[..., None], down], axis=0)  8.55 us
    unnamed x7, local copies, waits for them, and re-layouts  7.9 us
    ppermute x1, waiting for transfers between devices, per_device(): left = lax.ppermute(col_tail, 'gy', [(i, i + 1) for i in range(cols_y - 1)])  7.43 us
    ppermute x1, waiting for transfers between devices, per_device(): lax.ppermute(col_head, 'gy', [(i + 1, i) for i in range(cols_y - 1)])  5.35 us
  transfers between devices with their start and end apart: 4, of which 2 were waited for; matrix products, arithmetic and copies ran while one was open for 7% of the time, Pallas kernels for 0%

profile of v10, /device:TPU:8, one launch (start us, length us, event | category | flops | bytes accessed | tf_op | source)
XLA Modules:
  0.0 218.4 jit_solution(12625879045812023464)
XLA Ops:
  0.0 0.0 copy-start.2
  0.0 0.8 copy.18
  0.8 0.1 broadcast_in_dim.40
  0.9 0.1 broadcast_in_dim.41
  0.9 0.1 copy.19
  1.0 1.0 multiply_convert_fusion.4
  2.0 2.2 multiply_convert_fusion.3
  4.2 1.9 collective-permute-start.1
  6.1 2.4 %collective-permute-start = (bf16[1,16,64,128]{3,2,1,0:T(8,128)(2,1)}, bf16[1,16,64,128]{3,2,1,0:T(8,128)(2,1)}, u32[]{:S(2)}, u32[]{:S(2)}) collective-permute-start(bf16[1,16,64,128]{3,2,1,0:T(8,128)(2,1)} %get-tuple-element.7), channel_id=1, source_target_pairs={{0,16},{16,32},{32,48},{48,64},{64,80},{80,96},{96,112},{1,17},{17... | collective-permute-start | bytes 786440 | tf_op jit(solution)/shard_map/ppermute | solution.py:116
  8.6 0.0 copy-start.1
  8.6 8.5 %broadcast_multiply_fusion = bf16[32,16,64,128]{3,2,1,0:T(8,128)(2,1)} fusion(bf16[32,16,64,128]{3,2,1,0:T(8,128)(2,1)} %param.6, bf16[32,16,64]{2,1,0:T(8,128)(2,1)S(1)} %multiply_convert_fusion.4), kind=kLoop, calls=%fused_computation.10 | loop fusion | flops 4194304 | bytes 16842752 | tf_op jit(solution)/shard_map/mul | solution.py:118
  17.1 1.8 multiply_convert_fusion.1
  18.9 0.0 copy-done.2
  18.9 0.2 convert_reduce_fusion
  19.1 0.5 reshape.66
  19.6 0.1 copy.27
  19.7 0.4 reshape.63.m_ref
  20.1 0.0 collective-permute-done.1
  20.1 0.0 copy-start
  20.1 0.0 collective-permute-done
  20.1 0.8 fusion.10
  20.9 0.0 copy-done
  20.9 0.9 pad_maximum_fusion
  21.8 3.4 %collective-permute-start.2 = (bf16[34,1,64,128]{3,2,1,0:T(8,128)(2,1)}, bf16[34,1,64,128]{3,2,1,0:T(8,128)(2,1)S(1)}, u32[]{:S(2)}, u32[]{:S(2)}) collective-permute-start(bf16[34,1,64,128]{3,2,1,0:T(8,128)(2,1)} %pad_maximum_fusion), channel_id=1, source_target_pairs={{0,1},{1,2},{2,3},{3,4},{4,5},{5,6},{6,7},{7,8},{8,9},{9,10},{10,1... | collective-permute-start | bytes 1671176 | tf_op jit(solution)/shard_map/ppermute | solution.py:121
  25.2 0.9 pad_maximum_fusion.1
  26.1 1.3 collective-permute-start.3
  27.4 0.1 fusion.8
  27.5 2.3 %copy.24 = bf16[3,3,128,3,64]{4,3,2,1,0:T(4,128)(2,1)S(1)} copy(bf16[3,3,128,3,64]{2,4,1,0,3:T(8,128)(2,1)} %bitcast.30) | data formatting | bytes 884736 | tf_op jit(solution)/shard_map/reshape | solution.py:137
  29.8 0.7 reshape.67.w_ref
  30.6 0.0 copy-done.1
  30.6 0.1 copy.23.b_ref
  30.7 0.1 select_reduce_fusion
  30.8 0.1 pad_add_fusion.table_ref
  30.9 7.4 %collective-permute-done.2 = bf16[34,1,64,128]{3,2,1,0:T(8,128)(2,1)S(1)} collective-permute-done((bf16[34,1,64,128]{3,2,1,0:T(8,128)(2,1)}, bf16[34,1,64,128]{3,2,1,0:T(8,128)(2,1)S(1)}, u32[]{:S(2)}, u32[]{:S(2)}) %collective-permute-start.2) | collective-permute-done | bytes 557088 | tf_op jit(solution)/shard_map/ppermute | solution.py:121
  38.3 5.4 %collective-permute-done.3 = bf16[34,1,64,128]{3,2,1,0:T(8,128)(2,1)S(1)} collective-permute-done((bf16[34,1,64,128]{3,2,1,0:T(8,128)(2,1)}, bf16[34,1,64,128]{3,2,1,0:T(8,128)(2,1)S(1)}, u32[]{:S(2)}, u32[]{:S(2)}) %collective-permute-start.3) | collective-permute-done | bytes 557088 | tf_op jit(solution)/shard_map/ppermute | solution.py:122
  43.6 17.9 %select_maximum_fusion.x_ref = bf16[34,18,80,128]{3,2,1,0:T(8,128)(2,1)} fusion(bf16[34,1,64,128]{3,2,1,0:T(8,128)(2,1)S(1)} %collective-permute-done.3, bf16[34,1,64,128]{3,2,1,0:T(8,128)(2,1)S(1)} %collective-permute-done.2, bf16[1,16,64,128]{3,2,1,0:T(8,128)(2,1)} %copy-done, bf16[32,16,64,128]{3,2,1,0:T(8,128)(2,1)} %broadcast_multiply_fusion, ...), kind=kLoop, calls=%fused_computation.3 | loop fusion | flops 112803840 | bytes 22560768 | tf_op jit(solution)/shard_map/concatenate | solution.py:123
  61.5 41.9 %shard_map.67 = bf16[16,64,4096]{2,1,0:T(8,128)(2,1)} custom-call(s32[32]{0:T(128)S(1)} %pad_add_fusion.table_ref, bf16[34,18,80,128]{3,2,1,0:T(8,128)(2,1)} %select_maximum_fusion.x_ref, bf16[3,384,192]{2,1,0:T(8,128)(2,1)S(1)} %reshape.67.w_ref, f32[64,1]{1,0:T(8,128)S(1)} %copy.23.b_ref, f32[8,1,4096]{2,1,0:T(1,128)S(1)} %reshape.63.m_ref), custom_call_target="tpu_custom_call" | custom-call | tf_op jit(solution)/shard_map/pallas_call | solution.py:79
  103.4 107.1 %all_to_all.5 = bf16[16,64,4096]{2,1,0:T(8,128)(2,1)} all-to-all(bf16[16,64,4096]{2,1,0:T(8,128)(2,1)} %shard_map.67), channel_id=1, replica_groups=mesh['gx'=8,'gy'=16] {'gy'}, dimensions={0} | all-to-all | bytes 16777216 | tf_op jit(solution)/shard_map/all_to_all | solution.py:140
  210.5 7.9 %copy.29 = bf16[1,16,64,4096]{3,2,1,0:T(8,128)(2,1)} copy(bf16[1,16,64,4096]{3,2,1,0:T(8,128)(2,1)} %bitcast.28) | data formatting | bytes 16777216
  (6 shorter events, 0.1 us)
Async XLA Ops:
  0.0 18.9 %copy-start.2 = (s32[1,1,8,1]{2,3,1,0:T(1,128)S(1)}, s32[1,1,8,1]{2,3,1,0:T(1,128)}, u32[]{:S(2)}) copy-start(s32[1,1,8,1]{2,3,1,0:T(1,128)} %param.9) | copy-start | bytes 100
  4.2 15.9 %collective-permute-start.1 = (bf16[1,16,64,128]{3,2,1,0:T(8,128)(2,1)}, bf16[1,16,64,128]{3,2,1,0:T(8,128)(2,1)S(1)}, u32[]{:S(2)}, u32[]{:S(2)}) collective-permute-start(bf16[1,16,64,128]{3,2,1,0:T(8,128)(2,1)} %get-tuple-element.8), channel_id=1, source_target_pairs={{16,0},{32,16},{48,32},{64,48},{80,64},{96,80},{112,96},{17,1},{33... | collective-permute-start | bytes 786440 | tf_op jit(solution)/shard_map/ppermute | solution.py:117
  6.1 14.0 %collective-permute-start = (bf16[1,16,64,128]{3,2,1,0:T(8,128)(2,1)}, bf16[1,16,64,128]{3,2,1,0:T(8,128)(2,1)}, u32[]{:S(2)}, u32[]{:S(2)}) collective-permute-start(bf16[1,16,64,128]{3,2,1,0:T(8,128)(2,1)} %get-tuple-element.7), channel_id=1, source_target_pairs={{0,16},{16,32},{32,48},{48,64},{64,80},{80,96},{96,112},{1,17},{17... | collective-permute-start | bytes 786440 | tf_op jit(solution)/shard_map/ppermute | solution.py:116
  8.6 22.0 %copy-start.1 = (f32[64]{0:T(128)S(1)}, f32[64]{0:T(128)}, u32[]{:S(2)}) copy-start(f32[64]{0:T(128)} %param.11) | copy-start | bytes 772
  20.1 0.9 copy-start
  21.8 16.5 %collective-permute-start.2 = (bf16[34,1,64,128]{3,2,1,0:T(8,128)(2,1)}, bf16[34,1,64,128]{3,2,1,0:T(8,128)(2,1)S(1)}, u32[]{:S(2)}, u32[]{:S(2)}) collective-permute-start(bf16[34,1,64,128]{3,2,1,0:T(8,128)(2,1)} %pad_maximum_fusion), channel_id=1, source_target_pairs={{0,1},{1,2},{2,3},{3,4},{4,5},{5,6},{6,7},{7,8},{8,9},{9,10},{10,1... | collective-permute-start | bytes 1671176 | tf_op jit(solution)/shard_map/ppermute | solution.py:121
  26.1 17.5 %collective-permute-start.3 = (bf16[34,1,64,128]{3,2,1,0:T(8,128)(2,1)}, bf16[34,1,64,128]{3,2,1,0:T(8,128)(2,1)S(1)}, u32[]{:S(2)}, u32[]{:S(2)}) collective-permute-start(bf16[34,1,64,128]{3,2,1,0:T(8,128)(2,1)} %pad_maximum_fusion.1), channel_id=1, source_target_pairs={{1,0},{2,1},{3,2},{4,3},{5,4},{6,5},{7,6},{8,7},{9,8},{10,9},{11,1... | collective-permute-start | bytes 1671176 | tf_op jit(solution)/shard_map/ppermute | solution.py:122

commit v11 on v10

--- a/solution.py
+++ b/solution.py
@@ -25,6 +25,28 @@
             axis=dim,
         )
     return cells
+
+
+def shift(piece, axes, steps):
+    sizes = [lax.axis_size(axis) for axis in axes]
+    total = 1
+    for size in sizes:
+        total *= size
+    pairs = []
+    for source in range(total):
+        place = []
+        rest = source
+        for size in reversed(sizes):
+            place.append(rest % size)
+            rest //= size
+        place = place[::-1]
+        moved = [p + d for p, d in zip(place, steps)]
+        if all(0 <= m < size for m, size in zip(moved, sizes)):
+            target = 0
+            for m, size in zip(moved, sizes):
+                target = target * size + m
+            pairs.append((source, target))
+    return lax.ppermute(piece, axes if len(axes) > 1 else axes[0], pairs)
 
 
 def conv_kernel(table_ref, x_ref, w_ref, b_ref, m_ref, o_ref, part_ref):
@@ -116,10 +138,15 @@
     up = lax.ppermute(masked(np.s_[-1:]), "gx", [(i, i + 1) for i in range(rows_x - 1)])
     down = lax.ppermute(masked(np.s_[:1]), "gx", [(i + 1, i) for i in range(rows_x - 1)])
     extended = jnp.concatenate([up, features * live[..., None], down], axis=0)
-    col_tail = jnp.concatenate([up[:, -1:], masked(np.s_[:, -1:]), down[:, -1:]], axis=0)
-    col_head = jnp.concatenate([up[:, :1], masked(np.s_[:, :1]), down[:, :1]], axis=0)
-    left = lax.ppermute(col_tail, "gy", [(i, i + 1) for i in range(cols_y - 1)])
-    right = lax.ppermute(col_head, "gy", [(i + 1, i) for i in range(cols_y - 1)])
+    both = ("gx", "gy")
+    left = lax.ppermute(masked(np.s_[:, -1:]), "gy", [(i, i + 1) for i in range(cols_y - 1)])
+    right = lax.ppermute(masked(np.s_[:, :1]), "gy", [(i + 1, i) for i in range(cols_y - 1)])
+    up_left = shift(masked(np.s_[-1:, -1:]), both, (1, 1))
+    up_right = shift(masked(np.s_[-1:, :1]), both, (1, -1))
+    down_left = shift(masked(np.s_[:1, -1:]), both, (-1, 1))
+    down_right = shift(masked(np.s_[:1, :1]), both, (-1, -1))
+    left = jnp.concatenate([up_left, left, down_left], axis=0)
+    right = jnp.concatenate([up_right, right, down_right], axis=0)
     padded = jnp.concatenate([left, extended, right], axis=1)
     shifted = jnp.pad(padded, ((0, 0), (0, 0), (1, EDGE - 1), (0, 0)))
     brick_masks = live.astype(jnp.float32).reshape(bricks_x, EDGE, bricks_y, EDGE, bricks_z, EDGE)

time: 219 us -> 236 us (1.078)
  other arithmetic: 33.6 us -> 45.1 us
  starting transfers between devices: 9.01 us -> 20.1 us
  waiting for transfers between devices: 12.8 us -> 4.59 us
  blocking collectives: 107 us -> 110 us
    concatenate x1, other arithmetic: 17.9 us -> 29.5 us  [per_device(): padded = jnp.concatenate([left, extended, right], axis=1)]
    ppermute x2 -> x6, starting transfers between devices: 4.7 us -> 14.4 us  [the longest x4 9.98 us: shift(): return lax.ppermute(piece, axes if len(axes) > 1 else axes[0], pairs)]
    ppermute x2 -> x6, waiting for transfers between devices: 12.8 us -> 4.58 us  [the longest x4 4.58 us: shift(): return lax.ppermute(piece, axes if len(axes) > 1 else axes[0], pairs)]
    all_to_all x1, blocking collectives: 107 us -> 110 us  [per_device(): lax.all_to_all(sending, 'gy', split_axis=0, concat_axis=0, tiled=True)]
    convert_element_type x2 -> x3, other arithmetic: 3.94 us -> 5.58 us  [masked(): return edge.astype(features.dtype)]
    unnamed x7 -> x5, local copies, waits for them, and re-layouts: 7.9 us -> 7.89 us
  transfers between devices with their start and end apart: 4 -> 8, of which waited for: 2 -> 1; matrix products, arithmetic and copies ran while one was open for 7% -> 8% of each run, Pallas kernels for 0% -> 0%
where the time goes in v11:
time: 236 us; the launch traced here: 235 us
  blocking collectives  110 us (47%)
  other arithmetic  45.1 us (19%)
  Pallas kernels  42.1 us (18%)
  starting transfers between devices  20.1 us (9%)
  local copies, waits for them, and re-layouts  13 us (6%)
  waiting for transfers between devices  4.59 us (2%)
    all_to_all x1, blocking collectives, per_device(): lax.all_to_all(sending, 'gy', split_axis=0, concat_axis=0, tiled=True)  110 us
    pallas_call x1, Pallas kernels, conv_slots(): pl.pallas_call(conv_kernel, out_shape=jax.ShapeDtypeStruct((total, C, EDG...  42.1 us
    concatenate x1, other arithmetic, per_device(): padded = jnp.concatenate([left, extended, right], axis=1)  29.5 us
    ppermute x4, starting transfers between devices, shift(): return lax.ppermute(piece, axes if len(axes) > 1 else axes[0], pairs)  9.98 us
    mul x1, other arithmetic, per_device(): extended = jnp.concatenate([up, features * live[..., None], down], axis=0)  8.55 us
    unnamed x5, local copies, waits for them, and re-layouts  7.89 us
    convert_element_type x3, other arithmetic, masked(): return edge.astype(features.dtype)  5.58 us
  transfers between devices with their start and end apart: 8, of which 1 were waited for; matrix products, arithmetic and copies ran while one was open for 8% of the time, Pallas kernels for 0%

profile of v11, /device:TPU:8, one launch (start us, length us, event | category | flops | bytes accessed | tf_op | source)
XLA Modules:
  0.0 235.2 jit_solution(17823221863574348630)
XLA Ops:
  0.0 0.0 copy-start.1
  0.0 0.8 copy.18
  0.8 0.1 broadcast_in_dim.44
  0.9 0.1 broadcast_in_dim.45
  0.9 0.1 copy.19
  1.0 1.0 multiply_convert_fusion.4
  2.0 0.9 multiply_convert_fusion.8
  2.9 2.8 %collective-permute-start = (bf16[1,1,64,128]{3,2,1,0:T(8,128)(2,1)S(1)}, bf16[1,1,64,128]{3,2,1,0:T(8,128)(2,1)S(1)}, u32[]{:S(2)}, u32[]{:S(2)}) collective-permute-start(bf16[1,1,64,128]{3,2,1,0:T(8,128)(2,1)S(1)} %get-tuple-element.5), channel_id=1, source_target_pairs={{0,17},{1,18},{2,19},{3,20},{4,21},{5,22},{6,23},{7,24},{8,25},{9,... | collective-permute-start | bytes 49160 | tf_op jit(solution)/shard_map/ppermute | solution.py:49
  5.7 4.6 %collective-permute-start.2 = (bf16[1,1,64,128]{3,2,1,0:T(8,128)(2,1)S(1)}, bf16[1,1,64,128]{3,2,1,0:T(8,128)(2,1)S(1)}, u32[]{:S(2)}, u32[]{:S(2)}) collective-permute-start(bf16[1,1,64,128]{3,2,1,0:T(8,128)(2,1)S(1)} %get-tuple-element.7), channel_id=1, source_target_pairs={{16,1},{17,2},{18,3},{19,4},{20,5},{21,6},{22,7},{23,8},{24,9},{25... | collective-permute-start | bytes 49160 | tf_op jit(solution)/shard_map/ppermute | solution.py:49
  10.4 2.5 %multiply_convert_fusion.1 = (bf16[32,1,64,128]{3,2,1,0:T(8,128)(2,1)}, bf16[32,1,64,128]{3,2,1,0:T(8,128)(2,1)}) fusion(f32[32,64]{1,0:T(8,128)S(1)} %bitcast.52, bf16[32,16,64,128]{3,2,1,0:T(8,128)(2,1)} %param.6, f32[32,64]{1,0:T(8,128)S(1)} %bitcast.53), kind=kLoop, calls=%fused_computation.16 | loop fusion | flops 1572864 | bytes 2113536 | tf_op jit(solution)/shard_map/convert_element_type | solution.py:134
  12.9 3.1 %collective-permute-start.1 = (bf16[32,1,64,128]{3,2,1,0:T(8,128)(2,1)}, bf16[32,1,64,128]{3,2,1,0:T(8,128)(2,1)S(1)}, u32[]{:S(2)}, u32[]{:S(2)}) collective-permute-start(bf16[32,1,64,128]{3,2,1,0:T(8,128)(2,1)} %get-tuple-element.9), channel_id=1, source_target_pairs={{0,1},{1,2},{2,3},{3,4},{4,5},{5,6},{6,7},{7,8},{8,9},{9,10},{10,1... | collective-permute-start | bytes 1572872 | tf_op jit(solution)/shard_map/ppermute | solution.py:142
  16.0 1.3 collective-permute-start.6
  17.3 2.2 multiply_convert_fusion.3
  19.5 0.0 copy-start
  19.5 2.0 collective-permute-start.3
  21.6 8.6 %broadcast_multiply_fusion = bf16[32,16,64,128]{3,2,1,0:T(8,128)(2,1)} fusion(bf16[32,16,64,128]{3,2,1,0:T(8,128)(2,1)} %param.6, bf16[32,16,64]{2,1,0:T(8,128)(2,1)S(1)} %multiply_convert_fusion.4), kind=kLoop, calls=%fused_computation.13 | loop fusion | flops 4194304 | bytes 16842752 | tf_op jit(solution)/shard_map/mul | solution.py:140
  30.1 0.0 copy-done.1
  30.1 0.2 convert_reduce_fusion
  30.3 0.0 collective-permute-done
  30.3 3.6 %collective-permute-start.4 = (bf16[1,16,64,128]{3,2,1,0:T(8,128)(2,1)}, bf16[1,16,64,128]{3,2,1,0:T(8,128)(2,1)}, u32[]{:S(2)}, u32[]{:S(2)}) collective-permute-start(bf16[1,16,64,128]{3,2,1,0:T(8,128)(2,1)} %get-tuple-element.12), channel_id=1, source_target_pairs={{16,0},{32,16},{48,32},{64,48},{80,64},{96,80},{112,96},{17,1},{33... | collective-permute-start | bytes 786440 | tf_op jit(solution)/shard_map/ppermute | solution.py:139
  34.0 0.1 fusion.8
  34.1 0.0 collective-permute-done.2
  34.1 1.3 collective-permute-start.5
  35.4 0.1 select_reduce_fusion
  35.4 4.6 %collective-permute-done.5 = bf16[1,1,64,128]{3,2,1,0:T(8,128)(2,1)S(1)} collective-permute-done((bf16[1,1,64,128]{3,2,1,0:T(8,128)(2,1)S(1)}, bf16[1,1,64,128]{3,2,1,0:T(8,128)(2,1)S(1)}, u32[]{:S(2)}, u32[]{:S(2)}) %collective-permute-start.5) | collective-permute-done | bytes 16416 | tf_op jit(solution)/shard_map/ppermute | solution.py:49
  40.0 1.3 collective-permute-start.7
  41.3 0.1 pad_add_fusion.table_ref
  41.4 0.5 reshape.86
  41.8 0.1 copy.27
  41.9 0.4 reshape.83.m_ref
  42.3 2.3 copy.24
  44.7 0.7 reshape.87.w_ref
  45.4 0.0 copy-done
  45.4 0.1 copy.23.b_ref
  45.5 0.0 collective-permute-done.7
  45.5 0.0 collective-permute-done.3
  45.5 0.0 collective-permute-done.4
  45.5 0.0 collective-permute-done.1
  45.6 0.0 collective-permute-done.6
  45.6 29.5 %fusion.1.x_ref = bf16[34,18,80,128]{3,2,1,0:T(8,128)(2,1)} fusion(bf16[1,1,64,128]{3,2,1,0:T(8,128)(2,1)S(1)} %collective-permute-done.7, bf16[32,1,64,128]{3,2,1,0:T(8,128)(2,1)S(1)} %collective-permute-done.6, bf16[1,1,64,128]{3,2,1,0:T(8,128)(2,1)S(1)} %collective-permute-done.5, bf16[1,16,64,128]{3,2,1,0:T(8,128)(2,1)} %collective-permute-done.4, ...), kind=kLoop, calls=%fused_computation.4 | loop fusion | flops 188006400 | bytes 22560768 | tf_op jit(solution)/shard_map/concatenate | solution.py:150
  75.0 42.1 %shard_map.67 = bf16[16,64,4096]{2,1,0:T(8,128)(2,1)} custom-call(s32[32]{0:T(128)S(1)} %pad_add_fusion.table_ref, bf16[34,18,80,128]{3,2,1,0:T(8,128)(2,1)} %fusion.1.x_ref, bf16[3,384,192]{2,1,0:T(8,128)(2,1)S(1)} %reshape.87.w_ref, f32[64,1]{1,0:T(8,128)S(1)} %copy.23.b_ref, f32[8,1,4096]{2,1,0:T(1,128)S(1)} %reshape.83.m_ref), custom_call_target="tpu_custom_call" | custom-call | tf_op jit(solution)/shard_map/pallas_call | solution.py:101
  117.1 110.2 %all_to_all.5 = bf16[16,64,4096]{2,1,0:T(8,128)(2,1)} all-to-all(bf16[16,64,4096]{2,1,0:T(8,128)(2,1)} %shard_map.67), channel_id=1, replica_groups=mesh['gx'=8,'gy'=16] {'gy'}, dimensions={0} | all-to-all | bytes 16777216 | tf_op jit(solution)/shard_map/all_to_all | solution.py:167
  227.3 7.9 %copy.29 = bf16[1,16,64,4096]{3,2,1,0:T(8,128)(2,1)} copy(bf16[1,16,64,4096]{3,2,1,0:T(8,128)(2,1)} %bitcast.48) | data formatting | bytes 16777216
  (6 shorter events, 0.1 us)
Async XLA Ops:
  0.0 30.1 %copy-start.1 = (s32[1,1,8,1]{2,3,1,0:T(1,128)S(1)}, s32[1,1,8,1]{2,3,1,0:T(1,128)}, u32[]{:S(2)}) copy-start(s32[1,1,8,1]{2,3,1,0:T(1,128)} %param.9) | copy-start | bytes 100
  2.9 27.4 %collective-permute-start = (bf16[1,1,64,128]{3,2,1,0:T(8,128)(2,1)S(1)}, bf16[1,1,64,128]{3,2,1,0:T(8,128)(2,1)S(1)}, u32[]{:S(2)}, u32[]{:S(2)}) collective-permute-start(bf16[1,1,64,128]{3,2,1,0:T(8,128)(2,1)S(1)} %get-tuple-element.5), channel_id=1, source_target_pairs={{0,17},{1,18},{2,19},{3,20},{4,21},{5,22},{6,23},{7,24},{8,25},{9,... | collective-permute-start | bytes 49160 | tf_op jit(solution)/shard_map/ppermute | solution.py:49
  5.7 28.3 %collective-permute-start.2 = (bf16[1,1,64,128]{3,2,1,0:T(8,128)(2,1)S(1)}, bf16[1,1,64,128]{3,2,1,0:T(8,128)(2,1)S(1)}, u32[]{:S(2)}, u32[]{:S(2)}) collective-permute-start(bf16[1,1,64,128]{3,2,1,0:T(8,128)(2,1)S(1)} %get-tuple-element.7), channel_id=1, source_target_pairs={{16,1},{17,2},{18,3},{19,4},{20,5},{21,6},{22,7},{23,8},{24,9},{25... | collective-permute-start | bytes 49160 | tf_op jit(solution)/shard_map/ppermute | solution.py:49
  12.9 32.7 %collective-permute-start.1 = (bf16[32,1,64,128]{3,2,1,0:T(8,128)(2,1)}, bf16[32,1,64,128]{3,2,1,0:T(8,128)(2,1)S(1)}, u32[]{:S(2)}, u32[]{:S(2)}) collective-permute-start(bf16[32,1,64,128]{3,2,1,0:T(8,128)(2,1)} %get-tuple-element.9), channel_id=1, source_target_pairs={{0,1},{1,2},{2,3},{3,4},{4,5},{5,6},{6,7},{7,8},{8,9},{9,10},{10,1... | collective-permute-start | bytes 1572872 | tf_op jit(solution)/shard_map/ppermute | solution.py:142
  16.0 29.5 %collective-permute-start.6 = (bf16[32,1,64,128]{3,2,1,0:T(8,128)(2,1)}, bf16[32,1,64,128]{3,2,1,0:T(8,128)(2,1)S(1)}, u32[]{:S(2)}, u32[]{:S(2)}) collective-permute-start(bf16[32,1,64,128]{3,2,1,0:T(8,128)(2,1)} %get-tuple-element.10), channel_id=1, source_target_pairs={{1,0},{2,1},{3,2},{4,3},{5,4},{6,5},{7,6},{8,7},{9,8},{10,9},{11,1... | collective-permute-start | bytes 1572872 | tf_op jit(solution)/shard_map/ppermute | solution.py:143
  19.5 25.9 %copy-start = (f32[64]{0:T(128)S(1)}, f32[64]{0:T(128)}, u32[]{:S(2)}) copy-start(f32[64]{0:T(128)} %param.11) | copy-start | bytes 772
  19.5 26.0 %collective-permute-start.3 = (bf16[1,16,64,128]{3,2,1,0:T(8,128)(2,1)}, bf16[1,16,64,128]{3,2,1,0:T(8,128)(2,1)S(1)}, u32[]{:S(2)}, u32[]{:S(2)}) collective-permute-start(bf16[1,16,64,128]{3,2,1,0:T(8,128)(2,1)} %get-tuple-element.11), channel_id=1, source_target_pairs={{0,16},{16,32},{32,48},{48,64},{64,80},{80,96},{96,112},{1,17},{17... | collective-permute-start | bytes 786440 | tf_op jit(solution)/shard_map/ppermute | solution.py:138
  30.3 15.2 %collective-permute-start.4 = (bf16[1,16,64,128]{3,2,1,0:T(8,128)(2,1)}, bf16[1,16,64,128]{3,2,1,0:T(8,128)(2,1)}, u32[]{:S(2)}, u32[]{:S(2)}) collective-permute-start(bf16[1,16,64,128]{3,2,1,0:T(8,128)(2,1)} %get-tuple-element.12), channel_id=1, source_target_pairs={{16,0},{32,16},{48,32},{64,48},{80,64},{96,80},{112,96},{17,1},{33... | collective-permute-start | bytes 786440 | tf_op jit(solution)/shard_map/ppermute | solution.py:139
  34.1 6.0 %collective-permute-start.5 = (bf16[1,1,64,128]{3,2,1,0:T(8,128)(2,1)S(1)}, bf16[1,1,64,128]{3,2,1,0:T(8,128)(2,1)S(1)}, u32[]{:S(2)}, u32[]{:S(2)}) collective-permute-start(bf16[1,1,64,128]{3,2,1,0:T(8,128)(2,1)S(1)} %get-tuple-element.6), channel_id=1, source_target_pairs={{1,16},{2,17},{3,18},{4,19},{5,20},{6,21},{7,22},{8,23},{9,24},{10... | collective-permute-start | bytes 49160 | tf_op jit(solution)/shard_map/ppermute | solution.py:49
  40.0 5.5 %collective-permute-start.7 = (bf16[1,1,64,128]{3,2,1,0:T(8,128)(2,1)S(1)}, bf16[1,1,64,128]{3,2,1,0:T(8,128)(2,1)S(1)}, u32[]{:S(2)}, u32[]{:S(2)}) collective-permute-start(bf16[1,1,64,128]{3,2,1,0:T(8,128)(2,1)S(1)} %get-tuple-element.8), channel_id=1, source_target_pairs={{17,0},{18,1},{19,2},{20,3},{21,4},{22,5},{23,6},{24,7},{25,8},{26... | collective-permute-start | bytes 49160 | tf_op jit(solution)/shard_map/ppermute | solution.py:49

commit v12 on v10

--- a/solution.py
+++ b/solution.py
@@ -38,13 +38,12 @@
     @pl.when(valid > 0)
     def _():
         for first in range(0, EDGE + 2, group):
-            part = jnp.zeros((group * rows, 3 * C), jnp.float32)
-            for b in range(3):
-                lhs = jnp.concatenate(
-                    [x_ref[first:first + group, b:b + EDGE, c:c + EDGE, :] for c in range(3)], axis=-1
-                )
-                lhs = lhs.reshape(group * rows, lhs.shape[-1])
-                part = part + jnp.dot(lhs, w_ref[b], preferred_element_type=jnp.float32)
+            lhs = jnp.concatenate(
+                [x_ref[first:first + group, b:b + EDGE, c:c + EDGE, :] for b in range(3) for c in range(3)],
+                axis=-1,
+            )
+            lhs = lhs.reshape(group * rows, lhs.shape[-1])
+            part = jnp.dot(lhs, w_ref[...], preferred_element_type=jnp.float32)
             part_ref[:, first * rows:(first + group) * rows] = part.T
 
         def rows_out(piece, carry):
@@ -84,7 +83,7 @@
             grid=(total,),
             in_specs=[
                 pl.BlockSpec((pl.Element(EDGE + 2), pl.Element(span), pl.Element(window), pl.Element(depth)), x_map),
-                pl.BlockSpec(w9.shape, lambda j, t: (0, 0, 0)),
+                pl.BlockSpec(w9.shape, lambda j, t: (0, 0)),
                 pl.BlockSpec(bias_col.shape, lambda j, t: (0, 0)),
                 pl.BlockSpec((1, 1, EDGE**3), lambda j, t: (brick_of(j, t), 0, 0)),
             ],
@@ -134,7 +133,7 @@
     brick_of_slot = jnp.sum(jnp.where(hit, order[None, :], 0), axis=1)
     valid = jnp.any(hit, axis=1).astype(jnp.int32)
     table = jnp.concatenate([brick_of_slot, valid]).astype(jnp.int32)
-    w9 = weights.transpose(1, 2, 3, 0, 4).reshape(3, 3 * channels_in, 3 * C)
+    w9 = weights.transpose(1, 2, 3, 0, 4).reshape(9 * channels_in, 3 * C)
     bias_col = bias.reshape(C, 1).astype(jnp.float32)
     sending = conv_slots(table, shifted, w9, bias_col, brick_masks, total, bricks_z)
     decoded = lax.all_to_all(sending, "gy", split_axis=0, concat_axis=0, tiled=True)

time: 219 us -> 218 us (level)
  no operation moved by 1% of the time
where the time goes in v12:
time: 218 us
  blocking collectives  108 us (50%)
  Pallas kernels  40 us (18%)
  other arithmetic  33.6 us (15%)
  local copies, waits for them, and re-layouts  13.8 us (6%)
  waiting for transfers between devices  12.8 us (6%)
  starting transfers between devices  9.01 us (4%)
    all_to_all x1, blocking collectives, per_device(): lax.all_to_all(sending, 'gy', split_axis=0, concat_axis=0, tiled=True)  108 us
    pallas_call x1, Pallas kernels, conv_slots(): pl.pallas_call(conv_kernel, out_shape=jax.ShapeDtypeStruct((total, C, EDG...  40 us
    concatenate x1, other arithmetic, per_device(): padded = jnp.concatenate([left, extended, right], axis=1)  17.9 us
    mul x1, other arithmetic, per_device(): extended = jnp.concatenate([up, features * live[..., None], down], axis=0)  8.55 us
    unnamed x7, local copies, waits for them, and re-layouts  7.9 us
    ppermute x1, waiting for transfers between devices, per_device(): left = lax.ppermute(col_tail, 'gy', [(i, i + 1) for i in range(cols_y - 1)])  7.43 us
    ppermute x1, waiting for transfers between devices, per_device(): lax.ppermute(col_head, 'gy', [(i + 1, i) for i in range(cols_y - 1)])  5.35 us
  transfers between devices with their start and end apart: 4, of which 2 were waited for; matrix products, arithmetic and copies ran while one was open for 7% of the time, Pallas kernels for 0%

profile of v12, /device:TPU:8, one launch (start us, length us, event | category | flops | bytes accessed | tf_op | source)
XLA Modules:
  0.0 217.8 jit_solution(16890017349428226984)
XLA Ops:
  0.0 0.0 copy-start.2
  0.0 0.8 copy.18
  0.8 0.1 broadcast_in_dim.40
  0.9 0.1 broadcast_in_dim.41
  0.9 0.1 copy.19
  1.0 1.0 multiply_convert_fusion.4
  2.0 2.2 multiply_convert_fusion.3
  4.2 1.9 collective-permute-start.1
  6.1 2.4 %collective-permute-start = (bf16[1,16,64,128]{3,2,1,0:T(8,128)(2,1)}, bf16[1,16,64,128]{3,2,1,0:T(8,128)(2,1)}, u32[]{:S(2)}, u32[]{:S(2)}) collective-permute-start(bf16[1,16,64,128]{3,2,1,0:T(8,128)(2,1)} %get-tuple-element.7), channel_id=1, source_target_pairs={{0,16},{16,32},{32,48},{48,64},{64,80},{80,96},{96,112},{1,17},{17... | collective-permute-start | bytes 786440 | tf_op jit(solution)/shard_map/ppermute | solution.py:115
  8.6 0.0 copy-start.1
  8.6 8.5 %broadcast_multiply_fusion = bf16[32,16,64,128]{3,2,1,0:T(8,128)(2,1)} fusion(bf16[32,16,64,128]{3,2,1,0:T(8,128)(2,1)} %param.6, bf16[32,16,64]{2,1,0:T(8,128)(2,1)S(1)} %multiply_convert_fusion.4), kind=kLoop, calls=%fused_computation.10 | loop fusion | flops 4194304 | bytes 16842752 | tf_op jit(solution)/shard_map/mul | solution.py:117
  17.1 1.8 multiply_convert_fusion.1
  18.9 0.0 copy-done.2
  18.9 0.2 convert_reduce_fusion
  19.1 0.5 reshape.66
  19.6 0.1 copy.27
  19.7 0.4 reshape.63.m_ref
  20.1 0.0 collective-permute-done.1
  20.1 0.0 copy-start
  20.1 0.0 collective-permute-done
  20.1 0.8 fusion.10
  20.9 0.0 copy-done
  20.9 0.9 pad_maximum_fusion
  21.8 3.4 %collective-permute-start.2 = (bf16[34,1,64,128]{3,2,1,0:T(8,128)(2,1)}, bf16[34,1,64,128]{3,2,1,0:T(8,128)(2,1)S(1)}, u32[]{:S(2)}, u32[]{:S(2)}) collective-permute-start(bf16[34,1,64,128]{3,2,1,0:T(8,128)(2,1)} %pad_maximum_fusion), channel_id=1, source_target_pairs={{0,1},{1,2},{2,3},{3,4},{4,5},{5,6},{6,7},{7,8},{8,9},{9,10},{10,1... | collective-permute-start | bytes 1671176 | tf_op jit(solution)/shard_map/ppermute | solution.py:120
  25.2 0.9 pad_maximum_fusion.1
  26.1 1.3 collective-permute-start.3
  27.4 0.1 fusion.8
  27.5 2.3 %copy.24 = bf16[3,3,128,3,64]{4,3,2,1,0:T(4,128)(2,1)S(1)} copy(bf16[3,3,128,3,64]{2,4,1,0,3:T(8,128)(2,1)} %bitcast.30) | data formatting | bytes 884736 | tf_op jit(solution)/shard_map/reshape | solution.py:136
  29.8 0.7 reshape.67.w_ref
  30.6 0.0 copy-done.1
  30.6 0.1 copy.23.b_ref
  30.7 0.1 select_reduce_fusion
  30.8 0.1 pad_add_fusion.table_ref
  30.9 7.4 %collective-permute-done.2 = bf16[34,1,64,128]{3,2,1,0:T(8,128)(2,1)S(1)} collective-permute-done((bf16[34,1,64,128]{3,2,1,0:T(8,128)(2,1)}, bf16[34,1,64,128]{3,2,1,0:T(8,128)(2,1)S(1)}, u32[]{:S(2)}, u32[]{:S(2)}) %collective-permute-start.2) | collective-permute-done | bytes 557088 | tf_op jit(solution)/shard_map/ppermute | solution.py:120
  38.3 5.4 %collective-permute-done.3 = bf16[34,1,64,128]{3,2,1,0:T(8,128)(2,1)S(1)} collective-permute-done((bf16[34,1,64,128]{3,2,1,0:T(8,128)(2,1)}, bf16[34,1,64,128]{3,2,1,0:T(8,128)(2,1)S(1)}, u32[]{:S(2)}, u32[]{:S(2)}) %collective-permute-start.3) | collective-permute-done | bytes 557088 | tf_op jit(solution)/shard_map/ppermute | solution.py:121
  43.6 17.9 %select_maximum_fusion.x_ref = bf16[34,18,80,128]{3,2,1,0:T(8,128)(2,1)} fusion(bf16[34,1,64,128]{3,2,1,0:T(8,128)(2,1)S(1)} %collective-permute-done.3, bf16[34,1,64,128]{3,2,1,0:T(8,128)(2,1)S(1)} %collective-permute-done.2, bf16[1,16,64,128]{3,2,1,0:T(8,128)(2,1)} %copy-done, bf16[32,16,64,128]{3,2,1,0:T(8,128)(2,1)} %broadcast_multiply_fusion, ...), kind=kLoop, calls=%fused_computation.3 | loop fusion | flops 112803840 | bytes 22560768 | tf_op jit(solution)/shard_map/concatenate | solution.py:122
  61.5 40.0 %shard_map.67 = bf16[16,64,4096]{2,1,0:T(8,128)(2,1)} custom-call(s32[32]{0:T(128)S(1)} %pad_add_fusion.table_ref, bf16[34,18,80,128]{3,2,1,0:T(8,128)(2,1)} %select_maximum_fusion.x_ref, bf16[1152,192]{1,0:T(8,128)(2,1)S(1)} %reshape.67.w_ref, f32[64,1]{1,0:T(8,128)S(1)} %copy.23.b_ref, f32[8,1,4096]{2,1,0:T(1,128)S(1)} %reshape.63.m_ref), custom_call_target="tpu_custom_call" | custom-call | tf_op jit(solution)/shard_map/pallas_call | solution.py:78
  101.5 108.5 %all_to_all.5 = bf16[16,64,4096]{2,1,0:T(8,128)(2,1)} all-to-all(bf16[16,64,4096]{2,1,0:T(8,128)(2,1)} %shard_map.67), channel_id=1, replica_groups=mesh['gx'=8,'gy'=16] {'gy'}, dimensions={0} | all-to-all | bytes 16777216 | tf_op jit(solution)/shard_map/all_to_all | solution.py:139
  209.9 7.9 %copy.29 = bf16[1,16,64,4096]{3,2,1,0:T(8,128)(2,1)} copy(bf16[1,16,64,4096]{3,2,1,0:T(8,128)(2,1)} %bitcast.28) | data formatting | bytes 16777216
  (6 shorter events, 0.1 us)
Async XLA Ops:
  0.0 18.9 %copy-start.2 = (s32[1,1,8,1]{2,3,1,0:T(1,128)S(1)}, s32[1,1,8,1]{2,3,1,0:T(1,128)}, u32[]{:S(2)}) copy-start(s32[1,1,8,1]{2,3,1,0:T(1,128)} %param.9) | copy-start | bytes 100
  4.2 15.9 %collective-permute-start.1 = (bf16[1,16,64,128]{3,2,1,0:T(8,128)(2,1)}, bf16[1,16,64,128]{3,2,1,0:T(8,128)(2,1)S(1)}, u32[]{:S(2)}, u32[]{:S(2)}) collective-permute-start(bf16[1,16,64,128]{3,2,1,0:T(8,128)(2,1)} %get-tuple-element.8), channel_id=1, source_target_pairs={{16,0},{32,16},{48,32},{64,48},{80,64},{96,80},{112,96},{17,1},{33... | collective-permute-start | bytes 786440 | tf_op jit(solution)/shard_map/ppermute | solution.py:116
  6.1 14.0 %collective-permute-start = (bf16[1,16,64,128]{3,2,1,0:T(8,128)(2,1)}, bf16[1,16,64,128]{3,2,1,0:T(8,128)(2,1)}, u32[]{:S(2)}, u32[]{:S(2)}) collective-permute-start(bf16[1,16,64,128]{3,2,1,0:T(8,128)(2,1)} %get-tuple-element.7), channel_id=1, source_target_pairs={{0,16},{16,32},{32,48},{48,64},{64,80},{80,96},{96,112},{1,17},{17... | collective-permute-start | bytes 786440 | tf_op jit(solution)/shard_map/ppermute | solution.py:115
  8.6 22.0 %copy-start.1 = (f32[64]{0:T(128)S(1)}, f32[64]{0:T(128)}, u32[]{:S(2)}) copy-start(f32[64]{0:T(128)} %param.11) | copy-start | bytes 772
  20.1 0.9 copy-start
  21.8 16.5 %collective-permute-start.2 = (bf16[34,1,64,128]{3,2,1,0:T(8,128)(2,1)}, bf16[34,1,64,128]{3,2,1,0:T(8,128)(2,1)S(1)}, u32[]{:S(2)}, u32[]{:S(2)}) collective-permute-start(bf16[34,1,64,128]{3,2,1,0:T(8,128)(2,1)} %pad_maximum_fusion), channel_id=1, source_target_pairs={{0,1},{1,2},{2,3},{3,4},{4,5},{5,6},{6,7},{7,8},{8,9},{9,10},{10,1... | collective-permute-start | bytes 1671176 | tf_op jit(solution)/shard_map/ppermute | solution.py:120
  26.1 17.5 %collective-permute-start.3 = (bf16[34,1,64,128]{3,2,1,0:T(8,128)(2,1)}, bf16[34,1,64,128]{3,2,1,0:T(8,128)(2,1)S(1)}, u32[]{:S(2)}, u32[]{:S(2)}) collective-permute-start(bf16[34,1,64,128]{3,2,1,0:T(8,128)(2,1)} %pad_maximum_fusion.1), channel_id=1, source_target_pairs={{1,0},{2,1},{3,2},{4,3},{5,4},{6,5},{7,6},{8,7},{9,8},{10,9},{11,1... | collective-permute-start | bytes 1671176 | tf_op jit(solution)/shard_map/ppermute | solution.py:121

commit v13 on v12

--- a/solution.py
+++ b/solution.py
@@ -32,7 +32,7 @@
     slots = pl.num_programs(0)
     valid = table_ref[slots + slot]
     rows = EDGE * EDGE
-    group = 6
+    group = 9
     chunk = 4 * rows
 
     @pl.when(valid > 0)

time: 218 us -> 220 us (level)
  no operation moved by 1% of the time
where the time goes in v13:
time: 220 us; the launch traced here: 219 us
  blocking collectives  108 us (49%)
  Pallas kernels  41.9 us (19%)
  other arithmetic  33.6 us (15%)
  local copies, waits for them, and re-layouts  13.8 us (6%)
  waiting for transfers between devices  12.8 us (6%)
  starting transfers between devices  9.01 us (4%)
    all_to_all x1, blocking collectives, per_device(): lax.all_to_all(sending, 'gy', split_axis=0, concat_axis=0, tiled=True)  108 us
    pallas_call x1, Pallas kernels, conv_slots(): pl.pallas_call(conv_kernel, out_shape=jax.ShapeDtypeStruct((total, C, EDG...  41.9 us
    concatenate x1, other arithmetic, per_device(): padded = jnp.concatenate([left, extended, right], axis=1)  17.9 us
    mul x1, other arithmetic, per_device(): extended = jnp.concatenate([up, features * live[..., None], down], axis=0)  8.55 us
    unnamed x7, local copies, waits for them, and re-layouts  7.9 us
    ppermute x1, waiting for transfers between devices, per_device(): left = lax.ppermute(col_tail, 'gy', [(i, i + 1) for i in range(cols_y - 1)])  7.43 us
    ppermute x1, waiting for transfers between devices, per_device(): lax.ppermute(col_head, 'gy', [(i + 1, i) for i in range(cols_y - 1)])  5.35 us
  transfers between devices with their start and end apart: 4, of which 2 were waited for; matrix products, arithmetic and copies ran while one was open for 7% of the time, Pallas kernels for 0%

profile of v13, /device:TPU:8, one launch (start us, length us, event | category | flops | bytes accessed | tf_op | source)
XLA Modules:
  0.0 219.5 jit_solution(17743184057180160040)
XLA Ops:
  0.0 0.0 copy-start.2
  0.0 0.8 copy.18
  0.8 0.1 broadcast_in_dim.40
  0.9 0.1 broadcast_in_dim.41
  0.9 0.1 copy.19
  1.0 1.0 multiply_convert_fusion.4
  2.0 2.2 multiply_convert_fusion.3
  4.2 1.9 collective-permute-start.1
  6.1 2.4 %collective-permute-start = (bf16[1,16,64,128]{3,2,1,0:T(8,128)(2,1)}, bf16[1,16,64,128]{3,2,1,0:T(8,128)(2,1)}, u32[]{:S(2)}, u32[]{:S(2)}) collective-permute-start(bf16[1,16,64,128]{3,2,1,0:T(8,128)(2,1)} %get-tuple-element.7), channel_id=1, source_target_pairs={{0,16},{16,32},{32,48},{48,64},{64,80},{80,96},{96,112},{1,17},{17... | collective-permute-start | bytes 786440 | tf_op jit(solution)/shard_map/ppermute | solution.py:115
  8.6 0.0 copy-start.1
  8.6 8.5 %broadcast_multiply_fusion = bf16[32,16,64,128]{3,2,1,0:T(8,128)(2,1)} fusion(bf16[32,16,64,128]{3,2,1,0:T(8,128)(2,1)} %param.6, bf16[32,16,64]{2,1,0:T(8,128)(2,1)S(1)} %multiply_convert_fusion.4), kind=kLoop, calls=%fused_computation.10 | loop fusion | flops 4194304 | bytes 16842752 | tf_op jit(solution)/shard_map/mul | solution.py:117
  17.1 1.8 multiply_convert_fusion.1
  18.9 0.0 copy-done.2
  18.9 0.2 convert_reduce_fusion
  19.1 0.5 reshape.66
  19.6 0.1 copy.27
  19.7 0.4 reshape.63.m_ref
  20.1 0.0 collective-permute-done.1
  20.1 0.0 copy-start
  20.1 0.0 collective-permute-done
  20.1 0.8 fusion.10
  20.9 0.0 copy-done
  20.9 0.9 pad_maximum_fusion
  21.8 3.4 %collective-permute-start.2 = (bf16[34,1,64,128]{3,2,1,0:T(8,128)(2,1)}, bf16[34,1,64,128]{3,2,1,0:T(8,128)(2,1)S(1)}, u32[]{:S(2)}, u32[]{:S(2)}) collective-permute-start(bf16[34,1,64,128]{3,2,1,0:T(8,128)(2,1)} %pad_maximum_fusion), channel_id=1, source_target_pairs={{0,1},{1,2},{2,3},{3,4},{4,5},{5,6},{6,7},{7,8},{8,9},{9,10},{10,1... | collective-permute-start | bytes 1671176 | tf_op jit(solution)/shard_map/ppermute | solution.py:120
  25.2 0.9 pad_maximum_fusion.1
  26.1 1.3 collective-permute-start.3
  27.4 0.1 fusion.8
  27.5 2.3 %copy.24 = bf16[3,3,128,3,64]{4,3,2,1,0:T(4,128)(2,1)S(1)} copy(bf16[3,3,128,3,64]{2,4,1,0,3:T(8,128)(2,1)} %bitcast.30) | data formatting | bytes 884736 | tf_op jit(solution)/shard_map/reshape | solution.py:136
  29.8 0.7 reshape.67.w_ref
  30.6 0.0 copy-done.1
  30.6 0.1 copy.23.b_ref
  30.7 0.1 select_reduce_fusion
  30.8 0.1 pad_add_fusion.table_ref
  30.9 7.4 %collective-permute-done.2 = bf16[34,1,64,128]{3,2,1,0:T(8,128)(2,1)S(1)} collective-permute-done((bf16[34,1,64,128]{3,2,1,0:T(8,128)(2,1)}, bf16[34,1,64,128]{3,2,1,0:T(8,128)(2,1)S(1)}, u32[]{:S(2)}, u32[]{:S(2)}) %collective-permute-start.2) | collective-permute-done | bytes 557088 | tf_op jit(solution)/shard_map/ppermute | solution.py:120
  38.3 5.4 %collective-permute-done.3 = bf16[34,1,64,128]{3,2,1,0:T(8,128)(2,1)S(1)} collective-permute-done((bf16[34,1,64,128]{3,2,1,0:T(8,128)(2,1)}, bf16[34,1,64,128]{3,2,1,0:T(8,128)(2,1)S(1)}, u32[]{:S(2)}, u32[]{:S(2)}) %collective-permute-start.3) | collective-permute-done | bytes 557088 | tf_op jit(solution)/shard_map/ppermute | solution.py:121
  43.6 17.9 %select_maximum_fusion.x_ref = bf16[34,18,80,128]{3,2,1,0:T(8,128)(2,1)} fusion(bf16[34,1,64,128]{3,2,1,0:T(8,128)(2,1)S(1)} %collective-permute-done.3, bf16[34,1,64,128]{3,2,1,0:T(8,128)(2,1)S(1)} %collective-permute-done.2, bf16[1,16,64,128]{3,2,1,0:T(8,128)(2,1)} %copy-done, bf16[32,16,64,128]{3,2,1,0:T(8,128)(2,1)} %broadcast_multiply_fusion, ...), kind=kLoop, calls=%fused_computation.3 | loop fusion | flops 112803840 | bytes 22560768 | tf_op jit(solution)/shard_map/concatenate | solution.py:122
  61.5 41.9 %shard_map.67 = bf16[16,64,4096]{2,1,0:T(8,128)(2,1)} custom-call(s32[32]{0:T(128)S(1)} %pad_add_fusion.table_ref, bf16[34,18,80,128]{3,2,1,0:T(8,128)(2,1)} %select_maximum_fusion.x_ref, bf16[1152,192]{1,0:T(8,128)(2,1)S(1)} %reshape.67.w_ref, f32[64,1]{1,0:T(8,128)S(1)} %copy.23.b_ref, f32[8,1,4096]{2,1,0:T(1,128)S(1)} %reshape.63.m_ref), custom_call_target="tpu_custom_call" | custom-call | tf_op jit(solution)/shard_map/pallas_call | solution.py:78
  103.4 108.2 %all_to_all.5 = bf16[16,64,4096]{2,1,0:T(8,128)(2,1)} all-to-all(bf16[16,64,4096]{2,1,0:T(8,128)(2,1)} %shard_map.67), channel_id=1, replica_groups=mesh['gx'=8,'gy'=16] {'gy'}, dimensions={0} | all-to-all | bytes 16777216 | tf_op jit(solution)/shard_map/all_to_all | solution.py:139
  211.6 7.9 %copy.29 = bf16[1,16,64,4096]{3,2,1,0:T(8,128)(2,1)} copy(bf16[1,16,64,4096]{3,2,1,0:T(8,128)(2,1)} %bitcast.28) | data formatting | bytes 16777216
  (6 shorter events, 0.1 us)
Async XLA Ops:
  0.0 18.9 %copy-start.2 = (s32[1,1,8,1]{2,3,1,0:T(1,128)S(1)}, s32[1,1,8,1]{2,3,1,0:T(1,128)}, u32[]{:S(2)}) copy-start(s32[1,1,8,1]{2,3,1,0:T(1,128)} %param.9) | copy-start | bytes 100
  4.2 15.9 %collective-permute-start.1 = (bf16[1,16,64,128]{3,2,1,0:T(8,128)(2,1)}, bf16[1,16,64,128]{3,2,1,0:T(8,128)(2,1)S(1)}, u32[]{:S(2)}, u32[]{:S(2)}) collective-permute-start(bf16[1,16,64,128]{3,2,1,0:T(8,128)(2,1)} %get-tuple-element.8), channel_id=1, source_target_pairs={{16,0},{32,16},{48,32},{64,48},{80,64},{96,80},{112,96},{17,1},{33... | collective-permute-start | bytes 786440 | tf_op jit(solution)/shard_map/ppermute | solution.py:116
  6.1 14.0 %collective-permute-start = (bf16[1,16,64,128]{3,2,1,0:T(8,128)(2,1)}, bf16[1,16,64,128]{3,2,1,0:T(8,128)(2,1)}, u32[]{:S(2)}, u32[]{:S(2)}) collective-permute-start(bf16[1,16,64,128]{3,2,1,0:T(8,128)(2,1)} %get-tuple-element.7), channel_id=1, source_target_pairs={{0,16},{16,32},{32,48},{48,64},{64,80},{80,96},{96,112},{1,17},{17... | collective-permute-start | bytes 786440 | tf_op jit(solution)/shard_map/ppermute | solution.py:115
  8.6 22.0 %copy-start.1 = (f32[64]{0:T(128)S(1)}, f32[64]{0:T(128)}, u32[]{:S(2)}) copy-start(f32[64]{0:T(128)} %param.11) | copy-start | bytes 772
  20.1 0.9 copy-start
  21.8 16.5 %collective-permute-start.2 = (bf16[34,1,64,128]{3,2,1,0:T(8,128)(2,1)}, bf16[34,1,64,128]{3,2,1,0:T(8,128)(2,1)S(1)}, u32[]{:S(2)}, u32[]{:S(2)}) collective-permute-start(bf16[34,1,64,128]{3,2,1,0:T(8,128)(2,1)} %pad_maximum_fusion), channel_id=1, source_target_pairs={{0,1},{1,2},{2,3},{3,4},{4,5},{5,6},{6,7},{7,8},{8,9},{9,10},{10,1... | collective-permute-start | bytes 1671176 | tf_op jit(solution)/shard_map/ppermute | solution.py:120
  26.1 17.5 %collective-permute-start.3 = (bf16[34,1,64,128]{3,2,1,0:T(8,128)(2,1)}, bf16[34,1,64,128]{3,2,1,0:T(8,128)(2,1)S(1)}, u32[]{:S(2)}, u32[]{:S(2)}) collective-permute-start(bf16[34,1,64,128]{3,2,1,0:T(8,128)(2,1)} %pad_maximum_fusion.1), channel_id=1, source_target_pairs={{1,0},{2,1},{3,2},{4,3},{5,4},{6,5},{7,6},{8,7},{9,8},{10,9},{11,1... | collective-permute-start | bytes 1671176 | tf_op jit(solution)/shard_map/ppermute | solution.py:121

commit v14 on v12

--- a/solution.py
+++ b/solution.py
@@ -132,7 +132,10 @@
     hit = slots[None, :] == jnp.arange(total, dtype=jnp.int32)[:, None]
     brick_of_slot = jnp.sum(jnp.where(hit, order[None, :], 0), axis=1)
     valid = jnp.any(hit, axis=1).astype(jnp.int32)
-    table = jnp.concatenate([brick_of_slot, valid]).astype(jnp.int32)
+    seen = lax.cummax(jnp.where(valid > 0, jnp.arange(total, dtype=jnp.int32), -1))
+    first = jnp.argmax(valid)
+    held = jnp.where(seen >= 0, brick_of_slot[jnp.maximum(seen, 0)], brick_of_slot[first])
+    table = jnp.concatenate([held, valid]).astype(jnp.int32)
     w9 = weights.transpose(1, 2, 3, 0, 4).reshape(9 * channels_in, 3 * C)
     bias_col = bias.reshape(C, 1).astype(jnp.float32)
     sending = conv_slots(table, shifted, w9, bias_col, brick_masks, total, bricks_z)

time: 218 us -> 219 us (level)
  waiting for transfers between devices: 12.8 us -> 9.87 us
    ppermute x1, waiting for transfers between devices: 7.43 us -> 4.97 us  [per_device(): left = lax.ppermute(col_tail, 'gy', [(i, i + 1) for i in range(cols_y - 1)])]
  transfers between devices with their start and end apart: 4 -> 4, of which waited for: 2 -> 2; matrix products, arithmetic and copies ran while one was open for 7% -> 9% of each run, Pallas kernels for 0% -> 0%
where the time goes in v14:
time: 219 us; the launch traced here: 218 us
  blocking collectives  107 us (49%)
  Pallas kernels  40 us (18%)
  other arithmetic  34.3 us (16%)
  local copies, waits for them, and re-layouts  15 us (7%)
  starting transfers between devices  10.3 us (5%)
  waiting for transfers between devices  9.87 us (5%)
    all_to_all x1, blocking collectives, per_device(): lax.all_to_all(sending, 'gy', split_axis=0, concat_axis=0, tiled=True)  107 us
    pallas_call x1, Pallas kernels, conv_slots(): pl.pallas_call(conv_kernel, out_shape=jax.ShapeDtypeStruct((total, C, EDG...  40 us
    concatenate x1, other arithmetic, per_device(): padded = jnp.concatenate([left, extended, right], axis=1)  17.8 us
    unnamed x7, local copies, waits for them, and re-layouts  8.58 us
    mul x1, other arithmetic, per_device(): extended = jnp.concatenate([up, features * live[..., None], down], axis=0)  8.55 us
    ppermute x1, waiting for transfers between devices, per_device(): left = lax.ppermute(col_tail, 'gy', [(i, i + 1) for i in range(cols_y - 1)])  4.97 us
    ppermute x1, waiting for transfers between devices, per_device(): lax.ppermute(col_head, 'gy', [(i + 1, i) for i in range(cols_y - 1)])  4.89 us
  transfers between devices with their start and end apart: 4, of which 2 were waited for; matrix products, arithmetic and copies ran while one was open for 9% of the time, Pallas kernels for 0%

profile of v14, /device:TPU:8, one launch (start us, length us, event | category | flops | bytes accessed | tf_op | source)
XLA Modules:
  0.0 218.2 jit_solution(1111623091581630469)
XLA Ops:
  0.0 0.0 copy-start.2
  0.0 0.8 copy.21
  0.8 0.1 broadcast_in_dim.51
  0.9 0.1 broadcast_in_dim.52
  0.9 0.1 copy.22
  1.0 1.0 multiply_convert_fusion.4
  2.0 1.4 multiply_convert_fusion.3
  3.4 1.9 collective-permute-start
  5.3 3.6 %collective-permute-start.1 = (bf16[1,16,64,128]{3,2,1,0:T(8,128)(2,1)S(1)}, bf16[1,16,64,128]{3,2,1,0:T(8,128)(2,1)S(1)}, u32[]{:S(2)}, u32[]{:S(2)}) collective-permute-start(bf16[1,16,64,128]{3,2,1,0:T(8,128)(2,1)S(1)} %get-tuple-element.10), channel_id=1, source_target_pairs={{16,0},{32,16},{48,32},{64,48},{80,64},{96,80},{112,96},{17,1},{33... | collective-permute-start | bytes 786440 | tf_op jit(solution)/shard_map/ppermute | solution.py:116
  9.0 0.0 copy-start.1
  9.0 8.6 %broadcast_multiply_fusion = bf16[32,16,64,128]{3,2,1,0:T(8,128)(2,1)} fusion(bf16[32,16,64,128]{3,2,1,0:T(8,128)(2,1)} %param.6, bf16[32,16,64]{2,1,0:T(8,128)(2,1)S(1)} %multiply_convert_fusion.4), kind=kLoop, calls=%fused_computation.11 | loop fusion | flops 4194304 | bytes 16842752 | tf_op jit(solution)/shard_map/mul | solution.py:117
  17.6 0.0 copy-done.2
  17.6 0.2 convert_reduce_fusion
  17.8 0.1 fusion.8
  17.9 0.7 iota_reduce_fusion
  18.6 1.8 multiply_convert_fusion.1
  20.4 0.1 copy.20
  20.5 0.1 select_reduce_fusion
  20.6 0.1 maximum_reduce_fusion
  20.7 0.5 reshape.96
  22.8 0.6 dynamic_slice.3
  23.4 0.0 collective-permute-done
  23.4 0.0 collective-permute-done.1
  23.4 0.0 copy-start
  23.4 0.7 copy-done
  24.1 0.9 pad_maximum_fusion
  25.0 3.4 %collective-permute-start.2 = (bf16[34,1,64,128]{3,2,1,0:T(8,128)(2,1)}, bf16[34,1,64,128]{3,2,1,0:T(8,128)(2,1)S(1)}, u32[]{:S(2)}, u32[]{:S(2)}) collective-permute-start(bf16[34,1,64,128]{3,2,1,0:T(8,128)(2,1)} %pad_maximum_fusion), channel_id=1, source_target_pairs={{0,1},{1,2},{2,3},{3,4},{4,5},{5,6},{6,7},{7,8},{8,9},{9,10},{10,1... | collective-permute-start | bytes 1671176 | tf_op jit(solution)/shard_map/ppermute | solution.py:120
  28.4 0.9 pad_maximum_fusion.1
  29.3 1.3 collective-permute-start.3
  30.6 0.7 gather_fusion
  31.2 0.1 copy.30
  31.3 0.4 reshape.93.m_ref
  31.7 2.4 %copy.27 = bf16[3,3,128,3,64]{4,3,2,1,0:T(4,128)(2,1)S(1)} copy(bf16[3,3,128,3,64]{2,4,1,0,3:T(8,128)(2,1)} %bitcast.33) | data formatting | bytes 884736 | tf_op jit(solution)/shard_map/reshape | solution.py:139
  34.1 0.7 reshape.105.w_ref
  34.8 0.0 copy-done.1
  34.9 0.1 copy.26.b_ref
  34.9 0.1 compare_reduce_fusion
  35.1 0.6 broadcast_select_fusion
  35.6 0.1 pad_add_fusion.table_ref
  35.7 5.0 %collective-permute-done.2 = bf16[34,1,64,128]{3,2,1,0:T(8,128)(2,1)S(1)} collective-permute-done((bf16[34,1,64,128]{3,2,1,0:T(8,128)(2,1)}, bf16[34,1,64,128]{3,2,1,0:T(8,128)(2,1)S(1)}, u32[]{:S(2)}, u32[]{:S(2)}) %collective-permute-start.2) | collective-permute-done | bytes 557088 | tf_op jit(solution)/shard_map/ppermute | solution.py:120
  40.7 4.9 %collective-permute-done.3 = bf16[34,1,64,128]{3,2,1,0:T(8,128)(2,1)S(1)} collective-permute-done((bf16[34,1,64,128]{3,2,1,0:T(8,128)(2,1)}, bf16[34,1,64,128]{3,2,1,0:T(8,128)(2,1)S(1)}, u32[]{:S(2)}, u32[]{:S(2)}) %collective-permute-start.3) | collective-permute-done | bytes 557088 | tf_op jit(solution)/shard_map/ppermute | solution.py:121
  45.6 17.8 %select_maximum_fusion.x_ref = bf16[34,18,80,128]{3,2,1,0:T(8,128)(2,1)} fusion(bf16[34,1,64,128]{3,2,1,0:T(8,128)(2,1)S(1)} %collective-permute-done.3, bf16[34,1,64,128]{3,2,1,0:T(8,128)(2,1)S(1)} %collective-permute-done.2, bf16[1,16,64,128]{3,2,1,0:T(8,128)(2,1)} %copy-done, bf16[32,16,64,128]{3,2,1,0:T(8,128)(2,1)} %broadcast_multiply_fusion, ...), kind=kLoop, calls=%fused_computation.4 | loop fusion | flops 112803840 | bytes 22560768 | tf_op jit(solution)/shard_map/concatenate | solution.py:122
  63.4 40.0 %shard_map.67 = bf16[16,64,4096]{2,1,0:T(8,128)(2,1)} custom-call(s32[32]{0:T(128)S(1)} %pad_add_fusion.table_ref, bf16[34,18,80,128]{3,2,1,0:T(8,128)(2,1)} %select_maximum_fusion.x_ref, bf16[1152,192]{1,0:T(8,128)(2,1)S(1)} %reshape.105.w_ref, f32[64,1]{1,0:T(8,128)S(1)} %copy.26.b_ref, f32[8,1,4096]{2,1,0:T(1,128)S(1)} %reshape.93.m_ref), custom_call_target="tpu_custom_call" | custom-call | tf_op jit(solution)/shard_map/pallas_call | solution.py:78
  103.4 106.9 %all_to_all.5 = bf16[16,64,4096]{2,1,0:T(8,128)(2,1)} all-to-all(bf16[16,64,4096]{2,1,0:T(8,128)(2,1)} %shard_map.67), channel_id=1, replica_groups=mesh['gx'=8,'gy'=16] {'gy'}, dimensions={0} | all-to-all | bytes 16777216 | tf_op jit(solution)/shard_map/all_to_all | solution.py:142
  210.3 7.9 %copy.32 = bf16[1,16,64,4096]{3,2,1,0:T(8,128)(2,1)} copy(bf16[1,16,64,4096]{3,2,1,0:T(8,128)(2,1)} %bitcast.31) | data formatting | bytes 16777216
  (10 shorter events, 0.1 us)
Async XLA Ops:
  0.0 17.6 %copy-start.2 = (s32[1,1,8,1]{2,3,1,0:T(1,128)S(1)}, s32[1,1,8,1]{2,3,1,0:T(1,128)}, u32[]{:S(2)}) copy-start(s32[1,1,8,1]{2,3,1,0:T(1,128)} %param.9) | copy-start | bytes 100
  3.4 20.0 %collective-permute-start = (bf16[1,16,64,128]{3,2,1,0:T(8,128)(2,1)S(1)}, bf16[1,16,64,128]{3,2,1,0:T(8,128)(2,1)S(1)}, u32[]{:S(2)}, u32[]{:S(2)}) collective-permute-start(bf16[1,16,64,128]{3,2,1,0:T(8,128)(2,1)S(1)} %get-tuple-element.9), channel_id=1, source_target_pairs={{0,16},{16,32},{32,48},{48,64},{64,80},{80,96},{96,112},{1,17},{17... | collective-permute-start | bytes 786440 | tf_op jit(solution)/shard_map/ppermute | solution.py:115
  5.3 18.1 %collective-permute-start.1 = (bf16[1,16,64,128]{3,2,1,0:T(8,128)(2,1)S(1)}, bf16[1,16,64,128]{3,2,1,0:T(8,128)(2,1)S(1)}, u32[]{:S(2)}, u32[]{:S(2)}) collective-permute-start(bf16[1,16,64,128]{3,2,1,0:T(8,128)(2,1)S(1)} %get-tuple-element.10), channel_id=1, source_target_pairs={{16,0},{32,16},{48,32},{64,48},{80,64},{96,80},{112,96},{17,1},{33... | collective-permute-start | bytes 786440 | tf_op jit(solution)/shard_map/ppermute | solution.py:116
  9.0 25.8 %copy-start.1 = (f32[64]{0:T(128)S(1)}, f32[64]{0:T(128)}, u32[]{:S(2)}) copy-start(f32[64]{0:T(128)} %param.11) | copy-start | bytes 772
  23.4 0.7 copy-start
  25.0 15.7 %collective-permute-start.2 = (bf16[34,1,64,128]{3,2,1,0:T(8,128)(2,1)}, bf16[34,1,64,128]{3,2,1,0:T(8,128)(2,1)S(1)}, u32[]{:S(2)}, u32[]{:S(2)}) collective-permute-start(bf16[34,1,64,128]{3,2,1,0:T(8,128)(2,1)} %pad_maximum_fusion), channel_id=1, source_target_pairs={{0,1},{1,2},{2,3},{3,4},{4,5},{5,6},{6,7},{7,8},{8,9},{9,10},{10,1... | collective-permute-start | bytes 1671176 | tf_op jit(solution)/shard_map/ppermute | solution.py:120
  29.3 16.3 %collective-permute-start.3 = (bf16[34,1,64,128]{3,2,1,0:T(8,128)(2,1)}, bf16[34,1,64,128]{3,2,1,0:T(8,128)(2,1)S(1)}, u32[]{:S(2)}, u32[]{:S(2)}) collective-permute-start(bf16[34,1,64,128]{3,2,1,0:T(8,128)(2,1)} %pad_maximum_fusion.1), channel_id=1, source_target_pairs={{1,0},{2,1},{3,2},{4,3},{5,4},{6,5},{7,6},{8,7},{9,8},{10,9},{11,1... | collective-permute-start | bytes 1671176 | tf_op jit(solution)/shard_map/ppermute | solution.py:121
